TPU v7x, 512 devices: a whole 4x8x8 slice. The times are simulated.
512 devices in a mesh: grp: 8 (over y_hi, x), blk: 64 (over z, y_lo, core).
Axes of the slice: x: 4, y: 8 (y_hi: 2, y_lo: 4; y = y_hi * 4 + y_lo), z: 8, core: 2. Of those that a mesh axis runs over, the one named last changes fastest.
Arguments:
- vertex_embed: float32 [196608, 256], P(('grp', 'blk')), may hold values from -1.8 to 1.8
- context_embed: float32 [196608, 256], P(('grp', 'blk')), may hold values from -1.8 to 1.8
- counts: int32 [4, 196608, 384], P(None, ('grp', 'blk')), may hold values from 0 to 7
- negatives: int32 [4, 5, 196608], P(None, None, ('grp', 'blk')), may hold values from 0 to 383
- masks: int32 [4, 1536, 3], P(None, ('grp', 'blk')), may hold values 0 or 1
Outputs:
- vertex_final: float32 [196608, 256], P(('grp', 'blk'))
- context_final: float32 [196608, 256], P(('grp', 'blk'))
All inputs are finite; a program needn't handle non-finite values. No bound on the sum of `masks` on one device may be relied on, other than what follows from the above.
Results may differ from a plain program's by a relative error of at most 0.0003.
Values sent between devices are 32-bit elements; how exact they have to be, the bound alone decides.
No kernel may reach another device: no remote copies, remote signals or barrier semaphores. Data moves between devices by JAX's collectives and lax.ppermute only.
A program may use at most 64 MiB of HBM per device.

v0:
```python
import math

import jax
import jax.numpy as jnp
from jax import lax
from jax.sharding import PartitionSpec as P

ROUNDS = 2
ROUND_PASSES = 2


def passed_along(value, axis, steps):
    count = lax.axis_size(axis)
    pairs = [(source, (source + steps) % count) for source in range(count)]
    return lax.ppermute(value, axis, pairs)


def from_partner(value, axis, stride):
    return lax.ppermute(value, axis, [(i, i ^ 1 << stride) for i in range(lax.axis_size(axis))])


def one_pass(vert, ctx, cnt, neg_rows, tile_mask):
    highest = lax.Precision.HIGHEST
    rows = vert.shape[0]
    tiles = tile_mask.shape[0]
    tile = rows // tiles
    eta = 0.25 / math.sqrt(rows)
    columns = lax.broadcasted_iota(jnp.int32, (1, rows), 1)
    scores = jnp.einsum("iw,jw->ij", vert, ctx, precision=highest)
    sig = jax.nn.sigmoid(scores)
    negcount = jnp.zeros((rows, rows), jnp.float32)
    for sample in range(neg_rows.shape[0]):
        negcount = negcount + (neg_rows[sample][:, None] == columns).astype(jnp.float32)
    coef = cnt.astype(jnp.float32) * (1.0 - sig) - negcount * sig
    gate = tile_mask.astype(jnp.float32)[:, None, :, None]
    coef = (coef.reshape(tiles, tile, tiles, tile) * gate).reshape(rows, rows)
    new_ctx = ctx + eta * jnp.einsum("ij,iw->jw", coef, vert, precision=highest)
    new_vert = vert + eta * jnp.dot(coef, ctx, precision=highest)
    moved = passed_along(new_ctx, "blk", 1)
    return (new_vert, moved)


def on_device(vertex_embed, context_embed, counts, negatives, masks):
    vert = vertex_embed
    ctx = context_embed
    for rnd in range(ROUNDS):
        if rnd > 0:
            vert = from_partner(vert, "grp", 0)
        for step in range(ROUND_PASSES):
            index = rnd * ROUND_PASSES + step
            vert, ctx = one_pass(vert, ctx, counts[index], negatives[index], masks[index])
    return (vert, ctx)


def solution(mesh):
    placed = (
        P(("grp", "blk"), None),
        P(("grp", "blk"), None),
        P(None, ("grp", "blk"), None),
        P(None, None, ("grp", "blk")),
        P(None, ("grp", "blk"), None),
    )
    return jax.shard_map(
        on_device,
        mesh=mesh,
        in_specs=placed,
        out_specs=(P(("grp", "blk"), None), P(("grp", "blk"), None)),
        check_vma=False,
    )
```

profile of v0, /device:TPU:6, one launch (start us, length us, event | category | flops | bytes accessed | tf_op | source)
XLA Modules:
  0.0 74.0 jit_solution(5946520942031500294)
XLA Ops:
  0.6 1.0 %slice_reduce_fusion.4 = (s32[384]{0:T(512)S(1)}, s32[384]{0:T(512)S(1)}, s32[384]{0:T(512)S(1)}, s32[384]{0:T(512)S(1)}, s32[384]{0:T(512)S(1)}, /*index=5*/s32...) fusion(s32[4,5,384]{2,0,1:T(4,128)} %param.8), kind=kLoop, calls=%fused_computation.73 | loop fusion | bytes 58368 | tf_op jit(solution)/shard_map/slice | solution.py:33
  1.7 0.8 %slice_convert_fusion = (f32[1,3,3]{2,0,1:T(1,128)S(1)}, f32[1,3,3]{2,0,1:T(1,128)S(1)}, f32[1,3,3]{2,0,1:T(1,128)S(1)}, f32[1,3,3]{2,0,1:T(1,128)S(1)}) fusion(s32[4,3,3]{2,0,1:T(4,128)} %param.9), kind=kLoop, calls=%fused_computation.68 | loop fusion | flops 36 | bytes 288 | tf_op jit(solution)/shard_map/convert_element_type | solution.py:35
  2.5 0.2 mul.94
  2.7 0.0 copy-start
  2.7 0.0 copy-start.1
  2.7 2.4 %bitcast_multiply_fusion.3 = f32[384,384]{1,0:T(8,128)S(1)} fusion(f32[48,8,3,128]{3,2,1,0:T(4,128)S(1)} %bitcast.72, f32[384,256]{1,0:T(8,128)} %param.5, f32[384,256]{1,0:T(8,128)} %param.6, s32[4,384,384]{2,1,0:T(8,128)} %param.7, s32[384]{0:T(512)S(1)} %get-tuple-element.15, s32[384]{0:T(512)S(1)} %get-tuple-element.16, s32[384]{0:T(512)S(1)} %get-tuple-element.17, ...), kind=kOutput, calls=%fused_computation.35 | convolution fusion | flops 456376320 | bytes 2563584 | tf_op jit(solution)/shard_map/iw,jw->ij/dot_general | solution.py:29
  5.1 0.0 copy-start.2
  5.2 1.1 %fusion.18 = f32[384,256]{1,0:T(8,128)S(1)} fusion(f32[384,256]{1,0:T(8,128)S(1)} %copy-done.1, f32[384,384]{1,0:T(8,128)S(1)} %bitcast_multiply_fusion.3, f32[384,256]{1,0:T(8,128)S(1)} %copy-done), kind=kOutput, calls=%fused_computation.29 | convolution fusion | flops 453181440 | bytes 1769472 | tf_op jit(solution)/shard_map/ij,iw->jw/dot_general | solution.py:37
  6.3 1.9 %collective-permute-start = (f32[384,256]{1,0:T(8,128)S(1)}, f32[384,256]{1,0:T(8,128)S(1)}, u32[]{:S(2)}, u32[]{:S(2)}) collective-permute-start(f32[384,256]{1,0:T(8,128)S(1)} %fusion.18), channel_id=1, source_target_pairs={{0,1},{1,2},{2,3},{3,4},{4,5},{5,6},{6,7},{7,8},{8,9},{9,10},{10,1... | collective-permute-start | bytes 1179656 | tf_op jit(solution)/shard_map/ppermute | solution.py:15
  8.2 0.8 %fusion.19 = f32[384,256]{1,0:T(8,128)S(1)} fusion(f32[384,256]{1,0:T(8,128)S(1)} %copy-done, f32[384,384]{1,0:T(8,128)S(1)} %bitcast_multiply_fusion.3, f32[384,256]{1,0:T(8,128)S(1)} %copy-done.1), kind=kOutput, calls=%fused_computation.31 | convolution fusion | flops 453181440 | bytes 1769472 | tf_op jit(solution)/shard_map/dot_general | solution.py:38
  9.0 16.1 %collective-permute-done = f32[384,256]{1,0:T(8,128)S(1)} collective-permute-done((f32[384,256]{1,0:T(8,128)S(1)}, f32[384,256]{1,0:T(8,128)S(1)}, u32[]{:S(2)}, u32[]{:S(2)}) %collective-permute-start) | collective-permute-done | bytes 393248 | tf_op jit(solution)/shard_map/ppermute | solution.py:15
  25.2 0.2 mul.101
  25.4 1.7 %bitcast_multiply_fusion.2 = f32[384,384]{1,0:T(8,128)S(1)} fusion(f32[48,8,3,128]{3,2,1,0:T(4,128)S(1)} %bitcast.73, f32[384,256]{1,0:T(8,128)S(1)} %fusion.19, f32[384,256]{1,0:T(8,128)S(1)} %collective-permute-done, s32[4,384,384]{2,1,0:T(8,128)S(1)} %copy-done.2, s32[384]{0:T(512)S(1)} %get-tuple-element.10, s32[384]{0:T(512)S(1)} %get-tuple-element.11, ...), kind=kOutput, calls=%fused_computation.34 | convolution fusion | flops 456376320 | bytes 2563584 | tf_op jit(solution)/shard_map/iw,jw->ij/dot_general | solution.py:29
  27.1 1.1 %fusion.16 = f32[384,256]{1,0:T(8,128)S(1)} fusion(f32[384,256]{1,0:T(8,128)S(1)} %collective-permute-done, f32[384,384]{1,0:T(8,128)S(1)} %bitcast_multiply_fusion.2, f32[384,256]{1,0:T(8,128)S(1)} %fusion.19), kind=kOutput, calls=%fused_computation.25 | convolution fusion | flops 453181440 | bytes 1769472 | tf_op jit(solution)/shard_map/ij,iw->jw/dot_general | solution.py:37
  28.2 1.9 %collective-permute-start.2 = (f32[384,256]{1,0:T(8,128)S(1)}, f32[384,256]{1,0:T(8,128)S(1)}, u32[]{:S(2)}, u32[]{:S(2)}) collective-permute-start(f32[384,256]{1,0:T(8,128)S(1)} %fusion.16), channel_id=1, source_target_pairs={{0,1},{1,2},{2,3},{3,4},{4,5},{5,6},{6,7},{7,8},{8,9},{9,10},{10,1... | collective-permute-start | bytes 1179656 | tf_op jit(solution)/shard_map/ppermute | solution.py:15
  30.1 0.8 %fusion.17 = f32[384,256]{1,0:T(8,128)S(1)} fusion(f32[384,256]{1,0:T(8,128)S(1)} %fusion.19, f32[384,384]{1,0:T(8,128)S(1)} %bitcast_multiply_fusion.2, f32[384,256]{1,0:T(8,128)S(1)} %collective-permute-done), kind=kOutput, calls=%fused_computation.27 | convolution fusion | flops 453181440 | bytes 1769472 | tf_op jit(solution)/shard_map/dot_general | solution.py:38
  31.0 2.7 %collective-permute-start.1 = (f32[384,256]{1,0:T(8,128)S(1)}, f32[384,256]{1,0:T(8,128)S(1)}, u32[]{:S(2)}, u32[]{:S(2)}) collective-permute-start(f32[384,256]{1,0:T(8,128)S(1)} %fusion.17), channel_id=1, source_target_pairs={{0,64},{64,0},{128,192},{192,128},{256,320},{320,256},{384,448},{4... | collective-permute-start | bytes 1179656 | tf_op jit(solution)/shard_map/ppermute | solution.py:19
  33.7 7.5 %collective-permute-done.2 = f32[384,256]{1,0:T(8,128)S(1)} collective-permute-done((f32[384,256]{1,0:T(8,128)S(1)}, f32[384,256]{1,0:T(8,128)S(1)}, u32[]{:S(2)}, u32[]{:S(2)}) %collective-permute-start.2) | collective-permute-done | bytes 393248 | tf_op jit(solution)/shard_map/ppermute | solution.py:15
  41.2 0.2 mul.108
  41.4 1.7 %bitcast_multiply_fusion.1 = f32[384,384]{1,0:T(8,128)S(1)} fusion(f32[48,8,3,128]{3,2,1,0:T(4,128)S(1)} %bitcast.74, f32[384,256]{1,0:T(8,128)S(1)} %collective-permute-done.1, f32[384,256]{1,0:T(8,128)S(1)} %collective-permute-done.2, s32[4,384,384]{2,1,0:T(8,128)S(1)} %copy-done.2, s32[384]{0:T(512)S(1)} %get-tuple-element.5, ...), kind=kOutput, calls=%fused_computation.33 | convolution fusion | flops 456376320 | bytes 2563584 | tf_op jit(solution)/shard_map/iw,jw->ij/dot_general | solution.py:29
  43.1 1.1 %fusion.14 = f32[384,256]{1,0:T(8,128)S(1)} fusion(f32[384,256]{1,0:T(8,128)S(1)} %collective-permute-done.2, f32[384,384]{1,0:T(8,128)S(1)} %bitcast_multiply_fusion.1, f32[384,256]{1,0:T(8,128)S(1)} %collective-permute-done.1), kind=kOutput, calls=%fused_computation.21 | convolution fusion | flops 453181440 | bytes 1769472 | tf_op jit(solution)/shard_map/ij,iw->jw/dot_general | solution.py:37
  44.2 1.9 %collective-permute-start.3 = (f32[384,256]{1,0:T(8,128)S(1)}, f32[384,256]{1,0:T(8,128)S(1)}, u32[]{:S(2)}, u32[]{:S(2)}) collective-permute-start(f32[384,256]{1,0:T(8,128)S(1)} %fusion.14), channel_id=1, source_target_pairs={{0,1},{1,2},{2,3},{3,4},{4,5},{5,6},{6,7},{7,8},{8,9},{9,10},{10,1... | collective-permute-start | bytes 1179656 | tf_op jit(solution)/shard_map/ppermute | solution.py:15
  46.2 0.7 slice_reduce_fusion.1
  46.9 0.8 %fusion.15 = f32[384,256]{1,0:T(8,128)S(1)} fusion(f32[384,256]{1,0:T(8,128)S(1)} %collective-permute-done.1, f32[384,384]{1,0:T(8,128)S(1)} %bitcast_multiply_fusion.1, f32[384,256]{1,0:T(8,128)S(1)} %collective-permute-done.2), kind=kOutput, calls=%fused_computation.23 | convolution fusion | flops 453181440 | bytes 1769472 | tf_op jit(solution)/shard_map/dot_general | solution.py:38
  47.7 9.6 %collective-permute-done.3 = f32[384,256]{1,0:T(8,128)S(1)} collective-permute-done((f32[384,256]{1,0:T(8,128)S(1)}, f32[384,256]{1,0:T(8,128)S(1)}, u32[]{:S(2)}, u32[]{:S(2)}) %collective-permute-start.3) | collective-permute-done | bytes 393248 | tf_op jit(solution)/shard_map/ppermute | solution.py:15
  57.2 0.2 mul.115
  57.4 1.7 %bitcast_multiply_fusion = f32[384,384]{1,0:T(8,128)S(1)} fusion(f32[48,8,3,128]{3,2,1,0:T(4,128)S(1)} %bitcast.75, f32[384,256]{1,0:T(8,128)S(1)} %fusion.15, f32[384,256]{1,0:T(8,128)S(1)} %collective-permute-done.3, s32[4,384,384]{2,1,0:T(8,128)S(1)} %copy-done.2, s32[384]{0:T(512)S(1)} %get-tuple-element.20, s32[384]{0:T(512)S(1)} %slice_reduce_fusion.1, ...), kind=kOutput, calls=%fused_computation.32 | convolution fusion | flops 456376320 | bytes 2563584 | tf_op jit(solution)/shard_map/iw,jw->ij/dot_general | solution.py:29
  59.1 1.1 %fusion.12 = f32[384,256]{1,0:T(8,128)S(1)} fusion(f32[384,256]{1,0:T(8,128)S(1)} %collective-permute-done.3, f32[384,384]{1,0:T(8,128)S(1)} %bitcast_multiply_fusion, f32[384,256]{1,0:T(8,128)S(1)} %fusion.15), kind=kOutput, calls=%fused_computation.17 | convolution fusion | flops 453181440 | bytes 1769472 | tf_op jit(solution)/shard_map/ij,iw->jw/dot_general | solution.py:37
  60.2 1.9 %collective-permute-start.4 = (f32[384,256]{1,0:T(8,128)S(1)}, f32[384,256]{1,0:T(8,128)S(1)}, u32[]{:S(2)}, u32[]{:S(2)}) collective-permute-start(f32[384,256]{1,0:T(8,128)S(1)} %fusion.12), channel_id=1, source_target_pairs={{0,1},{1,2},{2,3},{3,4},{4,5},{5,6},{6,7},{7,8},{8,9},{9,10},{10,1... | collective-permute-start | bytes 1179656 | tf_op jit(solution)/shard_map/ppermute | solution.py:15
  62.2 1.5 %fusion.13 = f32[384,256]{1,0:T(8,128)} fusion(f32[384,256]{1,0:T(8,128)S(1)} %fusion.15, f32[384,384]{1,0:T(8,128)S(1)} %bitcast_multiply_fusion, f32[384,256]{1,0:T(8,128)S(1)} %collective-permute-done.3), kind=kOutput, calls=%fused_computation.19 | convolution fusion | flops 453181440 | bytes 1769472 | tf_op jit(solution)/shard_map/dot_general | solution.py:38
  63.7 9.5 %collective-permute-done.4 = f32[384,256]{1,0:T(8,128)S(1)} collective-permute-done((f32[384,256]{1,0:T(8,128)S(1)}, f32[384,256]{1,0:T(8,128)S(1)}, u32[]{:S(2)}, u32[]{:S(2)}) %collective-permute-start.4) | collective-permute-done | bytes 393248 | tf_op jit(solution)/shard_map/ppermute | solution.py:15
  73.2 0.7 %copy.24 = f32[384,256]{1,0:T(8,128)} copy(f32[384,256]{1,0:T(8,128)S(1)} %collective-permute-done.4) | data formatting | bytes 786432
  (6 shorter events, 0.0 us)
Async XLA Ops:
  2.7 2.4 %copy-start = (f32[384,256]{1,0:T(8,128)S(1)}, f32[384,256]{1,0:T(8,128)}, u32[]{:S(2)}) copy-start(f32[384,256]{1,0:T(8,128)} %param.5) | copy-start | bytes 1179652
  2.7 2.4 %copy-start.1 = (f32[384,256]{1,0:T(8,128)S(1)}, f32[384,256]{1,0:T(8,128)}, u32[]{:S(2)}) copy-start(f32[384,256]{1,0:T(8,128)} %param.6) | copy-start | bytes 1179652
  5.1 20.2 %copy-start.2 = (s32[4,384,384]{2,1,0:T(8,128)S(1)}, s32[4,384,384]{2,1,0:T(8,128)}, u32[]{:S(2)}) copy-start(s32[4,384,384]{2,1,0:T(8,128)} %param.7) | copy-start | bytes 7077892
  6.3 18.9 %collective-permute-start = (f32[384,256]{1,0:T(8,128)S(1)}, f32[384,256]{1,0:T(8,128)S(1)}, u32[]{:S(2)}, u32[]{:S(2)}) collective-permute-start(f32[384,256]{1,0:T(8,128)S(1)} %fusion.18), channel_id=1, source_target_pairs={{0,1},{1,2},{2,3},{3,4},{4,5},{5,6},{6,7},{7,8},{8,9},{9,10},{10,1... | collective-permute-start | bytes 1179656 | tf_op jit(solution)/shard_map/ppermute | solution.py:15
  28.2 13.0 %collective-permute-start.2 = (f32[384,256]{1,0:T(8,128)S(1)}, f32[384,256]{1,0:T(8,128)S(1)}, u32[]{:S(2)}, u32[]{:S(2)}) collective-permute-start(f32[384,256]{1,0:T(8,128)S(1)} %fusion.16), channel_id=1, source_target_pairs={{0,1},{1,2},{2,3},{3,4},{4,5},{5,6},{6,7},{7,8},{8,9},{9,10},{10,1... | collective-permute-start | bytes 1179656 | tf_op jit(solution)/shard_map/ppermute | solution.py:15
  31.0 10.3 %collective-permute-start.1 = (f32[384,256]{1,0:T(8,128)S(1)}, f32[384,256]{1,0:T(8,128)S(1)}, u32[]{:S(2)}, u32[]{:S(2)}) collective-permute-start(f32[384,256]{1,0:T(8,128)S(1)} %fusion.17), channel_id=1, source_target_pairs={{0,64},{64,0},{128,192},{192,128},{256,320},{320,256},{384,448},{4... | collective-permute-start | bytes 1179656 | tf_op jit(solution)/shard_map/ppermute | solution.py:19
  44.2 13.0 %collective-permute-start.3 = (f32[384,256]{1,0:T(8,128)S(1)}, f32[384,256]{1,0:T(8,128)S(1)}, u32[]{:S(2)}, u32[]{:S(2)}) collective-permute-start(f32[384,256]{1,0:T(8,128)S(1)} %fusion.14), channel_id=1, source_target_pairs={{0,1},{1,2},{2,3},{3,4},{4,5},{5,6},{6,7},{7,8},{8,9},{9,10},{10,1... | collective-permute-start | bytes 1179656 | tf_op jit(solution)/shard_map/ppermute | solution.py:15
  60.2 13.0 %collective-permute-start.4 = (f32[384,256]{1,0:T(8,128)S(1)}, f32[384,256]{1,0:T(8,128)S(1)}, u32[]{:S(2)}, u32[]{:S(2)}) collective-permute-start(f32[384,256]{1,0:T(8,128)S(1)} %fusion.12), channel_id=1, source_target_pairs={{0,1},{1,2},{2,3},{3,4},{4,5},{5,6},{6,7},{7,8},{8,9},{9,10},{10,1... | collective-permute-start | bytes 1179656 | tf_op jit(solution)/shard_map/ppermute | solution.py:15
where the time goes:
time: 74.4 us; the launch traced here: 74 us
  waiting for transfers between devices  42.8 us (58%)
  matrix products  16 us (22%)
  starting transfers between devices  10.4 us (14%)
  local copies, waits for them, and re-layouts  3.18 us (4%)
  other arithmetic  0.85 us (1%)
  between operations  0.84 us (1%)
    ppermute x4, waiting for transfers between devices, passed_along(): return lax.ppermute(value, axis, pairs)  42.7 us
    ppermute x4, starting transfers between devices, passed_along(): return lax.ppermute(value, axis, pairs)  7.68 us
    dot_general x4, matrix products, one_pass(): scores = jnp.einsum('iw,jw->ij', vert, ctx, precision=highest)  7.51 us
    dot_general x4, matrix products, one_pass(): new_ctx = ctx + eta * jnp.einsum('ij,iw->jw', coef, vert, precision=highest)  4.52 us
    dot_general x4, matrix products, one_pass(): new_vert = vert + eta * jnp.dot(coef, ctx, precision=highest)  3.94 us
    ppermute x1, starting transfers between devices, from_partner(): lax.ppermute(value, axis, [(i, i ^ 1 << stride) for i in range(lax.axis_s...  2.73 us
    slice x2, local copies, waits for them, and re-layouts, one_pass(): neg_rows[sample][:, None] == columns  1.73 us
  transfers between devices with their start and end apart: 5, of which 4 were waited for; matrix products, arithmetic and copies ran while one was open for 6% of the time, Pallas kernels for 0%

commit v1 on v0

v1 whole, which is shorter than its diff:
```python
import functools
import math

import jax
import jax.numpy as jnp
from jax import lax
from jax.experimental import pallas as pl
from jax.experimental.pallas import tpu as pltpu
from jax.sharding import PartitionSpec as P


F32 = jnp.float32
BF16 = jnp.bfloat16
NT = (((1,), (1,)), ((), ()))
NN = (((1,), (0,)), ((), ()))


def halves(x):
    high = x.astype(BF16)
    return high, (x - high.astype(F32)).astype(BF16)


def product(a, b, dims):
    dot = functools.partial(lax.dot_general, dimension_numbers=dims, preferred_element_type=F32)
    return dot(a[0], b[0]) + (dot(a[0], b[1]) + dot(a[1], b[0]))


def tables(step, slot, counts, neg_ref, mask_ref, base_ref, slope_ref):
    rows = counts.shape[0]
    tiles = mask_ref.shape[0]
    tile = rows // tiles
    scale = 0.125 / math.sqrt(rows)
    neg = jnp.transpose(neg_ref[:, step].astype(F32)).astype(jnp.int32)
    for ti in range(tiles):
        here = slice(ti * tile, (ti + 1) * tile)
        picks = [jnp.broadcast_to(neg[here, k : k + 1], (tile, tile)) for k in range(neg.shape[1])]
        for tj in range(tiles):
            there = slice(tj * tile, (tj + 1) * tile)
            column = lax.broadcasted_iota(jnp.int32, (tile, tile), 1) + tj * tile
            negcount = sum((pick == column).astype(F32) for pick in picks)
            cnt = counts[here, there].astype(F32)
            gate = mask_ref[ti, step, tj].astype(F32) * scale
            base_ref[slot, here, there] = (cnt - negcount) * gate
            slope_ref[slot, here, there] = (cnt + negcount) * gate


def pass_body(vert, ctx, base, slope):
    vs, cs = halves(vert), halves(ctx)
    coef = base - slope * jnp.tanh(0.5 * product(vs, cs, NT))
    new_ctx = ctx + product(halves(jnp.transpose(coef)), vs, NN)
    new_vert = vert + product(halves(coef), cs, NN)
    return new_vert, new_ctx


def first_kernel(vert_hbm, ctx_hbm, counts_hbm, neg_ref, mask_ref, new_vert_ref, new_ctx_ref, vert, ctx, cnt, base, slope, sems):
    copies = [
        pltpu.make_async_copy(counts_hbm.at[0], cnt, sems.at[0]),
        pltpu.make_async_copy(vert_hbm, vert, sems.at[1]),
        pltpu.make_async_copy(ctx_hbm, ctx, sems.at[2]),
    ]
    for copy in copies:
        copy.start()
    copies[0].wait()
    tables(0, 0, cnt, neg_ref, mask_ref, base, slope)
    copies[1].wait()
    copies[2].wait()
    new_vert_ref[...], new_ctx_ref[...] = pass_body(vert[...], ctx[...], base[0], slope[0])


def rest_kernel(after, counts_hbm, neg_ref, mask_ref, base_ref, slope_ref, cnt, sems):
    copies = [pltpu.make_async_copy(counts_hbm.at[i + 1], cnt.at[i], sems.at[i]) for i in range(cnt.shape[0])]
    for copy in copies:
        copy.start()
    for i, copy in enumerate(copies):
        copy.wait()
        tables(i + 1, i, cnt.at[i], neg_ref, mask_ref, base_ref, slope_ref)


def pass_kernel(step, core, after, vert_ref, ctx_ref, base_ref, slope_ref, new_vert_ref, new_ctx_ref):
    @pl.when(lax.axis_index("blk") % 2 == core)
    def _():
        new_vert_ref[...], new_ctx_ref[...] = pass_body(vert_ref[...], ctx_ref[...], base_ref[step - 1], slope_ref[step - 1])


def in_vmem(x):
    return pltpu.with_memory_space_constraint(x, pltpu.VMEM)


def in_hbm(x):
    return pltpu.with_memory_space_constraint(x, pltpu.HBM)


VMEM_SPEC = pl.BlockSpec(memory_space=pltpu.VMEM)
SMEM_SPEC = pl.BlockSpec(memory_space=pltpu.SMEM)
HBM_SPEC = pl.BlockSpec(memory_space=pltpu.HBM)
ANY_SPEC = pl.BlockSpec(memory_space=pl.ANY)


def params(mib):
    return pltpu.CompilerParams(vmem_limit_bytes=mib << 20)


def on_device(vertex_embed, context_embed, counts, negatives, masks):
    part = vertex_embed.shape
    passes, rows = counts.shape[0], counts.shape[1]
    negatives = jnp.transpose(negatives, (1, 0, 2))
    masks = jnp.transpose(masks, (1, 0, 2))
    state = pltpu.VMEM(part, F32)
    table = pltpu.VMEM((passes - 1, rows, rows), F32)
    square = pltpu.VMEM((1, rows, rows), F32)
    vert, out = pl.pallas_call(
        first_kernel,
        out_shape=(state, state),
        in_specs=[HBM_SPEC] * 3 + [VMEM_SPEC, SMEM_SPEC],
        out_specs=(VMEM_SPEC,) * 2,
        scratch_shapes=[state, state, pltpu.VMEM((rows, rows), jnp.int32), square, square, pltpu.SemaphoreType.DMA((3,))],
        compiler_params=params(20),
        name="first",
    )(in_hbm(vertex_embed), in_hbm(context_embed), in_hbm(counts), negatives, masks)
    base, slope = pl.pallas_call(
        rest_kernel,
        out_shape=(table, table),
        in_specs=[ANY_SPEC, HBM_SPEC, VMEM_SPEC, SMEM_SPEC],
        out_specs=(VMEM_SPEC,) * 2,
        scratch_shapes=[pltpu.VMEM((passes - 1, rows, rows), jnp.int32), pltpu.SemaphoreType.DMA((passes - 1,))],
        compiler_params=params(20),
        name="rest",
    )(vert, in_hbm(counts), negatives, masks)

    def one_pass(step, core, after, vert, ctx):
        return pl.pallas_call(
            functools.partial(pass_kernel, step, core),
            out_shape=(state, state),
            in_specs=[ANY_SPEC] + [VMEM_SPEC] * 4,
            out_specs=(VMEM_SPEC,) * 2,
            compiler_params=params(20),
        )(after, in_vmem(vert), in_vmem(ctx), in_vmem(base), in_vmem(slope))

    n_grp, n_blk = lax.axis_size("grp"), lax.axis_size("blk")

    def within_chip(value):
        return lax.ppermute(value, "blk", [(b, b + 1) for b in range(0, n_blk, 2)])

    def between_chips(value):
        return lax.ppermute(value, "blk", [(b, (b + 1) % n_blk) for b in range(1, n_blk, 2)])

    def swapped(core, value):
        pairs = [(g * n_blk + b, (g ^ 1) * n_blk + b) for g in range(n_grp) for b in range(core, n_blk, 2)]
        return lax.ppermute(value, ("grp", "blk"), pairs)

    x0 = between_chips(out)
    on0 = within_chip(out)
    vert_a, out_a = one_pass(1, 1, vert, vert, on0)
    x1 = between_chips(out_a)
    moved_a = swapped(1, vert_a)
    vert_b, out_b = one_pass(1, 0, vert_a, vert, x0)
    moved_b = swapped(0, vert_b)
    on1 = within_chip(out_b)
    vert_a, out_a = one_pass(2, 1, vert_b, moved_a, on1)
    x2 = between_chips(out_a)
    vert_b, out_b = one_pass(2, 0, vert_a, moved_b, x1)
    on2 = within_chip(out_b)
    vert_a, out_a = one_pass(3, 1, vert_b, vert_a, on2)
    x3 = between_chips(out_a)
    vert_b, out_b = one_pass(3, 0, vert_a, vert_b, x2)
    on3 = within_chip(out_b)
    odd = lax.axis_index("blk") % 2 == 1
    return jnp.where(odd, vert_a, vert_b), jnp.where(odd, on3, x3)


def solution(mesh):
    placed = (
        P(("grp", "blk"), None),
        P(("grp", "blk"), None),
        P(None, ("grp", "blk"), None),
        P(None, None, ("grp", "blk")),
        P(None, ("grp", "blk"), None),
    )

    return jax.shard_map(
        on_device,
        mesh=mesh,
        in_specs=placed,
        out_specs=(P(("grp", "blk"), None), P(("grp", "blk"), None)),
        check_vma=False,
    )
```

time: 74.4 us -> 76.4 us (1.027)
  matrix products: 16 us -> 0 us
  Pallas kernels: 0 us -> 11.2 us
  starting transfers between devices: 10.4 us -> 14.3 us
  waiting for transfers between devices: 42.8 us -> 46.3 us
  local copies, waits for them, and re-layouts: 3.18 us -> 1.44 us
    dot_general x12 -> x0, matrix products: 16 us -> none  [the longest x4 7.51 us: one_pass(): scores = jnp.einsum('iw,jw->ij', vert, ctx, precision=highest)]
    pallas_call x0 -> x8, Pallas kernels: none -> 11.2 us  [the longest x6 3.86 us: one_pass(): pl.pallas_call(functools.partial(pass_kernel, step, core), out_shape=(sta...]
    ppermute x5 -> x10, starting transfers between devices: 10.4 us -> 14.3 us  [the longest x4 5.7 us: within_chip(): return lax.ppermute(value, 'blk', [(b, b + 1) for b in range(0, n_blk, 2)])]
    ppermute x5 -> x10, waiting for transfers between devices: 42.8 us -> 46.3 us  [the longest x4 40.7 us: between_chips(): lax.ppermute(value, 'blk', [(b, (b + 1) % n_blk) for b in range(1, n_blk,...]
    slice x2 -> x0, local copies, waits for them, and re-layouts: 1.73 us -> none  [one_pass(): neg_rows[sample][:, None] == columns]
    select_n x0 -> x2, other arithmetic: none -> 1.59 us  [on_device(): return (jnp.where(odd, vert_a, vert_b), jnp.where(odd, on3, x3))]
    convert_element_type x1 -> x0, other arithmetic: 0.85 us -> none  [one_pass(): gate = tile_mask.astype(jnp.float32)[:, None, :, None]]
  transfers between devices with their start and end apart: 5 -> 10, of which waited for: 4 -> 5; matrix products, arithmetic and copies ran while one was open for 6% -> 1% of each run, Pallas kernels for 0% -> 7%
where the time goes in v1:
time: 76.4 us; the launch traced here: 75.6 us
  waiting for transfers between devices  46.3 us (61%)
  starting transfers between devices  14.3 us (19%)
  Pallas kernels  11.2 us (15%)
  other arithmetic  1.59 us (2%)
  local copies, waits for them, and re-layouts  1.44 us (2%)
  between operations  0.82 us (1%)
    ppermute x4, waiting for transfers between devices, between_chips(): lax.ppermute(value, 'blk', [(b, (b + 1) % n_blk) for b in range(1, n_blk,...  40.7 us
    ppermute x4, starting transfers between devices, within_chip(): return lax.ppermute(value, 'blk', [(b, b + 1) for b in range(0, n_blk, 2)])  5.7 us
    ppermute x2, waiting for transfers between devices, swapped(): return lax.ppermute(value, ('grp', 'blk'), pairs)  5.58 us
    ppermute x4, starting transfers between devices, between_chips(): lax.ppermute(value, 'blk', [(b, (b + 1) % n_blk) for b in range(1, n_blk,...  5.17 us
    pallas_call x6, Pallas kernels, one_pass(): pl.pallas_call(functools.partial(pass_kernel, step, core), out_shape=(sta...  3.86 us
    pallas_call x1, Pallas kernels, on_device(): pl.pallas_call(rest_kernel, out_shape=(table, table), in_specs=[ANY_SPEC,...  3.65 us
    pallas_call x1, Pallas kernels, on_device(): pl.pallas_call(first_kernel, out_shape=(state, state), in_specs=[HBM_SPEC...  3.64 us
    ppermute x2, starting transfers between devices, swapped(): return lax.ppermute(value, ('grp', 'blk'), pairs)  3.43 us
  transfers between devices with their start and end apart: 10, of which 5 were waited for; matrix products, arithmetic and copies ran while one was open for 1% of the time, Pallas kernels for 7%

profile of v1, /device:TPU:6, one launch (start us, length us, event | category | flops | bytes accessed | tf_op | source)
XLA Modules:
  0.0 75.6 jit_solution(10296834234336073598)
XLA Ops:
  0.6 0.0 copy-start
  0.6 0.7 copy-done
  1.4 0.0 copy-start.1
  1.4 0.7 copy-done.1
  2.1 3.6 %first.1 = (f32[384,256]{1,0:T(8,128)S(1)}, f32[384,256]{1,0:T(8,128)S(1)}) custom-call(f32[384,256]{1,0:T(8,128)} %vert_hbm.1, f32[384,256]{1,0:T(8,128)} %ctx_hbm.1, s32[4,384,384]{2,1,0:T(8,128)} %counts_hbm.3, s32[5,4,384]{2,1,0:T(4,128)S(1)} %bitcast.2, s32[3,4,3]{2,1,0:T(4,128)S(1)} %bitcast.4), custom_call_target="tpu_custom_call" | custom-call | tf_op jit(solution)/shard_map/first/pallas_call | solution.py:111
  5.7 1.8 %collective-permute-start = (f32[384,256]{1,0:T(8,128)S(1)}, f32[384,256]{1,0:T(8,128)S(1)}, u32[]{:S(2)}, u32[]{:S(2)}) collective-permute-start(f32[384,256]{1,0:T(8,128)S(1)} %get-tuple-element.19), channel_id=1, source_target_pairs={{0,1},{2,3},{4,5},{6,7},{8,9},{10,11},{12,13},{14,15},{16,17},{18,... | collective-permute-start | bytes 1179656 | tf_op jit(solution)/shard_map/ppermute | solution.py:142
  7.5 1.3 %collective-permute-start.1 = (f32[384,256]{1,0:T(8,128)S(1)}, f32[384,256]{1,0:T(8,128)S(1)}, u32[]{:S(2)}, u32[]{:S(2)}) collective-permute-start(f32[384,256]{1,0:T(8,128)S(1)} %get-tuple-element.19), channel_id=1, source_target_pairs={{1,2},{3,4},{5,6},{7,8},{9,10},{11,12},{13,14},{15,16},{17,18},{19... | collective-permute-start | bytes 1179656 | tf_op jit(solution)/shard_map/ppermute | solution.py:145
  8.8 3.6 %rest.1 = (f32[3,384,384]{2,1,0:T(8,128)S(1)}, f32[3,384,384]{2,1,0:T(8,128)S(1)}) custom-call(f32[384,256]{1,0:T(8,128)S(1)} %get-tuple-element.18.after.vert_ref, s32[4,384,384]{2,1,0:T(8,128)} %counts_hbm.3, s32[5,4,384]{2,1,0:T(4,128)S(1)} %bitcast.3, s32[3,4,3]{2,1,0:T(4,128)S(1)} %bitcast.5), custom_call_target="tpu_custom_call" | custom-call | tf_op jit(solution)/shard_map/rest/pallas_call | solution.py:120
  12.5 0.0 collective-permute-done.ctx_ref
  12.5 0.7 collective-permute-start.2
  13.2 12.1 %collective-permute-done.1.ctx_ref = f32[384,256]{1,0:T(8,128)S(1)} collective-permute-done((f32[384,256]{1,0:T(8,128)S(1)}, f32[384,256]{1,0:T(8,128)S(1)}, u32[]{:S(2)}, u32[]{:S(2)}) %collective-permute-start.1) | collective-permute-done | bytes 393248 | tf_op jit(solution)/shard_map/ppermute | solution.py:145
  25.3 1.3 %shard_map.69 = (f32[384,256]{1,0:T(8,128)S(1)}, f32[384,256]{1,0:T(8,128)S(1)}) custom-call(f32[384,256]{1,0:T(8,128)S(1)} %get-tuple-element.22.after, f32[384,256]{1,0:T(8,128)S(1)} %get-tuple-element.18.after.vert_ref, f32[384,256]{1,0:T(8,128)S(1)} %collective-permute-done.1.ctx_ref, f32[3,384,384]{2,1,0:T(8,128)S(1)} %get-tuple-element.20.base_ref, ...), custom_call_target="tpu_custom_call" | custom-call | tf_op jit(solution)/shard_map/pallas_call | solution.py:131
  26.6 1.3 %collective-permute-start.3 = (f32[384,256]{1,0:T(8,128)S(1)}, f32[384,256]{1,0:T(8,128)S(1)}, u32[]{:S(2)}, u32[]{:S(2)}) collective-permute-start(f32[384,256]{1,0:T(8,128)S(1)} %get-tuple-element.24), channel_id=1, source_target_pairs={{0,1},{2,3},{4,5},{6,7},{8,9},{10,11},{12,13},{14,15},{16,17},{18,... | collective-permute-start | bytes 1179656 | tf_op jit(solution)/shard_map/ppermute | solution.py:142
  27.9 2.7 %collective-permute-start.4 = (f32[384,256]{1,0:T(8,128)S(1)}, f32[384,256]{1,0:T(8,128)S(1)}, u32[]{:S(2)}, u32[]{:S(2)}) collective-permute-start(f32[384,256]{1,0:T(8,128)S(1)} %get-tuple-element.23.after), channel_id=1, source_target_pairs={{0,64},{2,66},{4,68},{6,70},{8,72},{10,74},{12,76},{14,78},{16,80}... | collective-permute-start | bytes 1179656 | tf_op jit(solution)/shard_map/ppermute | solution.py:149
  30.6 1.3 %collective-permute-start.5 = (f32[384,256]{1,0:T(8,128)S(1)}, f32[384,256]{1,0:T(8,128)S(1)}, u32[]{:S(2)}, u32[]{:S(2)}) collective-permute-start(f32[384,256]{1,0:T(8,128)S(1)} %get-tuple-element.26), channel_id=1, source_target_pairs={{1,2},{3,4},{5,6},{7,8},{9,10},{11,12},{13,14},{15,16},{17,18},{19... | collective-permute-start | bytes 1179656 | tf_op jit(solution)/shard_map/ppermute | solution.py:145
  31.9 0.0 collective-permute-done.3.ctx_ref
  31.9 0.0 collective-permute-done.2.vert_ref
  32.0 5.6 %collective-permute-done.4.vert_ref = f32[384,256]{1,0:T(8,128)S(1)} collective-permute-done((f32[384,256]{1,0:T(8,128)S(1)}, f32[384,256]{1,0:T(8,128)S(1)}, u32[]{:S(2)}, u32[]{:S(2)}) %collective-permute-start.4) | collective-permute-done | bytes 393248 | tf_op jit(solution)/shard_map/ppermute | solution.py:149
  37.5 6.1 %collective-permute-done.5.ctx_ref = f32[384,256]{1,0:T(8,128)S(1)} collective-permute-done((f32[384,256]{1,0:T(8,128)S(1)}, f32[384,256]{1,0:T(8,128)S(1)}, u32[]{:S(2)}, u32[]{:S(2)}) %collective-permute-start.5) | collective-permute-done | bytes 393248 | tf_op jit(solution)/shard_map/ppermute | solution.py:145
  43.6 1.3 %shard_map.71 = (f32[384,256]{1,0:T(8,128)S(1)}, f32[384,256]{1,0:T(8,128)S(1)}) custom-call(f32[384,256]{1,0:T(8,128)S(1)} %get-tuple-element.25.after.vert_ref, f32[384,256]{1,0:T(8,128)S(1)} %collective-permute-done.4.vert_ref, f32[384,256]{1,0:T(8,128)S(1)} %collective-permute-done.5.ctx_ref, f32[3,384,384]{2,1,0:T(8,128)S(1)} %get-tuple-element.20.base_ref, ...), custom_call_target="tpu_custom_call" | custom-call | tf_op jit(solution)/shard_map/pallas_call | solution.py:131
  44.9 1.3 %collective-permute-start.6 = (f32[384,256]{1,0:T(8,128)S(1)}, f32[384,256]{1,0:T(8,128)S(1)}, u32[]{:S(2)}, u32[]{:S(2)}) collective-permute-start(f32[384,256]{1,0:T(8,128)S(1)} %get-tuple-element.28), channel_id=1, source_target_pairs={{0,1},{2,3},{4,5},{6,7},{8,9},{10,11},{12,13},{14,15},{16,17},{18,... | collective-permute-start | bytes 1179656 | tf_op jit(solution)/shard_map/ppermute | solution.py:142
  46.2 1.3 %collective-permute-start.7 = (f32[384,256]{1,0:T(8,128)S(1)}, f32[384,256]{1,0:T(8,128)S(1)}, u32[]{:S(2)}, u32[]{:S(2)}) collective-permute-start(f32[384,256]{1,0:T(8,128)S(1)} %get-tuple-element.30), channel_id=1, source_target_pairs={{1,2},{3,4},{5,6},{7,8},{9,10},{11,12},{13,14},{15,16},{17,18},{19... | collective-permute-start | bytes 1179656 | tf_op jit(solution)/shard_map/ppermute | solution.py:145
  47.5 0.0 collective-permute-done.6.ctx_ref
  47.6 11.7 %collective-permute-done.7.ctx_ref = f32[384,256]{1,0:T(8,128)S(1)} collective-permute-done((f32[384,256]{1,0:T(8,128)S(1)}, f32[384,256]{1,0:T(8,128)S(1)}, u32[]{:S(2)}, u32[]{:S(2)}) %collective-permute-start.7) | collective-permute-done | bytes 393248 | tf_op jit(solution)/shard_map/ppermute | solution.py:145
  59.2 1.3 %shard_map.73 = (f32[384,256]{1,0:T(8,128)S(1)}, f32[384,256]{1,0:T(8,128)S(1)}) custom-call(f32[384,256]{1,0:T(8,128)S(1)} %get-tuple-element.29.after, f32[384,256]{1,0:T(8,128)S(1)} %get-tuple-element.27.after.vert_ref, f32[384,256]{1,0:T(8,128)S(1)} %collective-permute-done.7.ctx_ref, f32[3,384,384]{2,1,0:T(8,128)S(1)} %get-tuple-element.20.base_ref, ...), custom_call_target="tpu_custom_call" | custom-call | tf_op jit(solution)/shard_map/pallas_call | solution.py:131
  60.5 1.3 %collective-permute-start.8 = (f32[384,256]{1,0:T(8,128)S(1)}, f32[384,256]{1,0:T(8,128)S(1)}, u32[]{:S(2)}, u32[]{:S(2)}) collective-permute-start(f32[384,256]{1,0:T(8,128)S(1)} %get-tuple-element.32), channel_id=1, source_target_pairs={{0,1},{2,3},{4,5},{6,7},{8,9},{10,11},{12,13},{14,15},{16,17},{18,... | collective-permute-start | bytes 1179656 | tf_op jit(solution)/shard_map/ppermute | solution.py:142
  61.8 1.3 %collective-permute-start.9 = (f32[384,256]{1,0:T(8,128)S(1)}, f32[384,256]{1,0:T(8,128)S(1)}, u32[]{:S(2)}, u32[]{:S(2)}) collective-permute-start(f32[384,256]{1,0:T(8,128)S(1)} %get-tuple-element.33), channel_id=1, source_target_pairs={{1,2},{3,4},{5,6},{7,8},{9,10},{11,12},{13,14},{15,16},{17,18},{19... | collective-permute-start | bytes 1179656 | tf_op jit(solution)/shard_map/ppermute | solution.py:145
  63.1 0.8 %broadcast_select_fusion.1 = f32[384,256]{1,0:T(8,128)} fusion(f32[384,256]{1,0:T(8,128)S(1)} %get-tuple-element.29.after, f32[384,256]{1,0:T(8,128)S(1)} %get-tuple-element.31, pred[]{:T(512)S(6)} %eq.5), kind=kLoop, calls=%fused_computation.1 | loop fusion | flops 98304 | bytes 1179649 | tf_op jit(solution)/shard_map/jit(_where)/select_n | solution.py:168
  63.9 0.0 collective-permute-done.8
  63.9 10.9 %collective-permute-done.9 = f32[384,256]{1,0:T(8,128)S(1)} collective-permute-done((f32[384,256]{1,0:T(8,128)S(1)}, f32[384,256]{1,0:T(8,128)S(1)}, u32[]{:S(2)}, u32[]{:S(2)}) %collective-permute-start.9) | collective-permute-done | bytes 393248 | tf_op jit(solution)/shard_map/ppermute | solution.py:145
  74.8 0.8 %broadcast_select_fusion = f32[384,256]{1,0:T(8,128)} fusion(f32[384,256]{1,0:T(8,128)S(1)} %collective-permute-done.8, f32[384,256]{1,0:T(8,128)S(1)} %collective-permute-done.9, pred[]{:T(512)S(6)} %eq.5), kind=kLoop, calls=%fused_computation | loop fusion | flops 98304 | bytes 1179649 | tf_op jit(solution)/shard_map/jit(_where)/select_n | solution.py:168
  (3 shorter events, 0.1 us)
Async XLA Ops:
  0.6 0.8 copy-start
  1.4 0.7 copy-start.1
  5.7 6.7 %collective-permute-start = (f32[384,256]{1,0:T(8,128)S(1)}, f32[384,256]{1,0:T(8,128)S(1)}, u32[]{:S(2)}, u32[]{:S(2)}) collective-permute-start(f32[384,256]{1,0:T(8,128)S(1)} %get-tuple-element.19), channel_id=1, source_target_pairs={{0,1},{2,3},{4,5},{6,7},{8,9},{10,11},{12,13},{14,15},{16,17},{18,... | collective-permute-start | bytes 1179656 | tf_op jit(solution)/shard_map/ppermute | solution.py:142
  7.5 17.8 %collective-permute-start.1 = (f32[384,256]{1,0:T(8,128)S(1)}, f32[384,256]{1,0:T(8,128)S(1)}, u32[]{:S(2)}, u32[]{:S(2)}) collective-permute-start(f32[384,256]{1,0:T(8,128)S(1)} %get-tuple-element.19), channel_id=1, source_target_pairs={{1,2},{3,4},{5,6},{7,8},{9,10},{11,12},{13,14},{15,16},{17,18},{19... | collective-permute-start | bytes 1179656 | tf_op jit(solution)/shard_map/ppermute | solution.py:145
  12.5 19.4 %collective-permute-start.2 = (f32[384,256]{1,0:T(8,128)S(1)}, f32[384,256]{1,0:T(8,128)S(1)}, u32[]{:S(2)}, u32[]{:S(2)}) collective-permute-start(f32[384,256]{1,0:T(8,128)S(1)} %get-tuple-element.22.after), channel_id=1, source_target_pairs={{1,65},{3,67},{5,69},{7,71},{9,73},{11,75},{13,77},{15,79},{17,81}... | collective-permute-start | bytes 1179656 | tf_op jit(solution)/shard_map/ppermute | solution.py:149
  26.6 5.4 %collective-permute-start.3 = (f32[384,256]{1,0:T(8,128)S(1)}, f32[384,256]{1,0:T(8,128)S(1)}, u32[]{:S(2)}, u32[]{:S(2)}) collective-permute-start(f32[384,256]{1,0:T(8,128)S(1)} %get-tuple-element.24), channel_id=1, source_target_pairs={{0,1},{2,3},{4,5},{6,7},{8,9},{10,11},{12,13},{14,15},{16,17},{18,... | collective-permute-start | bytes 1179656 | tf_op jit(solution)/shard_map/ppermute | solution.py:142
  27.9 9.7 %collective-permute-start.4 = (f32[384,256]{1,0:T(8,128)S(1)}, f32[384,256]{1,0:T(8,128)S(1)}, u32[]{:S(2)}, u32[]{:S(2)}) collective-permute-start(f32[384,256]{1,0:T(8,128)S(1)} %get-tuple-element.23.after), channel_id=1, source_target_pairs={{0,64},{2,66},{4,68},{6,70},{8,72},{10,74},{12,76},{14,78},{16,80}... | collective-permute-start | bytes 1179656 | tf_op jit(solution)/shard_map/ppermute | solution.py:149
  30.6 13.0 %collective-permute-start.5 = (f32[384,256]{1,0:T(8,128)S(1)}, f32[384,256]{1,0:T(8,128)S(1)}, u32[]{:S(2)}, u32[]{:S(2)}) collective-permute-start(f32[384,256]{1,0:T(8,128)S(1)} %get-tuple-element.26), channel_id=1, source_target_pairs={{1,2},{3,4},{5,6},{7,8},{9,10},{11,12},{13,14},{15,16},{17,18},{19... | collective-permute-start | bytes 1179656 | tf_op jit(solution)/shard_map/ppermute | solution.py:145
  44.9 2.6 %collective-permute-start.6 = (f32[384,256]{1,0:T(8,128)S(1)}, f32[384,256]{1,0:T(8,128)S(1)}, u32[]{:S(2)}, u32[]{:S(2)}) collective-permute-start(f32[384,256]{1,0:T(8,128)S(1)} %get-tuple-element.28), channel_id=1, source_target_pairs={{0,1},{2,3},{4,5},{6,7},{8,9},{10,11},{12,13},{14,15},{16,17},{18,... | collective-permute-start | bytes 1179656 | tf_op jit(solution)/shard_map/ppermute | solution.py:142
  46.2 13.0 %collective-permute-start.7 = (f32[384,256]{1,0:T(8,128)S(1)}, f32[384,256]{1,0:T(8,128)S(1)}, u32[]{:S(2)}, u32[]{:S(2)}) collective-permute-start(f32[384,256]{1,0:T(8,128)S(1)} %get-tuple-element.30), channel_id=1, source_target_pairs={{1,2},{3,4},{5,6},{7,8},{9,10},{11,12},{13,14},{15,16},{17,18},{19... | collective-permute-start | bytes 1179656 | tf_op jit(solution)/shard_map/ppermute | solution.py:145
  60.5 3.4 %collective-permute-start.8 = (f32[384,256]{1,0:T(8,128)S(1)}, f32[384,256]{1,0:T(8,128)S(1)}, u32[]{:S(2)}, u32[]{:S(2)}) collective-permute-start(f32[384,256]{1,0:T(8,128)S(1)} %get-tuple-element.32), channel_id=1, source_target_pairs={{0,1},{2,3},{4,5},{6,7},{8,9},{10,11},{12,13},{14,15},{16,17},{18,... | collective-permute-start | bytes 1179656 | tf_op jit(solution)/shard_map/ppermute | solution.py:142
  61.8 13.0 %collective-permute-start.9 = (f32[384,256]{1,0:T(8,128)S(1)}, f32[384,256]{1,0:T(8,128)S(1)}, u32[]{:S(2)}, u32[]{:S(2)}) collective-permute-start(f32[384,256]{1,0:T(8,128)S(1)} %get-tuple-element.33), channel_id=1, source_target_pairs={{1,2},{3,4},{5,6},{7,8},{9,10},{11,12},{13,14},{15,16},{17,18},{19... | collective-permute-start | bytes 1179656 | tf_op jit(solution)/shard_map/ppermute | solution.py:145

commit v2 on v0

v2 whole, which is shorter than its diff:
```python
import functools
import math

import jax
import jax.numpy as jnp
from jax import lax
from jax.experimental import pallas as pl
from jax.experimental.pallas import tpu as pltpu
from jax.sharding import PartitionSpec as P


F32 = jnp.float32
BF16 = jnp.bfloat16
NT = (((1,), (1,)), ((), ()))
NN = (((1,), (0,)), ((), ()))
CHUNK = 32

VMEM_SPEC = pl.BlockSpec(memory_space=pltpu.VMEM)
HBM_SPEC = pl.BlockSpec(memory_space=pltpu.HBM)
ANY_SPEC = pl.BlockSpec(memory_space=pl.ANY)


def in_vmem(x):
    return pltpu.with_memory_space_constraint(x, pltpu.VMEM)


def in_hbm(x):
    return pltpu.with_memory_space_constraint(x, pltpu.HBM)


def params(mib):
    return pltpu.CompilerParams(vmem_limit_bytes=mib << 20)


def on_core(core):
    return lax.axis_index("blk") % 2 == core


def halves(x):
    high = x.astype(BF16)
    return high, (x - high.astype(F32)).astype(BF16)


def product(a, b, dims):
    along_a, along_b = dims[0][0][0], dims[0][1][0]
    left = jnp.concatenate([a[0], a[0], a[1]], along_a)
    right = jnp.concatenate([b[0], b[1], b[0]], along_b)
    return lax.dot_general(left, right, dims, preferred_element_type=F32)


def tables(cnt, neg, mask, base_ref, slope_ref):
    rows, tiles = cnt.shape[0], mask.shape[0]
    tile = rows // tiles
    scale = 0.125 / math.sqrt(rows)
    columns = jnp.transpose(neg.astype(F32)).astype(jnp.int32)
    for row in range(0, rows, CHUNK):
        here, ti = slice(row, row + CHUNK), row // tile
        picks = [jnp.broadcast_to(columns[here, k : k + 1], (CHUNK, tile)) for k in range(neg.shape[0])]
        for tj in range(tiles):
            there = slice(tj * tile, (tj + 1) * tile)
            column = lax.broadcasted_iota(jnp.int32, (CHUNK, tile), 1) + tj * tile
            negcount = sum((pick == column).astype(F32) for pick in picks)
            count = cnt[here, there].astype(F32)
            gate = jnp.broadcast_to(mask[ti : ti + 1, tj : tj + 1].astype(F32) * scale, (CHUNK, tile))
            base_ref[here, there] = (count - negcount) * gate
            slope_ref[here, there] = (count + negcount) * gate


def packed_rows(rows, negs, tiles, steps):
    return -(-steps * (rows + negs + tiles) // 8) * 8


def tables_from(pack, index, steps, negs, tiles, base_ref, slope_ref):
    rows = pack.shape[1]
    at_neg = steps * rows + index * negs
    at_mask = steps * (rows + negs) + index * tiles
    tables(
        pack.at[index * rows : (index + 1) * rows],
        pack[at_neg : at_neg + negs],
        pack[at_mask : at_mask + tiles, :tiles],
        base_ref,
        slope_ref,
    )


def fill_pack(pack, first, steps, neg, mask):
    negs, tiles, rows = neg.shape[0], mask.shape[0], pack.shape[1]
    for i in range(steps):
        at_neg = steps * rows + i * negs
        at_mask = steps * (rows + negs) + i * tiles
        pack[at_neg : at_neg + negs] = neg[:, first + i]
        pack[at_mask : at_mask + tiles, :tiles] = mask[:, first + i]


def pass_body(vert, ctx, base, slope):
    vs, cs = halves(vert), halves(ctx)
    coef = base - slope * jnp.tanh(0.5 * product(vs, cs, NT))
    new_ctx = ctx + product(halves(jnp.transpose(coef)), vs, NN)
    new_vert = vert + product(halves(coef), cs, NN)
    return new_vert, new_ctx


def first_kernel(
    core, kept, vert_hbm, ctx_hbm, counts_hbm, neg_hbm, mask_hbm, *refs
):
    new_vert_ref, new_ctx_ref, near, far, vert, ctx, cnt, neg, mask, base, slope, sems = refs[kept:]

    @pl.when(on_core(core))
    def _():
        rows = cnt.shape[0]
        pairs = [
            (neg_hbm, neg),
            (mask_hbm, mask),
            (counts_hbm.at[0], cnt),
            (vert_hbm, vert),
            (ctx_hbm, ctx),
            (counts_hbm.at[1], near.at[:rows]),
            (counts_hbm.at[2], far.at[:rows]),
            (counts_hbm.at[3], far.at[rows : 2 * rows]),
        ]
        copies = [pltpu.make_async_copy(source, target, sems.at[i]) for i, (source, target) in enumerate(pairs)]
        for copy in copies:
            copy.start()
        for copy in copies[:5]:
            copy.wait()
        tables(cnt, neg[:, 0], mask[:, 0], base, slope)
        new_vert_ref[...], new_ctx_ref[...] = pass_body(vert[...], ctx[...], base[...], slope[...])
        fill_pack(near, 1, 1, neg, mask)
        fill_pack(far, 2, 2, neg, mask)
        for copy in copies[5:]:
            copy.wait()


def near_kernel(negs, tiles, after, near, base_ref, slope_ref):
    tables_from(near, 0, 1, negs, tiles, base_ref, slope_ref)


def far_kernel(negs, tiles, after, own, mate, base2, slope2, mate_base3, mate_slope3, own_base3, own_slope3):
    tables_from(mate, 0, 2, negs, tiles, base2, slope2)

    @pl.when(on_core(1))
    def _():
        tables_from(own, 1, 2, negs, tiles, own_base3, own_slope3)
        tables_from(mate, 1, 2, negs, tiles, mate_base3, mate_slope3)


def pass_kernel(core, after, vert_ref, ctx_ref, base_ref, slope_ref, new_vert_ref, new_ctx_ref):
    @pl.when(on_core(core))
    def _():
        new_vert_ref[...], new_ctx_ref[...] = pass_body(vert_ref[...], ctx_ref[...], base_ref[...], slope_ref[...])


def store_kernel(even_vert, even_ctx, odd_vert, odd_ctx, vert_hbm, ctx_hbm, sems):
    for core, (vert, ctx) in enumerate(((even_vert, even_ctx), (odd_vert, odd_ctx))):

        @pl.when(on_core(core))
        def _(vert=vert, ctx=ctx):
            copies = [pltpu.make_async_copy(vert, vert_hbm, sems.at[0]), pltpu.make_async_copy(ctx, ctx_hbm, sems.at[1])]
            for copy in copies:
                copy.start()
            for copy in copies:
                copy.wait()


def on_device(vertex_embed, context_embed, counts, negatives, masks):
    part, rows = vertex_embed.shape, counts.shape[1]
    negs, tiles = negatives.shape[1], masks.shape[1]
    vertex_embed, context_embed, counts = in_hbm(vertex_embed), in_hbm(context_embed), in_hbm(counts)
    negatives = in_hbm(jnp.transpose(negatives, (1, 0, 2)))
    masks = in_hbm(jnp.transpose(masks, (1, 0, 2)))
    state = pltpu.VMEM(part, F32)
    square = pltpu.VMEM((rows, rows), F32)
    small = [pltpu.VMEM(negatives.shape, jnp.int32), pltpu.VMEM(masks.shape, jnp.int32)]
    packs = [pltpu.VMEM((packed_rows(rows, negs, tiles, steps), rows), jnp.int32) for steps in (1, 2)]

    def call(kernel, outs, arrays, in_specs=None, **kwargs):
        return pl.pallas_call(
            kernel,
            out_shape=tuple(outs),
            in_specs=in_specs or [ANY_SPEC] + [VMEM_SPEC] * (len(arrays) - 1),
            out_specs=(VMEM_SPEC,) * len(outs),
            compiler_params=params(20),
            **kwargs,
        )(*arrays)

    def first(core, *kept):
        arrays = (vertex_embed, context_embed, counts, negatives, masks, *map(in_vmem, kept))
        return call(
            functools.partial(first_kernel, core, len(kept)),
            (state, state, *packs),
            arrays,
            [HBM_SPEC] * 5 + [VMEM_SPEC] * len(kept),
            scratch_shapes=[state, state, pltpu.VMEM((rows, rows), jnp.int32), *small, square, square, pltpu.SemaphoreType.DMA((8,))],
            input_output_aliases={5 + i: 2 + i for i in range(len(kept))},
        )

    def one_pass(core, after, vert, ctx, base, slope):
        arrays = (after, *map(in_vmem, (vert, ctx, base, slope)))
        return call(functools.partial(pass_kernel, core), (state, state), arrays)

    n_grp, n_blk = lax.axis_size("grp"), lax.axis_size("blk")

    def moved(value, core, blocks, swap=False):
        pairs = [
            (g * n_blk + b, (g ^ swap) * n_blk + (b + blocks) % n_blk) for g in range(n_grp) for b in range(core, n_blk, 2)
        ]
        return lax.ppermute(value, ("grp", "blk"), pairs)

    vert_o, out, *packed = first(1)
    outer0 = moved(out, 1, 1)
    vert_e, out, near, far = first(0, *packed)
    inner0 = moved(out, 0, 1)
    mate = lax.ppermute(far, "blk", [(b, b ^ 1) for b in range(n_blk)])
    table1 = call(functools.partial(near_kernel, negs, tiles), (square,) * 2, (vert_e, in_vmem(near)))
    vert_o, out = one_pass(1, table1[0], vert_o, inner0, *table1)
    swap1 = moved(vert_o, 1, -1, True)
    outer1 = moved(out, 1, 2)
    vert_e, out = one_pass(0, vert_o, vert_e, outer0, *table1)
    swap0 = moved(vert_e, 0, 1, True)
    far_tables = call(functools.partial(far_kernel, negs, tiles), (square,) * 6, (vert_e, in_vmem(far), in_vmem(mate)))
    table2, even3, odd3 = far_tables[:2], far_tables[2:4], far_tables[4:]
    vert_o, out = one_pass(0, table2[0], swap1, out, *table2)
    lend = moved(vert_o, 0, 1)
    outer2 = moved(out, 0, 3)
    vert_e, out = one_pass(1, vert_o, swap0, outer1, *table2)
    vert_o, out = one_pass(1, vert_e, lend, out, *odd3)
    outer3 = moved(out, 1, 1)
    vert_e, out = one_pass(1, vert_o, vert_e, outer2, *even3)
    back = moved(vert_e, 1, -1)
    return pl.pallas_call(
        store_kernel,
        out_shape=(pltpu.HBM(part, F32),) * 2,
        in_specs=[VMEM_SPEC] * 4,
        out_specs=(HBM_SPEC,) * 2,
        scratch_shapes=[pltpu.SemaphoreType.DMA((2,))],
        compiler_params=params(4),
        name="store",
    )(*map(in_vmem, (back, outer3, vert_o, out)))


def solution(mesh):
    placed = (
        P(("grp", "blk"), None),
        P(("grp", "blk"), None),
        P(None, ("grp", "blk"), None),
        P(None, None, ("grp", "blk")),
        P(None, ("grp", "blk"), None),
    )

    return jax.shard_map(
        on_device,
        mesh=mesh,
        in_specs=placed,
        out_specs=(P(("grp", "blk"), None), P(("grp", "blk"), None)),
        check_vma=False,
    )
```

time: 74.4 us -> 54.3 us (0.73)
  matrix products: 16 us -> 0 us
  waiting for transfers between devices: 42.8 us -> 31.4 us
  Pallas kernels: 0 us -> 7.65 us
  starting transfers between devices: 10.4 us -> 14.1 us
  local copies, waits for them, and re-layouts: 3.18 us -> 0 us
  other arithmetic: 0.85 us -> 0 us
    dot_general x12 -> x0, matrix products: 16 us -> none  [the longest x4 7.51 us: one_pass(): scores = jnp.einsum('iw,jw->ij', vert, ctx, precision=highest)]
    ppermute x5 -> x10, waiting for transfers between devices: 42.8 us -> 31.4 us  [the longest x9 31.4 us: moved(): return lax.ppermute(value, ('grp', 'blk'), pairs)]
    pallas_call x0 -> x11, Pallas kernels: none -> 7.65 us  [the longest x10 6.75 us: call(): pl.pallas_call(kernel, out_shape=tuple(outs), in_specs=in_specs or [ANY_S...]
    ppermute x5 -> x10, starting transfers between devices: 10.4 us -> 14.1 us  [the longest x9 12.2 us: moved(): return lax.ppermute(value, ('grp', 'blk'), pairs)]
    slice x2 -> x0, local copies, waits for them, and re-layouts: 1.73 us -> none  [one_pass(): neg_rows[sample][:, None] == columns]
    convert_element_type x1 -> x0, other arithmetic: 0.85 us -> none  [one_pass(): gate = tile_mask.astype(jnp.float32)[:, None, :, None]]
    unnamed x9 -> x0, local copies, waits for them, and re-layouts: 0.77 us -> none
  transfers between devices with their start and end apart: 5 -> 10, of which waited for: 4 -> 4; matrix products, arithmetic and copies ran while one was open for 6% -> 0% of each run, Pallas kernels for 0% -> 7%
where the time goes in v2:
time: 54.3 us; the launch traced here: 54 us
  waiting for transfers between devices  31.4 us (58%)
  starting transfers between devices  14.1 us (26%)
  Pallas kernels  7.65 us (14%)
  between operations  0.81 us (1%)
    ppermute x9, waiting for transfers between devices, moved(): return lax.ppermute(value, ('grp', 'blk'), pairs)  31.4 us
    ppermute x9, starting transfers between devices, moved(): return lax.ppermute(value, ('grp', 'blk'), pairs)  12.2 us
    pallas_call x10, Pallas kernels, call(): pl.pallas_call(kernel, out_shape=tuple(outs), in_specs=in_specs or [ANY_S...  6.75 us
    ppermute x1, starting transfers between devices, on_device(): mate = lax.ppermute(far, 'blk', [(b, b ^ 1) for b in range(n_blk)])  1.92 us
  transfers between devices with their start and end apart: 10, of which 4 were waited for; matrix products, arithmetic and copies ran while one was open for 0% of the time, Pallas kernels for 7%

profile of v2, /device:TPU:6, one launch (start us, length us, event | category | flops | bytes accessed | tf_op | source)
XLA Modules:
  0.0 54.0 jit_solution(18176455765753747433)
XLA Ops:
  0.6 0.1 shard_map.68
  0.7 2.9 %shard_map.69 = (f32[384,256]{1,0:T(8,128)S(1)}, f32[384,256]{1,0:T(8,128)S(1)}, s32[392,384]{1,0:T(8,128)S(1)}, s32[784,384]{1,0:T(8,128)S(1)}) custom-call(f32[384,256]{1,0:T(8,128)} %vert_hbm.3, f32[384,256]{1,0:T(8,128)} %ctx_hbm.3, s32[4,384,384]{2,1,0:T(8,128)} %counts_hbm.3, ...), custom_call_target="tpu_custom_call", output_to_operand_aliasing={{2}: (5, {}), {3}: (6, {})} | custom-call | tf_op jit(solution)/shard_map/pallas_call | solution.py:177
  3.7 1.9 %collective-permute-start.2 = (s32[784,384]{1,0:T(8,128)S(1)}, s32[784,384]{1,0:T(8,128)S(1)}, u32[]{:S(2)}, u32[]{:S(2)}) collective-permute-start(s32[784,384]{1,0:T(8,128)S(1)} %get-tuple-element.41.own), channel_id=1, source_target_pairs={{0,1},{1,0},{2,3},{3,2},{4,5},{5,4},{6,7},{7,6},{8,9},{9,8},{10,11... | collective-permute-start | bytes 3612680 | tf_op jit(solution)/shard_map/ppermute | solution.py:213
  5.6 2.4 %collective-permute-start = (f32[384,256]{1,0:T(8,128)S(1)}, f32[384,256]{1,0:T(8,128)S(1)}, u32[]{:S(2)}, u32[]{:S(2)}) collective-permute-start(f32[384,256]{1,0:T(8,128)S(1)} %get-tuple-element.36), channel_id=1, source_target_pairs={{0,1},{2,3},{4,5},{6,7},{8,9},{10,11},{12,13},{14,15},{16,17},{18,... | collective-permute-start | bytes 1179656 | tf_op jit(solution)/shard_map/ppermute | solution.py:207
  8.0 1.3 %collective-permute-start.1 = (f32[384,256]{1,0:T(8,128)S(1)}, f32[384,256]{1,0:T(8,128)S(1)}, u32[]{:S(2)}, u32[]{:S(2)}) collective-permute-start(f32[384,256]{1,0:T(8,128)S(1)} %get-tuple-element.39), channel_id=1, source_target_pairs={{1,2},{3,4},{5,6},{7,8},{9,10},{11,12},{13,14},{15,16},{17,18},{19... | collective-permute-start | bytes 1179656 | tf_op jit(solution)/shard_map/ppermute | solution.py:207
  9.3 0.7 %shard_map.70 = (f32[384,384]{1,0:T(8,128)S(1)}, f32[384,384]{1,0:T(8,128)S(1)}) custom-call(f32[384,256]{1,0:T(8,128)S(1)} %get-tuple-element.32.after.vert_ref, s32[392,384]{1,0:T(8,128)S(1)} %get-tuple-element.33.near), custom_call_target="tpu_custom_call" | custom-call | tf_op jit(solution)/shard_map/pallas_call | solution.py:177
  10.0 0.0 collective-permute-done.ctx_ref
  10.1 1.3 %collective-permute-start.3 = (f32[384,256]{1,0:T(8,128)S(1)}, f32[384,256]{1,0:T(8,128)S(1)}, u32[]{:S(2)}, u32[]{:S(2)}) collective-permute-start(f32[384,256]{1,0:T(8,128)S(1)} %get-tuple-element.38.after), channel_id=1, source_target_pairs={{1,64},{3,66},{5,68},{7,70},{9,72},{11,74},{13,76},{15,78},{17,80}... | collective-permute-start | bytes 1179656 | tf_op jit(solution)/shard_map/ppermute | solution.py:207
  11.3 14.5 %collective-permute-done.1.ctx_ref = f32[384,256]{1,0:T(8,128)S(1)} collective-permute-done((f32[384,256]{1,0:T(8,128)S(1)}, f32[384,256]{1,0:T(8,128)S(1)}, u32[]{:S(2)}, u32[]{:S(2)}) %collective-permute-start.1) | collective-permute-done | bytes 393248 | tf_op jit(solution)/shard_map/ppermute | solution.py:207
  25.8 1.2 %shard_map.72 = (f32[384,256]{1,0:T(8,128)S(1)}, f32[384,256]{1,0:T(8,128)S(1)}) custom-call(f32[384,256]{1,0:T(8,128)S(1)} %get-tuple-element.38.after, f32[384,256]{1,0:T(8,128)S(1)} %get-tuple-element.32.after.vert_ref, f32[384,256]{1,0:T(8,128)S(1)} %collective-permute-done.1.ctx_ref, f32[384,384]{1,0:T(8,128)S(1)} %get-tuple-element.34.after.base_ref, ...), custom_call_target="tpu_custom_call" | custom-call | tf_op jit(solution)/shard_map/pallas_call | solution.py:177
  27.0 1.3 %collective-permute-start.4 = (f32[384,256]{1,0:T(8,128)S(1)}, f32[384,256]{1,0:T(8,128)S(1)}, u32[]{:S(2)}, u32[]{:S(2)}) collective-permute-start(f32[384,256]{1,0:T(8,128)S(1)} %get-tuple-element.40.after), channel_id=1, source_target_pairs={{0,65},{2,67},{4,69},{6,71},{8,73},{10,75},{12,77},{14,79},{16,81}... | collective-permute-start | bytes 1179656 | tf_op jit(solution)/shard_map/ppermute | solution.py:207
  28.3 0.7 %collective-permute-start.5 = (f32[384,256]{1,0:T(8,128)S(1)}, f32[384,256]{1,0:T(8,128)S(1)}, u32[]{:S(2)}, u32[]{:S(2)}) collective-permute-start(f32[384,256]{1,0:T(8,128)S(1)} %get-tuple-element.46), channel_id=1, source_target_pairs={{1,3},{3,5},{5,7},{7,9},{9,11},{11,13},{13,15},{15,17},{17,19},{19... | collective-permute-start | bytes 1179656 | tf_op jit(solution)/shard_map/ppermute | solution.py:207
  29.0 0.0 collective-permute-done.2.mate
  29.0 0.7 %shard_map.73 = (f32[384,384]{1,0:T(8,128)S(1)}, f32[384,384]{1,0:T(8,128)S(1)}, f32[384,384]{1,0:T(8,128)S(1)}, f32[384,384]{1,0:T(8,128)S(1)}, f32[384,384]{1,0:T(8,128)S(1)}, /*index=5*/f32[384,384]{1,0:T(8,128)S(1)}) custom-call(f32[384,256]{1,0:T(8,128)S(1)} %get-tuple-element.40.after, s32[784,384]{1,0:T(8,128)S(1)} %get-tuple-element.41.own, ...), custom_call_target="tpu_custom_call" | custom-call | tf_op jit(solution)/shard_map/pallas_call | solution.py:177
  29.7 0.0 collective-permute-done.3.vert_ref
  29.7 1.2 %shard_map.74 = (f32[384,256]{1,0:T(8,128)S(1)}, f32[384,256]{1,0:T(8,128)S(1)}) custom-call(f32[384,384]{1,0:T(8,128)S(1)} %get-tuple-element.42.after.base_ref, f32[384,256]{1,0:T(8,128)S(1)} %collective-permute-done.3.vert_ref, f32[384,256]{1,0:T(8,128)S(1)} %get-tuple-element.43.ctx_ref, f32[384,384]{1,0:T(8,128)S(1)} %get-tuple-element.42.after.base_ref, ...), custom_call_target="tpu_custom_call" | custom-call | tf_op jit(solution)/shard_map/pallas_call | solution.py:177
  30.9 1.3 %collective-permute-start.6 = (f32[384,256]{1,0:T(8,128)S(1)}, f32[384,256]{1,0:T(8,128)S(1)}, u32[]{:S(2)}, u32[]{:S(2)}) collective-permute-start(f32[384,256]{1,0:T(8,128)S(1)} %get-tuple-element.45.after), channel_id=1, source_target_pairs={{0,1},{2,3},{4,5},{6,7},{8,9},{10,11},{12,13},{14,15},{16,17},{18,... | collective-permute-start | bytes 1179656 | tf_op jit(solution)/shard_map/ppermute | solution.py:207
  32.2 1.3 %collective-permute-start.7 = (f32[384,256]{1,0:T(8,128)S(1)}, f32[384,256]{1,0:T(8,128)S(1)}, u32[]{:S(2)}, u32[]{:S(2)}) collective-permute-start(f32[384,256]{1,0:T(8,128)S(1)} %get-tuple-element.52), channel_id=1, source_target_pairs={{0,3},{2,5},{4,7},{6,9},{8,11},{10,13},{12,15},{14,17},{16,19},{18... | collective-permute-start | bytes 1179656 | tf_op jit(solution)/shard_map/ppermute | solution.py:207
  33.5 0.0 collective-permute-done.4.vert_ref
  33.6 0.0 collective-permute-done.5.ctx_ref
  33.6 0.0 collective-permute-done.6.vert_ref
  33.6 5.2 %collective-permute-done.7.ctx_ref = f32[384,256]{1,0:T(8,128)S(1)} collective-permute-done((f32[384,256]{1,0:T(8,128)S(1)}, f32[384,256]{1,0:T(8,128)S(1)}, u32[]{:S(2)}, u32[]{:S(2)}) %collective-permute-start.7) | collective-permute-done | bytes 393248 | tf_op jit(solution)/shard_map/ppermute | solution.py:207
  38.8 1.3 %collective-permute-start.8 = (f32[384,256]{1,0:T(8,128)S(1)}, f32[384,256]{1,0:T(8,128)S(1)}, u32[]{:S(2)}, u32[]{:S(2)}) collective-permute-start(f32[384,256]{1,0:T(8,128)S(1)} %get-tuple-element.55), channel_id=1, source_target_pairs={{1,0},{3,2},{5,4},{7,6},{9,8},{11,10},{13,12},{15,14},{17,16},{19,... | collective-permute-start | bytes 1179656 | tf_op jit(solution)/shard_map/ppermute | solution.py:207
  40.1 1.3 %collective-permute-start.9 = (f32[384,256]{1,0:T(8,128)S(1)}, f32[384,256]{1,0:T(8,128)S(1)}, u32[]{:S(2)}, u32[]{:S(2)}) collective-permute-start(f32[384,256]{1,0:T(8,128)S(1)} %get-tuple-element.56), channel_id=1, source_target_pairs={{1,2},{3,4},{5,6},{7,8},{9,10},{11,12},{13,14},{15,16},{17,18},{19... | collective-permute-start | bytes 1179656 | tf_op jit(solution)/shard_map/ppermute | solution.py:207
  41.4 4.7 %collective-permute-done.8.even_vert = f32[384,256]{1,0:T(8,128)S(1)} collective-permute-done((f32[384,256]{1,0:T(8,128)S(1)}, f32[384,256]{1,0:T(8,128)S(1)}, u32[]{:S(2)}, u32[]{:S(2)}) %collective-permute-start.8) | collective-permute-done | bytes 393248 | tf_op jit(solution)/shard_map/ppermute | solution.py:207
  46.1 7.0 %collective-permute-done.9.even_ctx = f32[384,256]{1,0:T(8,128)S(1)} collective-permute-done((f32[384,256]{1,0:T(8,128)S(1)}, f32[384,256]{1,0:T(8,128)S(1)}, u32[]{:S(2)}, u32[]{:S(2)}) %collective-permute-start.9) | collective-permute-done | bytes 393248 | tf_op jit(solution)/shard_map/ppermute | solution.py:207
  53.1 0.9 %store.1 = (f32[384,256]{1,0:T(8,128)}, f32[384,256]{1,0:T(8,128)}) custom-call(f32[384,256]{1,0:T(8,128)S(1)} %collective-permute-done.8.even_vert, f32[384,256]{1,0:T(8,128)S(1)} %collective-permute-done.9.even_ctx, f32[384,256]{1,0:T(8,128)S(1)} %get-tuple-element.51.after.odd_vert, f32[384,256]{1,0:T(8,128)S(1)} %get-tuple-element.57.odd_ctx), custom_call_target="tpu_custom_call" | custom-call | tf_op jit(solution)/shard_map/store/pallas_call | solution.py:230
  (4 shorter events, 0.0 us)
Async XLA Ops:
  3.7 25.3 %collective-permute-start.2 = (s32[784,384]{1,0:T(8,128)S(1)}, s32[784,384]{1,0:T(8,128)S(1)}, u32[]{:S(2)}, u32[]{:S(2)}) collective-permute-start(s32[784,384]{1,0:T(8,128)S(1)} %get-tuple-element.41.own), channel_id=1, source_target_pairs={{0,1},{1,0},{2,3},{3,2},{4,5},{5,4},{6,7},{7,6},{8,9},{9,8},{10,11... | collective-permute-start | bytes 3612680 | tf_op jit(solution)/shard_map/ppermute | solution.py:213
  5.6 4.4 %collective-permute-start = (f32[384,256]{1,0:T(8,128)S(1)}, f32[384,256]{1,0:T(8,128)S(1)}, u32[]{:S(2)}, u32[]{:S(2)}) collective-permute-start(f32[384,256]{1,0:T(8,128)S(1)} %get-tuple-element.36), channel_id=1, source_target_pairs={{0,1},{2,3},{4,5},{6,7},{8,9},{10,11},{12,13},{14,15},{16,17},{18,... | collective-permute-start | bytes 1179656 | tf_op jit(solution)/shard_map/ppermute | solution.py:207
  8.0 17.8 %collective-permute-start.1 = (f32[384,256]{1,0:T(8,128)S(1)}, f32[384,256]{1,0:T(8,128)S(1)}, u32[]{:S(2)}, u32[]{:S(2)}) collective-permute-start(f32[384,256]{1,0:T(8,128)S(1)} %get-tuple-element.39), channel_id=1, source_target_pairs={{1,2},{3,4},{5,6},{7,8},{9,10},{11,12},{13,14},{15,16},{17,18},{19... | collective-permute-start | bytes 1179656 | tf_op jit(solution)/shard_map/ppermute | solution.py:207
  10.1 19.7 %collective-permute-start.3 = (f32[384,256]{1,0:T(8,128)S(1)}, f32[384,256]{1,0:T(8,128)S(1)}, u32[]{:S(2)}, u32[]{:S(2)}) collective-permute-start(f32[384,256]{1,0:T(8,128)S(1)} %get-tuple-element.38.after), channel_id=1, source_target_pairs={{1,64},{3,66},{5,68},{7,70},{9,72},{11,74},{13,76},{15,78},{17,80}... | collective-permute-start | bytes 1179656 | tf_op jit(solution)/shard_map/ppermute | solution.py:207
  27.0 6.6 %collective-permute-start.4 = (f32[384,256]{1,0:T(8,128)S(1)}, f32[384,256]{1,0:T(8,128)S(1)}, u32[]{:S(2)}, u32[]{:S(2)}) collective-permute-start(f32[384,256]{1,0:T(8,128)S(1)} %get-tuple-element.40.after), channel_id=1, source_target_pairs={{0,65},{2,67},{4,69},{6,71},{8,73},{10,75},{12,77},{14,79},{16,81}... | collective-permute-start | bytes 1179656 | tf_op jit(solution)/shard_map/ppermute | solution.py:207
  28.3 5.3 %collective-permute-start.5 = (f32[384,256]{1,0:T(8,128)S(1)}, f32[384,256]{1,0:T(8,128)S(1)}, u32[]{:S(2)}, u32[]{:S(2)}) collective-permute-start(f32[384,256]{1,0:T(8,128)S(1)} %get-tuple-element.46), channel_id=1, source_target_pairs={{1,3},{3,5},{5,7},{7,9},{9,11},{11,13},{13,15},{15,17},{17,19},{19... | collective-permute-start | bytes 1179656 | tf_op jit(solution)/shard_map/ppermute | solution.py:207
  30.9 2.7 %collective-permute-start.6 = (f32[384,256]{1,0:T(8,128)S(1)}, f32[384,256]{1,0:T(8,128)S(1)}, u32[]{:S(2)}, u32[]{:S(2)}) collective-permute-start(f32[384,256]{1,0:T(8,128)S(1)} %get-tuple-element.45.after), channel_id=1, source_target_pairs={{0,1},{2,3},{4,5},{6,7},{8,9},{10,11},{12,13},{14,15},{16,17},{18,... | collective-permute-start | bytes 1179656 | tf_op jit(solution)/shard_map/ppermute | solution.py:207
  32.2 6.6 %collective-permute-start.7 = (f32[384,256]{1,0:T(8,128)S(1)}, f32[384,256]{1,0:T(8,128)S(1)}, u32[]{:S(2)}, u32[]{:S(2)}) collective-permute-start(f32[384,256]{1,0:T(8,128)S(1)} %get-tuple-element.52), channel_id=1, source_target_pairs={{0,3},{2,5},{4,7},{6,9},{8,11},{10,13},{12,15},{14,17},{16,19},{18... | collective-permute-start | bytes 1179656 | tf_op jit(solution)/shard_map/ppermute | solution.py:207
  38.8 7.3 %collective-permute-start.8 = (f32[384,256]{1,0:T(8,128)S(1)}, f32[384,256]{1,0:T(8,128)S(1)}, u32[]{:S(2)}, u32[]{:S(2)}) collective-permute-start(f32[384,256]{1,0:T(8,128)S(1)} %get-tuple-element.55), channel_id=1, source_target_pairs={{1,0},{3,2},{5,4},{7,6},{9,8},{11,10},{13,12},{15,14},{17,16},{19,... | collective-permute-start | bytes 1179656 | tf_op jit(solution)/shard_map/ppermute | solution.py:207
  40.1 13.0 %collective-permute-start.9 = (f32[384,256]{1,0:T(8,128)S(1)}, f32[384,256]{1,0:T(8,128)S(1)}, u32[]{:S(2)}, u32[]{:S(2)}) collective-permute-start(f32[384,256]{1,0:T(8,128)S(1)} %get-tuple-element.56), channel_id=1, source_target_pairs={{1,2},{3,4},{5,6},{7,8},{9,10},{11,12},{13,14},{15,16},{17,18},{19... | collective-permute-start | bytes 1179656 | tf_op jit(solution)/shard_map/ppermute | solution.py:207

commit v3 on v2

--- a/solution.py
+++ b/solution.py
@@ -135,13 +135,21 @@
     tables_from(near, 0, 1, negs, tiles, base_ref, slope_ref)
 
 
-def far_kernel(negs, tiles, after, own, mate, base2, slope2, mate_base3, mate_slope3, own_base3, own_slope3):
-    tables_from(mate, 0, 2, negs, tiles, base2, slope2)
+def far_kernel(negs, tiles, after, own, from_even, from_odd, base2, slope2, own_base3, own_slope3):
+    @pl.when(on_core(0))
+    def _():
+        tables_from(from_odd, 0, 2, negs, tiles, base2, slope2)
 
     @pl.when(on_core(1))
     def _():
+        tables_from(from_even, 0, 2, negs, tiles, base2, slope2)
         tables_from(own, 1, 2, negs, tiles, own_base3, own_slope3)
-        tables_from(mate, 1, 2, negs, tiles, mate_base3, mate_slope3)
+
+
+def last_kernel(negs, tiles, after, from_even, base_ref, slope_ref):
+    @pl.when(on_core(1))
+    def _():
+        tables_from(from_even, 1, 2, negs, tiles, base_ref, slope_ref)
 
 
 def pass_kernel(core, after, vert_ref, ctx_ref, base_ref, slope_ref, new_vert_ref, new_ctx_ref):
@@ -150,16 +158,16 @@
         new_vert_ref[...], new_ctx_ref[...] = pass_body(vert_ref[...], ctx_ref[...], base_ref[...], slope_ref[...])
 
 
-def store_kernel(even_vert, even_ctx, odd_vert, odd_ctx, vert_hbm, ctx_hbm, sems):
-    for core, (vert, ctx) in enumerate(((even_vert, even_ctx), (odd_vert, odd_ctx))):
-
-        @pl.when(on_core(core))
-        def _(vert=vert, ctx=ctx):
-            copies = [pltpu.make_async_copy(vert, vert_hbm, sems.at[0]), pltpu.make_async_copy(ctx, ctx_hbm, sems.at[1])]
-            for copy in copies:
-                copy.start()
-            for copy in copies:
-                copy.wait()
+def store_kernel(core, vert, ctx, *refs):
+    vert_hbm, ctx_hbm, sems = refs[-3:]
+
+    @pl.when(on_core(core))
+    def _():
+        copies = [pltpu.make_async_copy(vert, vert_hbm, sems.at[0]), pltpu.make_async_copy(ctx, ctx_hbm, sems.at[1])]
+        for copy in copies:
+            copy.start()
+        for copy in copies:
+            copy.wait()
 
 
 def on_device(vertex_embed, context_embed, counts, negatives, masks):
@@ -206,36 +214,43 @@
         ]
         return lax.ppermute(value, ("grp", "blk"), pairs)
 
+    def store(core, vert, ctx, *stored):
+        return pl.pallas_call(
+            functools.partial(store_kernel, core),
+            out_shape=(pltpu.HBM(part, F32),) * 2,
+            in_specs=[VMEM_SPEC] * 2 + [HBM_SPEC] * len(stored),
+            out_specs=(HBM_SPEC,) * 2,
+            scratch_shapes=[pltpu.SemaphoreType.DMA((2,))],
+            input_output_aliases={2 + i: i for i in range(len(stored))},
+            compiler_params=params(4),
+        )(*map(in_vmem, (vert, ctx)), *stored)
+
     vert_o, out, *packed = first(1)
     outer0 = moved(out, 1, 1)
     vert_e, out, near, far = first(0, *packed)
     inner0 = moved(out, 0, 1)
-    mate = lax.ppermute(far, "blk", [(b, b ^ 1) for b in range(n_blk)])
+    from_even = moved(far, 0, 1)
     table1 = call(functools.partial(near_kernel, negs, tiles), (square,) * 2, (vert_e, in_vmem(near)))
     vert_o, out = one_pass(1, table1[0], vert_o, inner0, *table1)
     swap1 = moved(vert_o, 1, -1, True)
+    from_odd = moved(far, 1, -1)
     outer1 = moved(out, 1, 2)
     vert_e, out = one_pass(0, vert_o, vert_e, outer0, *table1)
     swap0 = moved(vert_e, 0, 1, True)
-    far_tables = call(functools.partial(far_kernel, negs, tiles), (square,) * 6, (vert_e, in_vmem(far), in_vmem(mate)))
-    table2, even3, odd3 = far_tables[:2], far_tables[2:4], far_tables[4:]
+    arrays = (vert_e, *map(in_vmem, (far, from_even, from_odd)))
+    far_tables = call(functools.partial(far_kernel, negs, tiles), (square,) * 4, arrays)
+    table2, odd3 = far_tables[:2], far_tables[2:]
     vert_o, out = one_pass(0, table2[0], swap1, out, *table2)
     lend = moved(vert_o, 0, 1)
     outer2 = moved(out, 0, 3)
     vert_e, out = one_pass(1, vert_o, swap0, outer1, *table2)
     vert_o, out = one_pass(1, vert_e, lend, out, *odd3)
     outer3 = moved(out, 1, 1)
-    vert_e, out = one_pass(1, vert_o, vert_e, outer2, *even3)
+    even3 = call(functools.partial(last_kernel, negs, tiles), (square,) * 2, (vert_o, in_vmem(from_even)))
+    vert_e, out = one_pass(1, even3[0], vert_e, outer2, *even3)
     back = moved(vert_e, 1, -1)
-    return pl.pallas_call(
-        store_kernel,
-        out_shape=(pltpu.HBM(part, F32),) * 2,
-        in_specs=[VMEM_SPEC] * 4,
-        out_specs=(HBM_SPEC,) * 2,
-        scratch_shapes=[pltpu.SemaphoreType.DMA((2,))],
-        compiler_params=params(4),
-        name="store",
-    )(*map(in_vmem, (back, outer3, vert_o, out)))
+    stored = store(1, vert_o, out)
+    return tuple(store(0, back, outer3, *stored))
 
 
 def solution(mesh):

time: 54.3 us -> 56.2 us (1.035)
  starting transfers between devices: 14.1 us -> 16 us
    ppermute x9 -> x11, starting transfers between devices: 12.2 us -> 16 us  [moved(): return lax.ppermute(value, ('grp', 'blk'), pairs)]
    ppermute x1 -> x0, starting transfers between devices: 1.92 us -> none  [on_device(): mate = lax.ppermute(far, 'blk', [(b, b ^ 1) for b in range(n_blk)])]
    ppermute x9 -> x11, waiting for transfers between devices: 31.4 us -> 31.3 us  [moved(): return lax.ppermute(value, ('grp', 'blk'), pairs)]
    pallas_call x10 -> x11, Pallas kernels: 6.75 us -> 6.82 us  [call(): pl.pallas_call(kernel, out_shape=tuple(outs), in_specs=in_specs or [ANY_S...]
  transfers between devices with their start and end apart: 10 -> 11, of which waited for: 4 -> 4; matrix products, arithmetic and copies ran while one was open for 0% -> 0% of each run, Pallas kernels for 7% -> 7%
where the time goes in v3:
time: 56.2 us; the launch traced here: 55.9 us
  waiting for transfers between devices  31.3 us (56%)
  starting transfers between devices  16 us (28%)
  Pallas kernels  7.75 us (14%)
  between operations  0.86 us (2%)
    ppermute x11, waiting for transfers between devices, moved(): return lax.ppermute(value, ('grp', 'blk'), pairs)  31.3 us
    ppermute x11, starting transfers between devices, moved(): return lax.ppermute(value, ('grp', 'blk'), pairs)  16 us
    pallas_call x11, Pallas kernels, call(): pl.pallas_call(kernel, out_shape=tuple(outs), in_specs=in_specs or [ANY_S...  6.82 us
  transfers between devices with their start and end apart: 11, of which 4 were waited for; matrix products, arithmetic and copies ran while one was open for 0% of the time, Pallas kernels for 7%

profile of v3, /device:TPU:6, one launch (start us, length us, event | category | flops | bytes accessed | tf_op | source)
XLA Modules:
  0.0 55.9 jit_solution(9377355794954978500)
XLA Ops:
  0.6 0.1 shard_map.68
  0.7 2.9 %shard_map.69 = (f32[384,256]{1,0:T(8,128)S(1)}, f32[384,256]{1,0:T(8,128)S(1)}, s32[392,384]{1,0:T(8,128)S(1)}, s32[784,384]{1,0:T(8,128)S(1)}) custom-call(f32[384,256]{1,0:T(8,128)} %vert_hbm.3, f32[384,256]{1,0:T(8,128)} %ctx_hbm.3, s32[4,384,384]{2,1,0:T(8,128)} %counts_hbm.3, ...), custom_call_target="tpu_custom_call", output_to_operand_aliasing={{2}: (5, {}), {3}: (6, {})} | custom-call | tf_op jit(solution)/shard_map/pallas_call | solution.py:185
  3.7 1.8 %collective-permute-start.2 = (s32[784,384]{1,0:T(8,128)S(1)}, s32[784,384]{1,0:T(8,128)S(1)}, u32[]{:S(2)}, u32[]{:S(2)}) collective-permute-start(s32[784,384]{1,0:T(8,128)S(1)} %get-tuple-element.43.own), channel_id=1, source_target_pairs={{0,1},{2,3},{4,5},{6,7},{8,9},{10,11},{12,13},{14,15},{16,17},{18,... | collective-permute-start | bytes 3612680 | tf_op jit(solution)/shard_map/ppermute | solution.py:215
  5.5 1.3 %collective-permute-start.3 = (s32[784,384]{1,0:T(8,128)S(1)}, s32[784,384]{1,0:T(8,128)S(1)}, u32[]{:S(2)}, u32[]{:S(2)}) collective-permute-start(s32[784,384]{1,0:T(8,128)S(1)} %get-tuple-element.43.own), channel_id=1, source_target_pairs={{1,0},{3,2},{5,4},{7,6},{9,8},{11,10},{13,12},{15,14},{17,16},{19,... | collective-permute-start | bytes 3612680 | tf_op jit(solution)/shard_map/ppermute | solution.py:215
  6.8 3.1 %collective-permute-start = (f32[384,256]{1,0:T(8,128)S(1)}, f32[384,256]{1,0:T(8,128)S(1)}, u32[]{:S(2)}, u32[]{:S(2)}) collective-permute-start(f32[384,256]{1,0:T(8,128)S(1)} %get-tuple-element.38), channel_id=1, source_target_pairs={{0,1},{2,3},{4,5},{6,7},{8,9},{10,11},{12,13},{14,15},{16,17},{18,... | collective-permute-start | bytes 1179656 | tf_op jit(solution)/shard_map/ppermute | solution.py:215
  9.9 1.3 %collective-permute-start.1 = (f32[384,256]{1,0:T(8,128)S(1)}, f32[384,256]{1,0:T(8,128)S(1)}, u32[]{:S(2)}, u32[]{:S(2)}) collective-permute-start(f32[384,256]{1,0:T(8,128)S(1)} %get-tuple-element.41), channel_id=1, source_target_pairs={{1,2},{3,4},{5,6},{7,8},{9,10},{11,12},{13,14},{15,16},{17,18},{19... | collective-permute-start | bytes 1179656 | tf_op jit(solution)/shard_map/ppermute | solution.py:215
  11.2 0.7 %shard_map.70 = (f32[384,384]{1,0:T(8,128)S(1)}, f32[384,384]{1,0:T(8,128)S(1)}) custom-call(f32[384,256]{1,0:T(8,128)S(1)} %get-tuple-element.34.after.vert_ref, s32[392,384]{1,0:T(8,128)S(1)} %get-tuple-element.35.near), custom_call_target="tpu_custom_call" | custom-call | tf_op jit(solution)/shard_map/pallas_call | solution.py:185
  11.9 0.0 collective-permute-done.ctx_ref
  11.9 1.3 %collective-permute-start.4 = (f32[384,256]{1,0:T(8,128)S(1)}, f32[384,256]{1,0:T(8,128)S(1)}, u32[]{:S(2)}, u32[]{:S(2)}) collective-permute-start(f32[384,256]{1,0:T(8,128)S(1)} %get-tuple-element.40.after), channel_id=1, source_target_pairs={{1,64},{3,66},{5,68},{7,70},{9,72},{11,74},{13,76},{15,78},{17,80}... | collective-permute-start | bytes 1179656 | tf_op jit(solution)/shard_map/ppermute | solution.py:215
  13.2 14.5 %collective-permute-done.1.ctx_ref = f32[384,256]{1,0:T(8,128)S(1)} collective-permute-done((f32[384,256]{1,0:T(8,128)S(1)}, f32[384,256]{1,0:T(8,128)S(1)}, u32[]{:S(2)}, u32[]{:S(2)}) %collective-permute-start.1) | collective-permute-done | bytes 393248 | tf_op jit(solution)/shard_map/ppermute | solution.py:215
  27.7 1.2 %shard_map.72 = (f32[384,256]{1,0:T(8,128)S(1)}, f32[384,256]{1,0:T(8,128)S(1)}) custom-call(f32[384,256]{1,0:T(8,128)S(1)} %get-tuple-element.40.after, f32[384,256]{1,0:T(8,128)S(1)} %get-tuple-element.34.after.vert_ref, f32[384,256]{1,0:T(8,128)S(1)} %collective-permute-done.1.ctx_ref, f32[384,384]{1,0:T(8,128)S(1)} %get-tuple-element.36.after.base_ref, ...), custom_call_target="tpu_custom_call" | custom-call | tf_op jit(solution)/shard_map/pallas_call | solution.py:185
  28.9 1.3 %collective-permute-start.5 = (f32[384,256]{1,0:T(8,128)S(1)}, f32[384,256]{1,0:T(8,128)S(1)}, u32[]{:S(2)}, u32[]{:S(2)}) collective-permute-start(f32[384,256]{1,0:T(8,128)S(1)} %get-tuple-element.42.after), channel_id=1, source_target_pairs={{0,65},{2,67},{4,69},{6,71},{8,73},{10,75},{12,77},{14,79},{16,81}... | collective-permute-start | bytes 1179656 | tf_op jit(solution)/shard_map/ppermute | solution.py:215
  30.2 0.7 %collective-permute-start.6 = (f32[384,256]{1,0:T(8,128)S(1)}, f32[384,256]{1,0:T(8,128)S(1)}, u32[]{:S(2)}, u32[]{:S(2)}) collective-permute-start(f32[384,256]{1,0:T(8,128)S(1)} %get-tuple-element.48), channel_id=1, source_target_pairs={{1,3},{3,5},{5,7},{7,9},{9,11},{11,13},{13,15},{15,17},{17,19},{19... | collective-permute-start | bytes 1179656 | tf_op jit(solution)/shard_map/ppermute | solution.py:215
  30.9 0.0 collective-permute-done.2.from_even
  30.9 0.0 collective-permute-done.3.from_odd
  30.9 0.7 %shard_map.73 = (f32[384,384]{1,0:T(8,128)S(1)}, f32[384,384]{1,0:T(8,128)S(1)}, f32[384,384]{1,0:T(8,128)S(1)}, f32[384,384]{1,0:T(8,128)S(1)}) custom-call(f32[384,256]{1,0:T(8,128)S(1)} %get-tuple-element.42.after, s32[784,384]{1,0:T(8,128)S(1)} %get-tuple-element.43.own, s32[784,384]{1,0:T(8,128)S(1)} %collective-permute-done.2.from_even, ...), custom_call_target="tpu_custom_call" | custom-call | tf_op jit(solution)/shard_map/pallas_call | solution.py:185
  31.6 0.0 collective-permute-done.4.vert_ref
  31.6 1.2 %shard_map.74 = (f32[384,256]{1,0:T(8,128)S(1)}, f32[384,256]{1,0:T(8,128)S(1)}) custom-call(f32[384,384]{1,0:T(8,128)S(1)} %get-tuple-element.44.after.base_ref, f32[384,256]{1,0:T(8,128)S(1)} %collective-permute-done.4.vert_ref, f32[384,256]{1,0:T(8,128)S(1)} %get-tuple-element.45.ctx_ref, f32[384,384]{1,0:T(8,128)S(1)} %get-tuple-element.44.after.base_ref, ...), custom_call_target="tpu_custom_call" | custom-call | tf_op jit(solution)/shard_map/pallas_call | solution.py:185
  32.8 1.3 %collective-permute-start.7 = (f32[384,256]{1,0:T(8,128)S(1)}, f32[384,256]{1,0:T(8,128)S(1)}, u32[]{:S(2)}, u32[]{:S(2)}) collective-permute-start(f32[384,256]{1,0:T(8,128)S(1)} %get-tuple-element.47.after), channel_id=1, source_target_pairs={{0,1},{2,3},{4,5},{6,7},{8,9},{10,11},{12,13},{14,15},{16,17},{18,... | collective-permute-start | bytes 1179656 | tf_op jit(solution)/shard_map/ppermute | solution.py:215
  34.2 1.3 %collective-permute-start.8 = (f32[384,256]{1,0:T(8,128)S(1)}, f32[384,256]{1,0:T(8,128)S(1)}, u32[]{:S(2)}, u32[]{:S(2)}) collective-permute-start(f32[384,256]{1,0:T(8,128)S(1)} %get-tuple-element.55), channel_id=1, source_target_pairs={{0,3},{2,5},{4,7},{6,9},{8,11},{10,13},{12,15},{14,17},{16,19},{18... | collective-permute-start | bytes 1179656 | tf_op jit(solution)/shard_map/ppermute | solution.py:215
  35.5 0.0 collective-permute-done.5.vert_ref
  35.5 0.0 collective-permute-done.6.ctx_ref
  35.5 0.0 collective-permute-done.7.vert_ref
  35.6 5.1 %collective-permute-done.8.ctx_ref = f32[384,256]{1,0:T(8,128)S(1)} collective-permute-done((f32[384,256]{1,0:T(8,128)S(1)}, f32[384,256]{1,0:T(8,128)S(1)}, u32[]{:S(2)}, u32[]{:S(2)}) %collective-permute-start.8) | collective-permute-done | bytes 393248 | tf_op jit(solution)/shard_map/ppermute | solution.py:215
  40.7 1.3 %collective-permute-start.9 = (f32[384,256]{1,0:T(8,128)S(1)}, f32[384,256]{1,0:T(8,128)S(1)}, u32[]{:S(2)}, u32[]{:S(2)}) collective-permute-start(f32[384,256]{1,0:T(8,128)S(1)} %get-tuple-element.57), channel_id=1, source_target_pairs={{1,0},{3,2},{5,4},{7,6},{9,8},{11,10},{13,12},{15,14},{17,16},{19,... | collective-permute-start | bytes 1179656 | tf_op jit(solution)/shard_map/ppermute | solution.py:215
  42.0 1.3 %collective-permute-start.10 = (f32[384,256]{1,0:T(8,128)S(1)}, f32[384,256]{1,0:T(8,128)S(1)}, u32[]{:S(2)}, u32[]{:S(2)}) collective-permute-start(f32[384,256]{1,0:T(8,128)S(1)} %get-tuple-element.58), channel_id=1, source_target_pairs={{1,2},{3,4},{5,6},{7,8},{9,10},{11,12},{13,14},{15,16},{17,18},{19... | collective-permute-start | bytes 1179656 | tf_op jit(solution)/shard_map/ppermute | solution.py:215
  43.4 4.7 %collective-permute-done.9.vert = f32[384,256]{1,0:T(8,128)S(1)} collective-permute-done((f32[384,256]{1,0:T(8,128)S(1)}, f32[384,256]{1,0:T(8,128)S(1)}, u32[]{:S(2)}, u32[]{:S(2)}) %collective-permute-start.9) | collective-permute-done | bytes 393248 | tf_op jit(solution)/shard_map/ppermute | solution.py:215
  48.1 7.0 %collective-permute-done.10.ctx = f32[384,256]{1,0:T(8,128)S(1)} collective-permute-done((f32[384,256]{1,0:T(8,128)S(1)}, f32[384,256]{1,0:T(8,128)S(1)}, u32[]{:S(2)}, u32[]{:S(2)}) %collective-permute-start.10) | collective-permute-done | bytes 393248 | tf_op jit(solution)/shard_map/ppermute | solution.py:215
  55.0 0.9 %shard_map.80 = (f32[384,256]{1,0:T(8,128)}, f32[384,256]{1,0:T(8,128)}) custom-call(f32[384,256]{1,0:T(8,128)S(1)} %collective-permute-done.9.vert, f32[384,256]{1,0:T(8,128)S(1)} %collective-permute-done.10.ctx, f32[384,256]{1,0:T(8,128)} %get-tuple-element.60.refs_0_, ...), custom_call_target="tpu_custom_call", output_to_operand_aliasing={{0}: (2, {}), {1}: (3, {})} | custom-call | tf_op jit(solution)/shard_map/pallas_call | solution.py:218
  (6 shorter events, 0.1 us)
Async XLA Ops:
  3.7 27.2 %collective-permute-start.2 = (s32[784,384]{1,0:T(8,128)S(1)}, s32[784,384]{1,0:T(8,128)S(1)}, u32[]{:S(2)}, u32[]{:S(2)}) collective-permute-start(s32[784,384]{1,0:T(8,128)S(1)} %get-tuple-element.43.own), channel_id=1, source_target_pairs={{0,1},{2,3},{4,5},{6,7},{8,9},{10,11},{12,13},{14,15},{16,17},{18,... | collective-permute-start | bytes 3612680 | tf_op jit(solution)/shard_map/ppermute | solution.py:215
  5.5 25.4 %collective-permute-start.3 = (s32[784,384]{1,0:T(8,128)S(1)}, s32[784,384]{1,0:T(8,128)S(1)}, u32[]{:S(2)}, u32[]{:S(2)}) collective-permute-start(s32[784,384]{1,0:T(8,128)S(1)} %get-tuple-element.43.own), channel_id=1, source_target_pairs={{1,0},{3,2},{5,4},{7,6},{9,8},{11,10},{13,12},{15,14},{17,16},{19,... | collective-permute-start | bytes 3612680 | tf_op jit(solution)/shard_map/ppermute | solution.py:215
  6.8 5.1 %collective-permute-start = (f32[384,256]{1,0:T(8,128)S(1)}, f32[384,256]{1,0:T(8,128)S(1)}, u32[]{:S(2)}, u32[]{:S(2)}) collective-permute-start(f32[384,256]{1,0:T(8,128)S(1)} %get-tuple-element.38), channel_id=1, source_target_pairs={{0,1},{2,3},{4,5},{6,7},{8,9},{10,11},{12,13},{14,15},{16,17},{18,... | collective-permute-start | bytes 1179656 | tf_op jit(solution)/shard_map/ppermute | solution.py:215
  9.9 17.8 %collective-permute-start.1 = (f32[384,256]{1,0:T(8,128)S(1)}, f32[384,256]{1,0:T(8,128)S(1)}, u32[]{:S(2)}, u32[]{:S(2)}) collective-permute-start(f32[384,256]{1,0:T(8,128)S(1)} %get-tuple-element.41), channel_id=1, source_target_pairs={{1,2},{3,4},{5,6},{7,8},{9,10},{11,12},{13,14},{15,16},{17,18},{19... | collective-permute-start | bytes 1179656 | tf_op jit(solution)/shard_map/ppermute | solution.py:215
  11.9 19.7 %collective-permute-start.4 = (f32[384,256]{1,0:T(8,128)S(1)}, f32[384,256]{1,0:T(8,128)S(1)}, u32[]{:S(2)}, u32[]{:S(2)}) collective-permute-start(f32[384,256]{1,0:T(8,128)S(1)} %get-tuple-element.40.after), channel_id=1, source_target_pairs={{1,64},{3,66},{5,68},{7,70},{9,72},{11,74},{13,76},{15,78},{17,80}... | collective-permute-start | bytes 1179656 | tf_op jit(solution)/shard_map/ppermute | solution.py:215
  28.9 6.6 %collective-permute-start.5 = (f32[384,256]{1,0:T(8,128)S(1)}, f32[384,256]{1,0:T(8,128)S(1)}, u32[]{:S(2)}, u32[]{:S(2)}) collective-permute-start(f32[384,256]{1,0:T(8,128)S(1)} %get-tuple-element.42.after), channel_id=1, source_target_pairs={{0,65},{2,67},{4,69},{6,71},{8,73},{10,75},{12,77},{14,79},{16,81}... | collective-permute-start | bytes 1179656 | tf_op jit(solution)/shard_map/ppermute | solution.py:215
  30.2 5.3 %collective-permute-start.6 = (f32[384,256]{1,0:T(8,128)S(1)}, f32[384,256]{1,0:T(8,128)S(1)}, u32[]{:S(2)}, u32[]{:S(2)}) collective-permute-start(f32[384,256]{1,0:T(8,128)S(1)} %get-tuple-element.48), channel_id=1, source_target_pairs={{1,3},{3,5},{5,7},{7,9},{9,11},{11,13},{13,15},{15,17},{17,19},{19... | collective-permute-start | bytes 1179656 | tf_op jit(solution)/shard_map/ppermute | solution.py:215
  32.8 2.7 %collective-permute-start.7 = (f32[384,256]{1,0:T(8,128)S(1)}, f32[384,256]{1,0:T(8,128)S(1)}, u32[]{:S(2)}, u32[]{:S(2)}) collective-permute-start(f32[384,256]{1,0:T(8,128)S(1)} %get-tuple-element.47.after), channel_id=1, source_target_pairs={{0,1},{2,3},{4,5},{6,7},{8,9},{10,11},{12,13},{14,15},{16,17},{18,... | collective-permute-start | bytes 1179656 | tf_op jit(solution)/shard_map/ppermute | solution.py:215
  34.2 6.6 %collective-permute-start.8 = (f32[384,256]{1,0:T(8,128)S(1)}, f32[384,256]{1,0:T(8,128)S(1)}, u32[]{:S(2)}, u32[]{:S(2)}) collective-permute-start(f32[384,256]{1,0:T(8,128)S(1)} %get-tuple-element.55), channel_id=1, source_target_pairs={{0,3},{2,5},{4,7},{6,9},{8,11},{10,13},{12,15},{14,17},{16,19},{18... | collective-permute-start | bytes 1179656 | tf_op jit(solution)/shard_map/ppermute | solution.py:215
  40.7 7.3 %collective-permute-start.9 = (f32[384,256]{1,0:T(8,128)S(1)}, f32[384,256]{1,0:T(8,128)S(1)}, u32[]{:S(2)}, u32[]{:S(2)}) collective-permute-start(f32[384,256]{1,0:T(8,128)S(1)} %get-tuple-element.57), channel_id=1, source_target_pairs={{1,0},{3,2},{5,4},{7,6},{9,8},{11,10},{13,12},{15,14},{17,16},{19,... | collective-permute-start | bytes 1179656 | tf_op jit(solution)/shard_map/ppermute | solution.py:215
  42.0 13.0 %collective-permute-start.10 = (f32[384,256]{1,0:T(8,128)S(1)}, f32[384,256]{1,0:T(8,128)S(1)}, u32[]{:S(2)}, u32[]{:S(2)}) collective-permute-start(f32[384,256]{1,0:T(8,128)S(1)} %get-tuple-element.58), channel_id=1, source_target_pairs={{1,2},{3,4},{5,6},{7,8},{9,10},{11,12},{13,14},{15,16},{17,18},{19... | collective-permute-start | bytes 1179656 | tf_op jit(solution)/shard_map/ppermute | solution.py:215

commit v4 on v3

--- a/solution.py
+++ b/solution.py
@@ -48,8 +48,8 @@
     return lax.dot_general(left, right, dims, preferred_element_type=F32)
 
 
-def tables(cnt, neg, mask, base_ref, slope_ref):
-    rows, tiles = cnt.shape[0], mask.shape[0]
+def tables(block, neg, mask, base_ref, slope_ref):
+    rows, tiles = base_ref.shape[0], mask.shape[0]
     tile = rows // tiles
     scale = 0.125 / math.sqrt(rows)
     columns = jnp.transpose(neg.astype(F32)).astype(jnp.int32)
@@ -60,7 +60,7 @@
             there = slice(tj * tile, (tj + 1) * tile)
             column = lax.broadcasted_iota(jnp.int32, (CHUNK, tile), 1) + tj * tile
             negcount = sum((pick == column).astype(F32) for pick in picks)
-            count = cnt[here, there].astype(F32)
+            count = block(here, there).astype(F32)
             gate = jnp.broadcast_to(mask[ti : ti + 1, tj : tj + 1].astype(F32) * scale, (CHUNK, tile))
             base_ref[here, there] = (count - negcount) * gate
             slope_ref[here, there] = (count + negcount) * gate
@@ -70,17 +70,62 @@
     return -(-steps * (rows + negs + tiles) // 8) * 8
 
 
-def tables_from(pack, index, steps, negs, tiles, base_ref, slope_ref):
+def pack_parts(pack, index, steps, negs, tiles):
     rows = pack.shape[1]
     at_neg = steps * rows + index * negs
     at_mask = steps * (rows + negs) + index * tiles
-    tables(
-        pack.at[index * rows : (index + 1) * rows],
-        pack[at_neg : at_neg + negs],
-        pack[at_mask : at_mask + tiles, :tiles],
-        base_ref,
-        slope_ref,
-    )
+    counts = pack.at[index * rows : (index + 1) * rows]
+    return counts, pack[at_neg : at_neg + negs], pack[at_mask : at_mask + tiles, :tiles]
+
+
+def tables_from(pack, index, steps, negs, tiles, base_ref, slope_ref):
+    counts, neg, mask = pack_parts(pack, index, steps, negs, tiles)
+    tables(lambda here, there: counts[here, there], neg, mask, base_ref, slope_ref)
+
+
+def folded_places(rows, width, negs, tiles):
+    half, rest = rows // 2, rows - width
+    first, second = slice(0, width), slice(width, rows)
+    counts = [
+        ((slice(0, rows), first), (slice(0, rows), first)),
+        ((slice(rows, rows + half), slice(0, rest)), (slice(0, half), second)),
+        ((slice(rows, rows + half), slice(rest, 2 * rest)), (slice(half, rows), second)),
+    ]
+    top = rows + half
+    neg = [(slice(top, top + negs), first), (slice(top + negs, top + 2 * negs), slice(0, rest))]
+    mask = (slice(top + 2 * negs, top + 2 * negs + tiles), slice(0, tiles))
+    return counts, neg, mask
+
+
+def folded_rows(rows, negs, tiles):
+    return -(-(rows + rows // 2 + 2 * negs + tiles) // 8) * 8
+
+
+def fold(pack, steps, negs, tiles, folded):
+    counts, neg, mask = pack_parts(pack, 0, steps, negs, tiles)
+    rows, width = pack.shape[1], folded.shape[1]
+    at_counts, at_neg, at_mask = folded_places(rows, width, negs, tiles)
+    for there, here in at_counts:
+        folded[there] = counts[here].astype(F32)
+    folded[at_neg[0]] = neg[:, :width].astype(F32)
+    folded[at_neg[1]] = neg[:, width:].astype(F32)
+    folded[at_mask] = mask.astype(F32)
+
+
+def tables_folded(folded, rows, negs, tiles, base_ref, slope_ref):
+    width, half = folded.shape[1], rows // 2
+    _, at_neg, at_mask = folded_places(rows, width, negs, tiles)
+
+    def block(here, there):
+        if there.stop <= width:
+            return folded[here, there]
+        low = here.stop <= half
+        row = rows + here.start - (0 if low else half)
+        column = there.start - width + (0 if low else rows - width)
+        return folded[row : row + CHUNK, column : column + there.stop - there.start]
+
+    neg = jnp.concatenate([folded[at_neg[0]], folded[at_neg[1]]], 1)
+    tables(block, neg, folded[at_mask], base_ref, slope_ref)
 
 
 def fill_pack(pack, first, steps, neg, mask):
@@ -100,14 +145,12 @@
     return new_vert, new_ctx
 
 
-def first_kernel(
-    core, kept, vert_hbm, ctx_hbm, counts_hbm, neg_hbm, mask_hbm, *refs
-):
+def first_kernel(core, kept, vert_hbm, ctx_hbm, counts_hbm, neg_hbm, mask_hbm, *refs):
     new_vert_ref, new_ctx_ref, near, far, vert, ctx, cnt, neg, mask, base, slope, sems = refs[kept:]
+    rows, negs, tiles = cnt.shape[0], neg.shape[0], mask.shape[0]
 
     @pl.when(on_core(core))
     def _():
-        rows = cnt.shape[0]
         pairs = [
             (neg_hbm, neg),
             (mask_hbm, mask),
@@ -123,22 +166,30 @@
             copy.start()
         for copy in copies[:5]:
             copy.wait()
-        tables(cnt, neg[:, 0], mask[:, 0], base, slope)
-        new_vert_ref[...], new_ctx_ref[...] = pass_body(vert[...], ctx[...], base[...], slope[...])
+        tables(lambda here, there: cnt[here, there], neg[:, 0], mask[:, 0], base, slope)
+        new_vert_ref[...], new_ctx_ref[: vert.shape[0]] = pass_body(vert[...], ctx[...], base[...], slope[...])
         fill_pack(near, 1, 1, neg, mask)
         fill_pack(far, 2, 2, neg, mask)
         for copy in copies[5:]:
             copy.wait()
 
-
-def near_kernel(negs, tiles, after, near, base_ref, slope_ref):
-    tables_from(near, 0, 1, negs, tiles, base_ref, slope_ref)
+    if core == 0:
+
+        @pl.when(on_core(1))
+        def _():
+            fold(far, 2, negs, tiles, new_ctx_ref)
+
+
+def near_kernel(core, negs, tiles, after, near, base_ref, slope_ref):
+    @pl.when(on_core(core))
+    def _():
+        tables_from(near, 0, 1, negs, tiles, base_ref, slope_ref)
 
 
 def far_kernel(negs, tiles, after, own, from_even, from_odd, base2, slope2, own_base3, own_slope3):
     @pl.when(on_core(0))
     def _():
-        tables_from(from_odd, 0, 2, negs, tiles, base2, slope2)
+        tables_folded(from_odd, own.shape[1], negs, tiles, base2, slope2)
 
     @pl.when(on_core(1))
     def _():
@@ -155,7 +206,9 @@
 def pass_kernel(core, after, vert_ref, ctx_ref, base_ref, slope_ref, new_vert_ref, new_ctx_ref):
     @pl.when(on_core(core))
     def _():
-        new_vert_ref[...], new_ctx_ref[...] = pass_body(vert_ref[...], ctx_ref[...], base_ref[...], slope_ref[...])
+        new_vert_ref[...], new_ctx_ref[...] = pass_body(
+            vert_ref[...], ctx_ref[: vert_ref.shape[0]], base_ref[...], slope_ref[...]
+        )
 
 
 def store_kernel(core, vert, ctx, *refs):
@@ -179,6 +232,7 @@
     state = pltpu.VMEM(part, F32)
     square = pltpu.VMEM((rows, rows), F32)
     small = [pltpu.VMEM(negatives.shape, jnp.int32), pltpu.VMEM(masks.shape, jnp.int32)]
+    folded = pltpu.VMEM((folded_rows(rows, negs, tiles), part[1]), F32)
     packs = [pltpu.VMEM((packed_rows(rows, negs, tiles, steps), rows), jnp.int32) for steps in (1, 2)]
 
     def call(kernel, outs, arrays, in_specs=None, **kwargs):
@@ -195,7 +249,7 @@
         arrays = (vertex_embed, context_embed, counts, negatives, masks, *map(in_vmem, kept))
         return call(
             functools.partial(first_kernel, core, len(kept)),
-            (state, state, *packs),
+            (state, state if core else folded, *packs),
             arrays,
             [HBM_SPEC] * 5 + [VMEM_SPEC] * len(kept),
             scratch_shapes=[state, state, pltpu.VMEM((rows, rows), jnp.int32), *small, square, square, pltpu.SemaphoreType.DMA((8,))],
@@ -228,16 +282,16 @@
     vert_o, out, *packed = first(1)
     outer0 = moved(out, 1, 1)
     vert_e, out, near, far = first(0, *packed)
-    inner0 = moved(out, 0, 1)
+    inner0 = lax.ppermute(out, "blk", [(b, b ^ 1) for b in range(n_blk)])
     from_even = moved(far, 0, 1)
-    table1 = call(functools.partial(near_kernel, negs, tiles), (square,) * 2, (vert_e, in_vmem(near)))
+    table1 = call(functools.partial(near_kernel, 1, negs, tiles), (square,) * 2, (vert_e, in_vmem(near)))
     vert_o, out = one_pass(1, table1[0], vert_o, inner0, *table1)
     swap1 = moved(vert_o, 1, -1, True)
-    from_odd = moved(far, 1, -1)
     outer1 = moved(out, 1, 2)
-    vert_e, out = one_pass(0, vert_o, vert_e, outer0, *table1)
+    table1 = call(functools.partial(near_kernel, 0, negs, tiles), (square,) * 2, (vert_o, in_vmem(near)))
+    vert_e, out = one_pass(0, table1[0], vert_e, outer0, *table1)
     swap0 = moved(vert_e, 0, 1, True)
-    arrays = (vert_e, *map(in_vmem, (far, from_even, from_odd)))
+    arrays = (vert_e, *map(in_vmem, (far, from_even, inner0)))
     far_tables = call(functools.partial(far_kernel, negs, tiles), (square,) * 4, arrays)
     table2, odd3 = far_tables[:2], far_tables[2:]
     vert_o, out = one_pass(0, table2[0], swap1, out, *table2)

time: 56.2 us -> 54.9 us (0.977)
  starting transfers between devices: 16 us -> 13.6 us
  waiting for transfers between devices: 31.3 us -> 32.5 us
    ppermute x11 -> x9, starting transfers between devices: 16 us -> 11.6 us  [moved(): return lax.ppermute(value, ('grp', 'blk'), pairs)]
    ppermute x0 -> x1, starting transfers between devices: none -> 1.92 us  [on_device(): inner0 = lax.ppermute(out, 'blk', [(b, b ^ 1) for b in range(n_blk)])]
    ppermute x0 -> x1, waiting for transfers between devices: none -> 0.67 us  [on_device(): inner0 = lax.ppermute(out, 'blk', [(b, b ^ 1) for b in range(n_blk)])]
    ppermute x11 -> x9, waiting for transfers between devices: 31.3 us -> 31.8 us  [moved(): return lax.ppermute(value, ('grp', 'blk'), pairs)]
    pallas_call x11 -> x12, Pallas kernels: 6.82 us -> 6.79 us  [call(): pl.pallas_call(kernel, out_shape=tuple(outs), in_specs=in_specs or [ANY_S...]
  transfers between devices with their start and end apart: 11 -> 10, of which waited for: 4 -> 5; matrix products, arithmetic and copies ran while one was open for 0% -> 0% of each run, Pallas kernels for 7% -> 7%
where the time goes in v4:
time: 54.9 us; the launch traced here: 54.6 us
  waiting for transfers between devices  32.5 us (59%)
  starting transfers between devices  13.6 us (25%)
  Pallas kernels  7.72 us (14%)
  between operations  0.82 us (1%)
    ppermute x9, waiting for transfers between devices, moved(): return lax.ppermute(value, ('grp', 'blk'), pairs)  31.8 us
    ppermute x9, starting transfers between devices, moved(): return lax.ppermute(value, ('grp', 'blk'), pairs)  11.6 us
    pallas_call x12, Pallas kernels, call(): pl.pallas_call(kernel, out_shape=tuple(outs), in_specs=in_specs or [ANY_S...  6.79 us
    ppermute x1, starting transfers between devices, on_device(): inner0 = lax.ppermute(out, 'blk', [(b, b ^ 1) for b in range(n_blk)])  1.92 us
  transfers between devices with their start and end apart: 10, of which 5 were waited for; matrix products, arithmetic and copies ran while one was open for 0% of the time, Pallas kernels for 7%

profile of v4, /device:TPU:6, one launch (start us, length us, event | category | flops | bytes accessed | tf_op | source)
XLA Modules:
  0.0 54.6 jit_solution(11939483750750432029)
XLA Ops:
  0.6 0.1 shard_map.68
  0.7 2.9 %shard_map.69 = (f32[384,256]{1,0:T(8,128)S(1)}, f32[592,256]{1,0:T(8,128)S(1)}, s32[392,384]{1,0:T(8,128)S(1)}, s32[784,384]{1,0:T(8,128)S(1)}) custom-call(f32[384,256]{1,0:T(8,128)} %vert_hbm.3, f32[384,256]{1,0:T(8,128)} %ctx_hbm.3, s32[4,384,384]{2,1,0:T(8,128)} %counts_hbm.3, ...), custom_call_target="tpu_custom_call", output_to_operand_aliasing={{2}: (5, {}), {3}: (6, {})} | custom-call | tf_op jit(solution)/shard_map/pallas_call | solution.py:239
  3.7 1.9 %collective-permute-start.2 = (s32[784,384]{1,0:T(8,128)S(1)}, s32[784,384]{1,0:T(8,128)S(1)}, u32[]{:S(2)}, u32[]{:S(2)}) collective-permute-start(s32[784,384]{1,0:T(8,128)S(1)} %get-tuple-element.47.own), channel_id=1, source_target_pairs={{0,1},{2,3},{4,5},{6,7},{8,9},{10,11},{12,13},{14,15},{16,17},{18,... | collective-permute-start | bytes 3612680 | tf_op jit(solution)/shard_map/ppermute | solution.py:269
  5.5 1.9 %collective-permute-start = (f32[592,256]{1,0:T(8,128)S(1)}, f32[592,256]{1,0:T(8,128)S(1)}, u32[]{:S(2)}, u32[]{:S(2)}) collective-permute-start(f32[592,256]{1,0:T(8,128)S(1)} %get-tuple-element.40), channel_id=1, source_target_pairs={{0,1},{1,0},{2,3},{3,2},{4,5},{5,4},{6,7},{7,6},{8,9},{9,8},{10,11... | collective-permute-start | bytes 1818632 | tf_op jit(solution)/shard_map/ppermute | solution.py:285
  7.5 1.3 %collective-permute-start.1 = (f32[384,256]{1,0:T(8,128)S(1)}, f32[384,256]{1,0:T(8,128)S(1)}, u32[]{:S(2)}, u32[]{:S(2)}) collective-permute-start(f32[384,256]{1,0:T(8,128)S(1)} %get-tuple-element.44), channel_id=1, source_target_pairs={{1,2},{3,4},{5,6},{7,8},{9,10},{11,12},{13,14},{15,16},{17,18},{19... | collective-permute-start | bytes 1179656 | tf_op jit(solution)/shard_map/ppermute | solution.py:269
  8.8 0.7 %collective-permute-done.ctx_ref.from_odd = f32[592,256]{1,0:T(8,128)S(1)} collective-permute-done((f32[592,256]{1,0:T(8,128)S(1)}, f32[592,256]{1,0:T(8,128)S(1)}, u32[]{:S(2)}, u32[]{:S(2)}) %collective-permute-start) | collective-permute-done | bytes 606240 | tf_op jit(solution)/shard_map/ppermute | solution.py:285
  9.5 1.3 %collective-permute-start.3 = (f32[384,256]{1,0:T(8,128)S(1)}, f32[384,256]{1,0:T(8,128)S(1)}, u32[]{:S(2)}, u32[]{:S(2)}) collective-permute-start(f32[384,256]{1,0:T(8,128)S(1)} %get-tuple-element.42.after), channel_id=1, source_target_pairs={{1,64},{3,66},{5,68},{7,70},{9,72},{11,74},{13,76},{15,78},{17,80}... | collective-permute-start | bytes 1179656 | tf_op jit(solution)/shard_map/ppermute | solution.py:269
  10.8 0.7 %shard_map.72 = (f32[384,384]{1,0:T(8,128)S(1)}, f32[384,384]{1,0:T(8,128)S(1)}) custom-call(f32[384,256]{1,0:T(8,128)S(1)} %get-tuple-element.42.after, s32[392,384]{1,0:T(8,128)S(1)} %get-tuple-element.37.near), custom_call_target="tpu_custom_call" | custom-call | tf_op jit(solution)/shard_map/pallas_call | solution.py:239
  11.4 14.9 %collective-permute-done.1.ctx_ref = f32[384,256]{1,0:T(8,128)S(1)} collective-permute-done((f32[384,256]{1,0:T(8,128)S(1)}, f32[384,256]{1,0:T(8,128)S(1)}, u32[]{:S(2)}, u32[]{:S(2)}) %collective-permute-start.1) | collective-permute-done | bytes 393248 | tf_op jit(solution)/shard_map/ppermute | solution.py:269
  26.4 1.2 %shard_map.73 = (f32[384,256]{1,0:T(8,128)S(1)}, f32[384,256]{1,0:T(8,128)S(1)}) custom-call(f32[384,384]{1,0:T(8,128)S(1)} %get-tuple-element.43.after.base_ref, f32[384,256]{1,0:T(8,128)S(1)} %get-tuple-element.36.after.vert_ref, f32[384,256]{1,0:T(8,128)S(1)} %collective-permute-done.1.ctx_ref, f32[384,384]{1,0:T(8,128)S(1)} %get-tuple-element.43.after.base_ref, ...), custom_call_target="tpu_custom_call" | custom-call | tf_op jit(solution)/shard_map/pallas_call | solution.py:239
  27.6 1.3 %collective-permute-start.4 = (f32[384,256]{1,0:T(8,128)S(1)}, f32[384,256]{1,0:T(8,128)S(1)}, u32[]{:S(2)}, u32[]{:S(2)}) collective-permute-start(f32[384,256]{1,0:T(8,128)S(1)} %get-tuple-element.46.after), channel_id=1, source_target_pairs={{0,65},{2,67},{4,69},{6,71},{8,73},{10,75},{12,77},{14,79},{16,81}... | collective-permute-start | bytes 1179656 | tf_op jit(solution)/shard_map/ppermute | solution.py:269
  28.9 0.7 %collective-permute-start.5 = (f32[384,256]{1,0:T(8,128)S(1)}, f32[384,256]{1,0:T(8,128)S(1)}, u32[]{:S(2)}, u32[]{:S(2)}) collective-permute-start(f32[384,256]{1,0:T(8,128)S(1)} %get-tuple-element.52), channel_id=1, source_target_pairs={{1,3},{3,5},{5,7},{7,9},{9,11},{11,13},{13,15},{15,17},{17,19},{19... | collective-permute-start | bytes 1179656 | tf_op jit(solution)/shard_map/ppermute | solution.py:269
  29.6 0.0 collective-permute-done.2.from_even
  29.6 0.7 %shard_map.74 = (f32[384,384]{1,0:T(8,128)S(1)}, f32[384,384]{1,0:T(8,128)S(1)}, f32[384,384]{1,0:T(8,128)S(1)}, f32[384,384]{1,0:T(8,128)S(1)}) custom-call(f32[384,256]{1,0:T(8,128)S(1)} %get-tuple-element.46.after, s32[784,384]{1,0:T(8,128)S(1)} %get-tuple-element.47.own, s32[784,384]{1,0:T(8,128)S(1)} %collective-permute-done.2.from_even, ...), custom_call_target="tpu_custom_call" | custom-call | tf_op jit(solution)/shard_map/pallas_call | solution.py:239
  30.3 0.0 collective-permute-done.3.vert_ref
  30.3 1.2 %shard_map.75 = (f32[384,256]{1,0:T(8,128)S(1)}, f32[384,256]{1,0:T(8,128)S(1)}) custom-call(f32[384,384]{1,0:T(8,128)S(1)} %get-tuple-element.48.after.base_ref, f32[384,256]{1,0:T(8,128)S(1)} %collective-permute-done.3.vert_ref, f32[384,256]{1,0:T(8,128)S(1)} %get-tuple-element.49.ctx_ref, f32[384,384]{1,0:T(8,128)S(1)} %get-tuple-element.48.after.base_ref, ...), custom_call_target="tpu_custom_call" | custom-call | tf_op jit(solution)/shard_map/pallas_call | solution.py:239
  31.5 1.3 %collective-permute-start.6 = (f32[384,256]{1,0:T(8,128)S(1)}, f32[384,256]{1,0:T(8,128)S(1)}, u32[]{:S(2)}, u32[]{:S(2)}) collective-permute-start(f32[384,256]{1,0:T(8,128)S(1)} %get-tuple-element.51.after), channel_id=1, source_target_pairs={{0,1},{2,3},{4,5},{6,7},{8,9},{10,11},{12,13},{14,15},{16,17},{18,... | collective-permute-start | bytes 1179656 | tf_op jit(solution)/shard_map/ppermute | solution.py:269
  32.8 1.3 %collective-permute-start.7 = (f32[384,256]{1,0:T(8,128)S(1)}, f32[384,256]{1,0:T(8,128)S(1)}, u32[]{:S(2)}, u32[]{:S(2)}) collective-permute-start(f32[384,256]{1,0:T(8,128)S(1)} %get-tuple-element.59), channel_id=1, source_target_pairs={{0,3},{2,5},{4,7},{6,9},{8,11},{10,13},{12,15},{14,17},{16,19},{18... | collective-permute-start | bytes 1179656 | tf_op jit(solution)/shard_map/ppermute | solution.py:269
  34.1 0.0 collective-permute-done.4.vert_ref
  34.2 0.0 collective-permute-done.5.ctx_ref
  34.2 0.0 collective-permute-done.6.vert_ref
  34.2 5.1 %collective-permute-done.7.ctx_ref = f32[384,256]{1,0:T(8,128)S(1)} collective-permute-done((f32[384,256]{1,0:T(8,128)S(1)}, f32[384,256]{1,0:T(8,128)S(1)}, u32[]{:S(2)}, u32[]{:S(2)}) %collective-permute-start.7) | collective-permute-done | bytes 393248 | tf_op jit(solution)/shard_map/ppermute | solution.py:269
  39.4 1.3 %collective-permute-start.8 = (f32[384,256]{1,0:T(8,128)S(1)}, f32[384,256]{1,0:T(8,128)S(1)}, u32[]{:S(2)}, u32[]{:S(2)}) collective-permute-start(f32[384,256]{1,0:T(8,128)S(1)} %get-tuple-element.61), channel_id=1, source_target_pairs={{1,0},{3,2},{5,4},{7,6},{9,8},{11,10},{13,12},{15,14},{17,16},{19,... | collective-permute-start | bytes 1179656 | tf_op jit(solution)/shard_map/ppermute | solution.py:269
  40.7 1.3 %collective-permute-start.9 = (f32[384,256]{1,0:T(8,128)S(1)}, f32[384,256]{1,0:T(8,128)S(1)}, u32[]{:S(2)}, u32[]{:S(2)}) collective-permute-start(f32[384,256]{1,0:T(8,128)S(1)} %get-tuple-element.62), channel_id=1, source_target_pairs={{1,2},{3,4},{5,6},{7,8},{9,10},{11,12},{13,14},{15,16},{17,18},{19... | collective-permute-start | bytes 1179656 | tf_op jit(solution)/shard_map/ppermute | solution.py:269
  42.0 3.6 %collective-permute-done.8.vert = f32[384,256]{1,0:T(8,128)S(1)} collective-permute-done((f32[384,256]{1,0:T(8,128)S(1)}, f32[384,256]{1,0:T(8,128)S(1)}, u32[]{:S(2)}, u32[]{:S(2)}) %collective-permute-start.8) | collective-permute-done | bytes 393248 | tf_op jit(solution)/shard_map/ppermute | solution.py:269
  45.6 8.1 %collective-permute-done.9.ctx = f32[384,256]{1,0:T(8,128)S(1)} collective-permute-done((f32[384,256]{1,0:T(8,128)S(1)}, f32[384,256]{1,0:T(8,128)S(1)}, u32[]{:S(2)}, u32[]{:S(2)}) %collective-permute-start.9) | collective-permute-done | bytes 393248 | tf_op jit(solution)/shard_map/ppermute | solution.py:269
  53.7 0.9 %shard_map.81 = (f32[384,256]{1,0:T(8,128)}, f32[384,256]{1,0:T(8,128)}) custom-call(f32[384,256]{1,0:T(8,128)S(1)} %collective-permute-done.8.vert, f32[384,256]{1,0:T(8,128)S(1)} %collective-permute-done.9.ctx, f32[384,256]{1,0:T(8,128)} %get-tuple-element.64.refs_0_, ...), custom_call_target="tpu_custom_call", output_to_operand_aliasing={{0}: (2, {}), {1}: (3, {})} | custom-call | tf_op jit(solution)/shard_map/pallas_call | solution.py:272
  (7 shorter events, 0.1 us)
Async XLA Ops:
  3.7 25.9 %collective-permute-start.2 = (s32[784,384]{1,0:T(8,128)S(1)}, s32[784,384]{1,0:T(8,128)S(1)}, u32[]{:S(2)}, u32[]{:S(2)}) collective-permute-start(s32[784,384]{1,0:T(8,128)S(1)} %get-tuple-element.47.own), channel_id=1, source_target_pairs={{0,1},{2,3},{4,5},{6,7},{8,9},{10,11},{12,13},{14,15},{16,17},{18,... | collective-permute-start | bytes 3612680 | tf_op jit(solution)/shard_map/ppermute | solution.py:269
  5.5 3.9 %collective-permute-start = (f32[592,256]{1,0:T(8,128)S(1)}, f32[592,256]{1,0:T(8,128)S(1)}, u32[]{:S(2)}, u32[]{:S(2)}) collective-permute-start(f32[592,256]{1,0:T(8,128)S(1)} %get-tuple-element.40), channel_id=1, source_target_pairs={{0,1},{1,0},{2,3},{3,2},{4,5},{5,4},{6,7},{7,6},{8,9},{9,8},{10,11... | collective-permute-start | bytes 1818632 | tf_op jit(solution)/shard_map/ppermute | solution.py:285
  7.5 18.9 %collective-permute-start.1 = (f32[384,256]{1,0:T(8,128)S(1)}, f32[384,256]{1,0:T(8,128)S(1)}, u32[]{:S(2)}, u32[]{:S(2)}) collective-permute-start(f32[384,256]{1,0:T(8,128)S(1)} %get-tuple-element.44), channel_id=1, source_target_pairs={{1,2},{3,4},{5,6},{7,8},{9,10},{11,12},{13,14},{15,16},{17,18},{19... | collective-permute-start | bytes 1179656 | tf_op jit(solution)/shard_map/ppermute | solution.py:269
  9.5 20.8 %collective-permute-start.3 = (f32[384,256]{1,0:T(8,128)S(1)}, f32[384,256]{1,0:T(8,128)S(1)}, u32[]{:S(2)}, u32[]{:S(2)}) collective-permute-start(f32[384,256]{1,0:T(8,128)S(1)} %get-tuple-element.42.after), channel_id=1, source_target_pairs={{1,64},{3,66},{5,68},{7,70},{9,72},{11,74},{13,76},{15,78},{17,80}... | collective-permute-start | bytes 1179656 | tf_op jit(solution)/shard_map/ppermute | solution.py:269
  27.6 6.6 %collective-permute-start.4 = (f32[384,256]{1,0:T(8,128)S(1)}, f32[384,256]{1,0:T(8,128)S(1)}, u32[]{:S(2)}, u32[]{:S(2)}) collective-permute-start(f32[384,256]{1,0:T(8,128)S(1)} %get-tuple-element.46.after), channel_id=1, source_target_pairs={{0,65},{2,67},{4,69},{6,71},{8,73},{10,75},{12,77},{14,79},{16,81}... | collective-permute-start | bytes 1179656 | tf_op jit(solution)/shard_map/ppermute | solution.py:269
  28.9 5.3 %collective-permute-start.5 = (f32[384,256]{1,0:T(8,128)S(1)}, f32[384,256]{1,0:T(8,128)S(1)}, u32[]{:S(2)}, u32[]{:S(2)}) collective-permute-start(f32[384,256]{1,0:T(8,128)S(1)} %get-tuple-element.52), channel_id=1, source_target_pairs={{1,3},{3,5},{5,7},{7,9},{9,11},{11,13},{13,15},{15,17},{17,19},{19... | collective-permute-start | bytes 1179656 | tf_op jit(solution)/shard_map/ppermute | solution.py:269
  31.5 2.7 %collective-permute-start.6 = (f32[384,256]{1,0:T(8,128)S(1)}, f32[384,256]{1,0:T(8,128)S(1)}, u32[]{:S(2)}, u32[]{:S(2)}) collective-permute-start(f32[384,256]{1,0:T(8,128)S(1)} %get-tuple-element.51.after), channel_id=1, source_target_pairs={{0,1},{2,3},{4,5},{6,7},{8,9},{10,11},{12,13},{14,15},{16,17},{18,... | collective-permute-start | bytes 1179656 | tf_op jit(solution)/shard_map/ppermute | solution.py:269
  32.8 6.6 %collective-permute-start.7 = (f32[384,256]{1,0:T(8,128)S(1)}, f32[384,256]{1,0:T(8,128)S(1)}, u32[]{:S(2)}, u32[]{:S(2)}) collective-permute-start(f32[384,256]{1,0:T(8,128)S(1)} %get-tuple-element.59), channel_id=1, source_target_pairs={{0,3},{2,5},{4,7},{6,9},{8,11},{10,13},{12,15},{14,17},{16,19},{18... | collective-permute-start | bytes 1179656 | tf_op jit(solution)/shard_map/ppermute | solution.py:269
  39.4 6.2 %collective-permute-start.8 = (f32[384,256]{1,0:T(8,128)S(1)}, f32[384,256]{1,0:T(8,128)S(1)}, u32[]{:S(2)}, u32[]{:S(2)}) collective-permute-start(f32[384,256]{1,0:T(8,128)S(1)} %get-tuple-element.61), channel_id=1, source_target_pairs={{1,0},{3,2},{5,4},{7,6},{9,8},{11,10},{13,12},{15,14},{17,16},{19,... | collective-permute-start | bytes 1179656 | tf_op jit(solution)/shard_map/ppermute | solution.py:269
  40.7 13.0 %collective-permute-start.9 = (f32[384,256]{1,0:T(8,128)S(1)}, f32[384,256]{1,0:T(8,128)S(1)}, u32[]{:S(2)}, u32[]{:S(2)}) collective-permute-start(f32[384,256]{1,0:T(8,128)S(1)} %get-tuple-element.62), channel_id=1, source_target_pairs={{1,2},{3,4},{5,6},{7,8},{9,10},{11,12},{13,14},{15,16},{17,18},{19... | collective-permute-start | bytes 1179656 | tf_op jit(solution)/shard_map/ppermute | solution.py:269

commit v5 on v4

--- a/solution.py
+++ b/solution.py
@@ -48,22 +48,41 @@
     return lax.dot_general(left, right, dims, preferred_element_type=F32)
 
 
+def row_product(a, b):
+    left = jnp.concatenate([a[0], a[0], a[1]], 1)
+    right = jnp.concatenate([b[0], b[1], b[0]], 0)
+    half = left.shape[0] // 2
+    dot = functools.partial(lax.dot_general, dimension_numbers=NN, preferred_element_type=F32)
+    return jnp.concatenate([dot(left[:half], right), dot(left[half:], right)], 0)
+
+
+def negcounts(block_rows, tile, tiles, neg):
+    columns = jnp.transpose(neg.astype(F32)).astype(jnp.int32)
+    for row in range(0, columns.shape[0], block_rows):
+        here = slice(row, row + block_rows)
+        picks = [jnp.broadcast_to(columns[here, k : k + 1], (block_rows, tile)) for k in range(neg.shape[0])]
+        for tj in range(tiles):
+            column = lax.broadcasted_iota(jnp.int32, (block_rows, tile), 1) + tj * tile
+            yield here, slice(tj * tile, (tj + 1) * tile), sum((pick == column).astype(F32) for pick in picks)
+
+
+def gate_of(mask, tile, scale):
+    tiles = mask.shape[0]
+    mask = mask.astype(F32) * scale
+    spread = [[jnp.broadcast_to(mask[i : i + 1, j : j + 1], (tile, tile)) for j in range(tiles)] for i in range(tiles)]
+    return jnp.concatenate([jnp.concatenate(row, 1) for row in spread], 0)
+
+
 def tables(block, neg, mask, base_ref, slope_ref):
     rows, tiles = base_ref.shape[0], mask.shape[0]
     tile = rows // tiles
     scale = 0.125 / math.sqrt(rows)
-    columns = jnp.transpose(neg.astype(F32)).astype(jnp.int32)
-    for row in range(0, rows, CHUNK):
-        here, ti = slice(row, row + CHUNK), row // tile
-        picks = [jnp.broadcast_to(columns[here, k : k + 1], (CHUNK, tile)) for k in range(neg.shape[0])]
-        for tj in range(tiles):
-            there = slice(tj * tile, (tj + 1) * tile)
-            column = lax.broadcasted_iota(jnp.int32, (CHUNK, tile), 1) + tj * tile
-            negcount = sum((pick == column).astype(F32) for pick in picks)
-            count = block(here, there).astype(F32)
-            gate = jnp.broadcast_to(mask[ti : ti + 1, tj : tj + 1].astype(F32) * scale, (CHUNK, tile))
-            base_ref[here, there] = (count - negcount) * gate
-            slope_ref[here, there] = (count + negcount) * gate
+    for here, there, negcount in negcounts(CHUNK, tile, tiles, neg):
+        ti, tj = here.start // tile, there.start // tile
+        count = block(here, there).astype(F32)
+        gate = jnp.broadcast_to(mask[ti : ti + 1, tj : tj + 1].astype(F32) * scale, (CHUNK, tile))
+        base_ref[here, there] = (count - negcount) * gate
+        slope_ref[here, there] = (count + negcount) * gate
 
 
 def packed_rows(rows, negs, tiles, steps):
@@ -145,18 +164,28 @@
     return new_vert, new_ctx
 
 
+def context_part(vs, ctx, coef):
+    return ctx + row_product(halves(jnp.transpose(coef)), vs)
+
+
+def vertex_part(vert, ctx, coef):
+    return vert + row_product(halves(coef), halves(ctx))
+
+
 def first_kernel(core, kept, vert_hbm, ctx_hbm, counts_hbm, neg_hbm, mask_hbm, *refs):
-    new_vert_ref, new_ctx_ref, near, far, vert, ctx, cnt, neg, mask, base, slope, sems = refs[kept:]
+    refs, (cnt, neg, mask, negcount, sems) = refs[:-5], refs[-5:]
+    before, (near, far, vert, ctx, coef_ref, new_ctx_ref, *late) = refs[:kept], refs[kept:]
     rows, negs, tiles = cnt.shape[0], neg.shape[0], mask.shape[0]
+    tile = rows // tiles
 
     @pl.when(on_core(core))
     def _():
         pairs = [
             (neg_hbm, neg),
             (mask_hbm, mask),
-            (counts_hbm.at[0], cnt),
             (vert_hbm, vert),
             (ctx_hbm, ctx),
+            (counts_hbm.at[0], cnt),
             (counts_hbm.at[1], near.at[:rows]),
             (counts_hbm.at[2], far.at[:rows]),
             (counts_hbm.at[3], far.at[rows : 2 * rows]),
@@ -164,10 +193,18 @@
         copies = [pltpu.make_async_copy(source, target, sems.at[i]) for i, (source, target) in enumerate(pairs)]
         for copy in copies:
             copy.start()
-        for copy in copies[:5]:
+        copies[0].wait()
+        for here, there, value in negcounts(CHUNK, tile, tiles, neg[:, 0]):
+            negcount[here, there] = value
+        for copy in copies[1:5]:
             copy.wait()
-        tables(lambda here, there: cnt[here, there], neg[:, 0], mask[:, 0], base, slope)
-        new_vert_ref[...], new_ctx_ref[: vert.shape[0]] = pass_body(vert[...], ctx[...], base[...], slope[...])
+        vs, cs = halves(vert[...]), halves(ctx[...])
+        tanh = jnp.tanh(0.5 * product(vs, cs, NT))
+        count = cnt[...].astype(F32)
+        gate = gate_of(mask[:, 0], tile, 0.125 / math.sqrt(rows))
+        coef = gate * ((count - negcount[...]) - (count + negcount[...]) * tanh)
+        coef_ref[...] = coef
+        new_ctx_ref[: ctx.shape[0]] = context_part(vs, ctx[...], coef)
         fill_pack(near, 1, 1, neg, mask)
         fill_pack(far, 2, 2, neg, mask)
         for copy in copies[5:]:
@@ -178,29 +215,45 @@
         @pl.when(on_core(1))
         def _():
             fold(far, 2, negs, tiles, new_ctx_ref)
-
-
-def near_kernel(core, negs, tiles, after, near, base_ref, slope_ref):
-    @pl.when(on_core(core))
+            late[0][...] = vertex_part(*(ref[...] for ref in before[2:]))
+
+
+def odd_near_kernel(negs, tiles, after, near, base_ref, slope_ref):
+    @pl.when(on_core(1))
     def _():
         tables_from(near, 0, 1, negs, tiles, base_ref, slope_ref)
 
 
-def far_kernel(negs, tiles, after, own, from_even, from_odd, base2, slope2, own_base3, own_slope3):
+def even_near_kernel(negs, tiles, after, near, from_odd, vert, ctx, coef, base1, slope1, base2, slope2, new_vert_ref):
     @pl.when(on_core(0))
     def _():
-        tables_folded(from_odd, own.shape[1], negs, tiles, base2, slope2)
-
+        tables_from(near, 0, 1, negs, tiles, base1, slope1)
+        tables_folded(from_odd, near.shape[1], negs, tiles, base2, slope2)
+        new_vert_ref[...] = vertex_part(vert[...], ctx[...], coef[...])
+
+
+def odd_far_kernel(negs, tiles, after, own, from_even, base2, slope2, own_base3, own_slope3):
     @pl.when(on_core(1))
     def _():
         tables_from(from_even, 0, 2, negs, tiles, base2, slope2)
         tables_from(own, 1, 2, negs, tiles, own_base3, own_slope3)
 
 
-def last_kernel(negs, tiles, after, from_even, base_ref, slope_ref):
+def last_kernel(negs, tiles, after, from_even, vert2, ctx2, coef2, vert3, ctx3, coef3, base_ref, slope_ref, even_vert_ref, odd_vert_ref):
     @pl.when(on_core(1))
     def _():
         tables_from(from_even, 1, 2, negs, tiles, base_ref, slope_ref)
+        even_vert_ref[...] = vertex_part(vert2[...], ctx2[...], coef2[...])
+        odd_vert_ref[...] = vertex_part(vert3[...], ctx3[...], coef3[...])
+
+
+def context_kernel(core, after, vert_ref, ctx_ref, base_ref, slope_ref, coef_ref, new_ctx_ref):
+    @pl.when(on_core(core))
+    def _():
+        vs, cs = halves(vert_ref[...]), halves(ctx_ref[...])
+        coef = base_ref[...] - slope_ref[...] * jnp.tanh(0.5 * product(vs, cs, NT))
+        coef_ref[...] = coef
+        new_ctx_ref[...] = context_part(vs, ctx_ref[...], coef)
 
 
 def pass_kernel(core, after, vert_ref, ctx_ref, base_ref, slope_ref, new_vert_ref, new_ctx_ref):
@@ -211,12 +264,12 @@
         )
 
 
-def store_kernel(core, vert, ctx, *refs):
-    vert_hbm, ctx_hbm, sems = refs[-3:]
+def store_kernel(core, count, *refs):
+    sources, targets, sems = refs[:count], refs[-1 - count : -1], refs[-1]
 
     @pl.when(on_core(core))
     def _():
-        copies = [pltpu.make_async_copy(vert, vert_hbm, sems.at[0]), pltpu.make_async_copy(ctx, ctx_hbm, sems.at[1])]
+        copies = [pltpu.make_async_copy(s, t, sems.at[i]) for i, (s, t) in enumerate(zip(sources, targets, strict=True))]
         for copy in copies:
             copy.start()
         for copy in copies:
@@ -249,12 +302,16 @@
         arrays = (vertex_embed, context_embed, counts, negatives, masks, *map(in_vmem, kept))
         return call(
             functools.partial(first_kernel, core, len(kept)),
-            (state, state if core else folded, *packs),
+            (*packs, state, state, square) + ((state,) if core else (folded, state)),
             arrays,
             [HBM_SPEC] * 5 + [VMEM_SPEC] * len(kept),
-            scratch_shapes=[state, state, pltpu.VMEM((rows, rows), jnp.int32), *small, square, square, pltpu.SemaphoreType.DMA((8,))],
-            input_output_aliases={5 + i: 2 + i for i in range(len(kept))},
+            scratch_shapes=[pltpu.VMEM((rows, rows), jnp.int32), *small, square, pltpu.SemaphoreType.DMA((8,))],
+            input_output_aliases={5 + i: i for i in range(len(kept[:2]))},
         )
+
+    def context_pass(core, after, vert, ctx, base, slope):
+        arrays = (after, *map(in_vmem, (vert, ctx, base, slope)))
+        return call(functools.partial(context_kernel, core), (square, state), arrays)
 
     def one_pass(core, after, vert, ctx, base, slope):
         arrays = (after, *map(in_vmem, (vert, ctx, base, slope)))
@@ -268,43 +325,47 @@
         ]
         return lax.ppermute(value, ("grp", "blk"), pairs)
 
-    def store(core, vert, ctx, *stored):
+    def store(core, arrays, stored=()):
+        count = len(arrays)
         return pl.pallas_call(
-            functools.partial(store_kernel, core),
-            out_shape=(pltpu.HBM(part, F32),) * 2,
-            in_specs=[VMEM_SPEC] * 2 + [HBM_SPEC] * len(stored),
-            out_specs=(HBM_SPEC,) * 2,
-            scratch_shapes=[pltpu.SemaphoreType.DMA((2,))],
-            input_output_aliases={2 + i: i for i in range(len(stored))},
+            functools.partial(store_kernel, core, count),
+            out_shape=(pltpu.HBM(part, F32),) * count,
+            in_specs=[VMEM_SPEC] * count + [HBM_SPEC] * len(stored),
+            out_specs=(HBM_SPEC,) * count,
+            scratch_shapes=[pltpu.SemaphoreType.DMA((count,))],
+            input_output_aliases={count + i: i for i in range(len(stored))},
             compiler_params=params(4),
-        )(*map(in_vmem, (vert, ctx)), *stored)
-
-    vert_o, out, *packed = first(1)
+        )(*map(in_vmem, arrays), *stored)
+
+    near, far, *start_o, out = first(1)
     outer0 = moved(out, 1, 1)
-    vert_e, out, near, far = first(0, *packed)
+    near, far, *start_e, out, vert_o = first(0, near, far, *start_o)
     inner0 = lax.ppermute(out, "blk", [(b, b ^ 1) for b in range(n_blk)])
-    from_even = moved(far, 0, 1)
-    table1 = call(functools.partial(near_kernel, 1, negs, tiles), (square,) * 2, (vert_e, in_vmem(near)))
-    vert_o, out = one_pass(1, table1[0], vert_o, inner0, *table1)
+    table = call(functools.partial(odd_near_kernel, negs, tiles), (square,) * 2, (start_e[2], in_vmem(near)))
+    vert_o, out = one_pass(1, table[0], vert_o, inner0, *table)
     swap1 = moved(vert_o, 1, -1, True)
     outer1 = moved(out, 1, 2)
-    table1 = call(functools.partial(near_kernel, 0, negs, tiles), (square,) * 2, (vert_o, in_vmem(near)))
-    vert_e, out = one_pass(0, table1[0], vert_e, outer0, *table1)
+    arrays = (vert_o, *map(in_vmem, (near, inner0, *start_e)))
+    *table, vert_e = call(functools.partial(even_near_kernel, negs, tiles), (square,) * 4 + (state,), arrays)
+    vert_e, out = one_pass(0, table[3], vert_e, outer0, *table[:2])
     swap0 = moved(vert_e, 0, 1, True)
-    arrays = (vert_e, *map(in_vmem, (far, from_even, inner0)))
-    far_tables = call(functools.partial(far_kernel, negs, tiles), (square,) * 4, arrays)
-    table2, odd3 = far_tables[:2], far_tables[2:]
-    vert_o, out = one_pass(0, table2[0], swap1, out, *table2)
+    from_even = moved(far, 0, 1)
+    vert_o, out = one_pass(0, vert_e, swap1, out, *table[2:])
+    outer2 = moved(out, 0, 3)
     lend = moved(vert_o, 0, 1)
-    outer2 = moved(out, 0, 3)
-    vert_e, out = one_pass(1, vert_o, swap0, outer1, *table2)
-    vert_o, out = one_pass(1, vert_e, lend, out, *odd3)
-    outer3 = moved(out, 1, 1)
-    even3 = call(functools.partial(last_kernel, negs, tiles), (square,) * 2, (vert_o, in_vmem(from_even)))
-    vert_e, out = one_pass(1, even3[0], vert_e, outer2, *even3)
+    arrays = (vert_o, in_vmem(far), in_vmem(from_even))
+    table = call(functools.partial(odd_far_kernel, negs, tiles), (square,) * 4, arrays)
+    coef2, out2 = context_pass(1, table[3], swap0, outer1, *table[:2])
+    coef3, out3 = context_pass(1, coef2, lend, out2, *table[2:])
+    outer3 = moved(out3, 1, 1)
+    arrays = (coef3, *map(in_vmem, (from_even, swap0, outer1, coef2, lend, out2, coef3)))
+    *table, vert_e, vert_o = call(functools.partial(last_kernel, negs, tiles), (square, square, state, state), arrays)
+    vert_e, out = one_pass(1, table[1], vert_e, outer2, *table)
     back = moved(vert_e, 1, -1)
-    stored = store(1, vert_o, out)
-    return tuple(store(0, back, outer3, *stored))
+    vert_done, ctx_done = store(1, (vert_o, out))
+    (vert_done,) = store(0, (back,), (vert_done,))
+    (ctx_done,) = store(0, (outer3,), (ctx_done,))
+    return vert_done, ctx_done
 
 
 def solution(mesh):

time: 54.9 us -> 52.9 us (0.964)
  waiting for transfers between devices: 32.5 us -> 29.8 us
  starting transfers between devices: 13.6 us -> 14.2 us
    ppermute x9, waiting for transfers between devices: 31.8 us -> 29.8 us  [moved(): return lax.ppermute(value, ('grp', 'blk'), pairs)]
    ppermute x1, waiting for transfers between devices: 0.67 us -> 0.01 us  [on_device(): inner0 = lax.ppermute(out, 'blk', [(b, b ^ 1) for b in range(n_blk)])]
    pallas_call x2 -> x3, Pallas kernels: 0.93 us -> 1.54 us  [store(): pl.pallas_call(functools.partial(store_kernel, core, count), out_shape=(p...]
  transfers between devices with their start and end apart: 10 -> 10, of which waited for: 5 -> 5; matrix products, arithmetic and copies ran while one was open for 0% -> 0% of each run, Pallas kernels for 7% -> 9%
where the time goes in v5:
time: 52.9 us; the launch traced here: 52.6 us
  waiting for transfers between devices  29.8 us (56%)
  starting transfers between devices  14.2 us (27%)
  Pallas kernels  7.81 us (15%)
  between operations  0.82 us (2%)
    ppermute x9, waiting for transfers between devices, moved(): return lax.ppermute(value, ('grp', 'blk'), pairs)  29.8 us
    ppermute x9, starting transfers between devices, moved(): return lax.ppermute(value, ('grp', 'blk'), pairs)  11.9 us
    pallas_call x12, Pallas kernels, call(): pl.pallas_call(kernel, out_shape=tuple(outs), in_specs=in_specs or [ANY_S...  6.27 us
    ppermute x1, starting transfers between devices, on_device(): inner0 = lax.ppermute(out, 'blk', [(b, b ^ 1) for b in range(n_blk)])  2.23 us
    pallas_call x3, Pallas kernels, store(): pl.pallas_call(functools.partial(store_kernel, core, count), out_shape=(p...  1.54 us
  transfers between devices with their start and end apart: 10, of which 5 were waited for; matrix products, arithmetic and copies ran while one was open for 0% of the time, Pallas kernels for 9%

profile of v5, /device:TPU:6, one launch (start us, length us, event | category | flops | bytes accessed | tf_op | source)
XLA Modules:
  0.0 52.6 jit_solution(10616014847104357510)
XLA Ops:
  0.6 0.1 shard_map.68
  0.7 2.4 %shard_map.69 = (s32[392,384]{1,0:T(8,128)S(1)}, s32[784,384]{1,0:T(8,128)S(1)}, f32[384,256]{1,0:T(8,128)S(1)}, f32[384,256]{1,0:T(8,128)S(1)}, f32[384,384]{1,...) custom-call(f32[384,256]{1,0:T(8,128)} %vert_hbm.3, ...), custom_call_target="tpu_custom_call", output_to_operand_aliasing={{0}: (5, {}), {1}: (6, {})} | custom-call | tf_op jit(solution)/shard_map/pallas_call | solution.py:292
  3.1 2.2 %collective-permute-start = (f32[592,256]{1,0:T(8,128)S(1)}, f32[592,256]{1,0:T(8,128)S(1)}, u32[]{:S(2)}, u32[]{:S(2)}) collective-permute-start(f32[592,256]{1,0:T(8,128)S(1)} %get-tuple-element.53), channel_id=1, source_target_pairs={{0,1},{1,0},{2,3},{3,2},{4,5},{5,4},{6,7},{7,6},{8,9},{9,8},{10,11... | collective-permute-start | bytes 1818632 | tf_op jit(solution)/shard_map/ppermute | solution.py:343
  5.4 2.2 %collective-permute-start.3 = (s32[784,384]{1,0:T(8,128)S(1)}, s32[784,384]{1,0:T(8,128)S(1)}, u32[]{:S(2)}, u32[]{:S(2)}) collective-permute-start(s32[784,384]{1,0:T(8,128)S(1)} %get-tuple-element.67.own), channel_id=1, source_target_pairs={{0,1},{2,3},{4,5},{6,7},{8,9},{10,11},{12,13},{14,15},{16,17},{18,... | collective-permute-start | bytes 3612680 | tf_op jit(solution)/shard_map/ppermute | solution.py:326
  7.5 1.3 %collective-permute-start.1 = (f32[384,256]{1,0:T(8,128)S(1)}, f32[384,256]{1,0:T(8,128)S(1)}, u32[]{:S(2)}, u32[]{:S(2)}) collective-permute-start(f32[384,256]{1,0:T(8,128)S(1)} %get-tuple-element.60), channel_id=1, source_target_pairs={{1,2},{3,4},{5,6},{7,8},{9,10},{11,12},{13,14},{15,16},{17,18},{19... | collective-permute-start | bytes 1179656 | tf_op jit(solution)/shard_map/ppermute | solution.py:326
  8.9 0.0 collective-permute-done.ctx_ref.from_odd
  8.9 1.3 %collective-permute-start.2 = (f32[384,256]{1,0:T(8,128)S(1)}, f32[384,256]{1,0:T(8,128)S(1)}, u32[]{:S(2)}, u32[]{:S(2)}) collective-permute-start(f32[384,256]{1,0:T(8,128)S(1)} %get-tuple-element.55.after), channel_id=1, source_target_pairs={{1,64},{3,66},{5,68},{7,70},{9,72},{11,74},{13,76},{15,78},{17,80}... | collective-permute-start | bytes 1179656 | tf_op jit(solution)/shard_map/ppermute | solution.py:326
  10.2 1.4 %shard_map.72 = (f32[384,384]{1,0:T(8,128)S(1)}, f32[384,384]{1,0:T(8,128)S(1)}, f32[384,384]{1,0:T(8,128)S(1)}, f32[384,384]{1,0:T(8,128)S(1)}, f32[384,256]{1,0:T(8,128)S(1)}) custom-call(f32[384,256]{1,0:T(8,128)S(1)} %get-tuple-element.55.after, s32[392,384]{1,0:T(8,128)S(1)} %get-tuple-element.50.near, ...), custom_call_target="tpu_custom_call" | custom-call | tf_op jit(solution)/shard_map/pallas_call | solution.py:292
  11.6 13.7 %collective-permute-done.1.ctx_ref = f32[384,256]{1,0:T(8,128)S(1)} collective-permute-done((f32[384,256]{1,0:T(8,128)S(1)}, f32[384,256]{1,0:T(8,128)S(1)}, u32[]{:S(2)}, u32[]{:S(2)}) %collective-permute-start.1) | collective-permute-done | bytes 393248 | tf_op jit(solution)/shard_map/ppermute | solution.py:326
  25.3 1.2 %shard_map.73 = (f32[384,256]{1,0:T(8,128)S(1)}, f32[384,256]{1,0:T(8,128)S(1)}) custom-call(f32[384,384]{1,0:T(8,128)S(1)} %get-tuple-element.58.after.slope_ref, f32[384,256]{1,0:T(8,128)S(1)} %get-tuple-element.59.vert_ref, f32[384,256]{1,0:T(8,128)S(1)} %collective-permute-done.1.ctx_ref, f32[384,384]{1,0:T(8,128)S(1)} %get-tuple-element.61.base_ref, ...), custom_call_target="tpu_custom_call" | custom-call | tf_op jit(solution)/shard_map/pallas_call | solution.py:292
  26.4 1.3 %collective-permute-start.4 = (f32[384,256]{1,0:T(8,128)S(1)}, f32[384,256]{1,0:T(8,128)S(1)}, u32[]{:S(2)}, u32[]{:S(2)}) collective-permute-start(f32[384,256]{1,0:T(8,128)S(1)} %get-tuple-element.63.after), channel_id=1, source_target_pairs={{0,65},{2,67},{4,69},{6,71},{8,73},{10,75},{12,77},{14,79},{16,81}... | collective-permute-start | bytes 1179656 | tf_op jit(solution)/shard_map/ppermute | solution.py:326
  27.8 0.7 %collective-permute-start.5 = (f32[384,256]{1,0:T(8,128)S(1)}, f32[384,256]{1,0:T(8,128)S(1)}, u32[]{:S(2)}, u32[]{:S(2)}) collective-permute-start(f32[384,256]{1,0:T(8,128)S(1)} %get-tuple-element.69), channel_id=1, source_target_pairs={{1,3},{3,5},{5,7},{7,9},{9,11},{11,13},{13,15},{15,17},{17,19},{19... | collective-permute-start | bytes 1179656 | tf_op jit(solution)/shard_map/ppermute | solution.py:326
  28.5 0.0 collective-permute-done.2.vert_ref
  28.5 1.2 %shard_map.74 = (f32[384,256]{1,0:T(8,128)S(1)}, f32[384,256]{1,0:T(8,128)S(1)}) custom-call(f32[384,256]{1,0:T(8,128)S(1)} %get-tuple-element.63.after, f32[384,256]{1,0:T(8,128)S(1)} %collective-permute-done.2.vert_ref, f32[384,256]{1,0:T(8,128)S(1)} %get-tuple-element.64.ctx_ref, f32[384,384]{1,0:T(8,128)S(1)} %get-tuple-element.65.base_ref, ...), custom_call_target="tpu_custom_call" | custom-call | tf_op jit(solution)/shard_map/pallas_call | solution.py:292
  29.7 1.3 %collective-permute-start.6 = (f32[384,256]{1,0:T(8,128)S(1)}, f32[384,256]{1,0:T(8,128)S(1)}, u32[]{:S(2)}, u32[]{:S(2)}) collective-permute-start(f32[384,256]{1,0:T(8,128)S(1)} %get-tuple-element.66.after), channel_id=1, source_target_pairs={{0,1},{2,3},{4,5},{6,7},{8,9},{10,11},{12,13},{14,15},{16,17},{18,... | collective-permute-start | bytes 1179656 | tf_op jit(solution)/shard_map/ppermute | solution.py:326
  31.0 1.3 %collective-permute-start.7 = (f32[384,256]{1,0:T(8,128)S(1)}, f32[384,256]{1,0:T(8,128)S(1)}, u32[]{:S(2)}, u32[]{:S(2)}) collective-permute-start(f32[384,256]{1,0:T(8,128)S(1)} %get-tuple-element.78), channel_id=1, source_target_pairs={{0,3},{2,5},{4,7},{6,9},{8,11},{10,13},{12,15},{14,17},{16,19},{18... | collective-permute-start | bytes 1179656 | tf_op jit(solution)/shard_map/ppermute | solution.py:326
  32.3 0.0 collective-permute-done.3.from_even
  32.4 0.7 %collective-permute-done.4.vert_ref.vert2 = f32[384,256]{1,0:T(8,128)S(1)} collective-permute-done((f32[384,256]{1,0:T(8,128)S(1)}, f32[384,256]{1,0:T(8,128)S(1)}, u32[]{:S(2)}, u32[]{:S(2)}) %collective-permute-start.4) | collective-permute-done | bytes 393248 | tf_op jit(solution)/shard_map/ppermute | solution.py:326
  33.0 0.0 collective-permute-done.5.ctx_ref.ctx2
  33.0 0.0 collective-permute-done.6.vert_ref.vert3
  33.0 4.5 %collective-permute-done.7.ctx_ref = f32[384,256]{1,0:T(8,128)S(1)} collective-permute-done((f32[384,256]{1,0:T(8,128)S(1)}, f32[384,256]{1,0:T(8,128)S(1)}, u32[]{:S(2)}, u32[]{:S(2)}) %collective-permute-start.7) | collective-permute-done | bytes 393248 | tf_op jit(solution)/shard_map/ppermute | solution.py:326
  37.6 1.3 %collective-permute-start.8 = (f32[384,256]{1,0:T(8,128)S(1)}, f32[384,256]{1,0:T(8,128)S(1)}, u32[]{:S(2)}, u32[]{:S(2)}) collective-permute-start(f32[384,256]{1,0:T(8,128)S(1)} %get-tuple-element.80), channel_id=1, source_target_pairs={{1,0},{3,2},{5,4},{7,6},{9,8},{11,10},{13,12},{15,14},{17,16},{19,... | collective-permute-start | bytes 1179656 | tf_op jit(solution)/shard_map/ppermute | solution.py:326
  38.9 1.3 %collective-permute-start.9 = (f32[384,256]{1,0:T(8,128)S(1)}, f32[384,256]{1,0:T(8,128)S(1)}, u32[]{:S(2)}, u32[]{:S(2)}) collective-permute-start(f32[384,256]{1,0:T(8,128)S(1)} %get-tuple-element.84), channel_id=1, source_target_pairs={{1,2},{3,4},{5,6},{7,8},{9,10},{11,12},{13,14},{15,16},{17,18},{19... | collective-permute-start | bytes 1179656 | tf_op jit(solution)/shard_map/ppermute | solution.py:326
  40.2 4.7 %collective-permute-done.8.refs_0_ = f32[384,256]{1,0:T(8,128)S(1)} collective-permute-done((f32[384,256]{1,0:T(8,128)S(1)}, f32[384,256]{1,0:T(8,128)S(1)}, u32[]{:S(2)}, u32[]{:S(2)}) %collective-permute-start.8) | collective-permute-done | bytes 393248 | tf_op jit(solution)/shard_map/ppermute | solution.py:326
  44.9 0.8 %shard_map.81 = f32[384,256]{1,0:T(8,128)} custom-call(f32[384,256]{1,0:T(8,128)S(1)} %collective-permute-done.8.refs_0_, f32[384,256]{1,0:T(8,128)} %get-tuple-element.83.refs_1_), custom_call_target="tpu_custom_call", output_to_operand_aliasing={{}: (1, {})} | custom-call | tf_op jit(solution)/shard_map/pallas_call | solution.py:330
  45.7 6.2 %collective-permute-done.9.refs_0_ = f32[384,256]{1,0:T(8,128)S(1)} collective-permute-done((f32[384,256]{1,0:T(8,128)S(1)}, f32[384,256]{1,0:T(8,128)S(1)}, u32[]{:S(2)}, u32[]{:S(2)}) %collective-permute-start.9) | collective-permute-done | bytes 393248 | tf_op jit(solution)/shard_map/ppermute | solution.py:326
  51.9 0.8 %shard_map.82 = f32[384,256]{1,0:T(8,128)} custom-call(f32[384,256]{1,0:T(8,128)S(1)} %collective-permute-done.9.refs_0_, f32[384,256]{1,0:T(8,128)} %get-tuple-element.85.refs_1_), custom_call_target="tpu_custom_call", output_to_operand_aliasing={{}: (1, {})} | custom-call | tf_op jit(solution)/shard_map/pallas_call | solution.py:330
  (8 shorter events, 0.1 us)
Async XLA Ops:
  3.1 5.7 %collective-permute-start = (f32[592,256]{1,0:T(8,128)S(1)}, f32[592,256]{1,0:T(8,128)S(1)}, u32[]{:S(2)}, u32[]{:S(2)}) collective-permute-start(f32[592,256]{1,0:T(8,128)S(1)} %get-tuple-element.53), channel_id=1, source_target_pairs={{0,1},{1,0},{2,3},{3,2},{4,5},{5,4},{6,7},{7,6},{8,9},{9,8},{10,11... | collective-permute-start | bytes 1818632 | tf_op jit(solution)/shard_map/ppermute | solution.py:343
  5.4 26.9 %collective-permute-start.3 = (s32[784,384]{1,0:T(8,128)S(1)}, s32[784,384]{1,0:T(8,128)S(1)}, u32[]{:S(2)}, u32[]{:S(2)}) collective-permute-start(s32[784,384]{1,0:T(8,128)S(1)} %get-tuple-element.67.own), channel_id=1, source_target_pairs={{0,1},{2,3},{4,5},{6,7},{8,9},{10,11},{12,13},{14,15},{16,17},{18,... | collective-permute-start | bytes 3612680 | tf_op jit(solution)/shard_map/ppermute | solution.py:326
  7.5 17.7 %collective-permute-start.1 = (f32[384,256]{1,0:T(8,128)S(1)}, f32[384,256]{1,0:T(8,128)S(1)}, u32[]{:S(2)}, u32[]{:S(2)}) collective-permute-start(f32[384,256]{1,0:T(8,128)S(1)} %get-tuple-element.60), channel_id=1, source_target_pairs={{1,2},{3,4},{5,6},{7,8},{9,10},{11,12},{13,14},{15,16},{17,18},{19... | collective-permute-start | bytes 1179656 | tf_op jit(solution)/shard_map/ppermute | solution.py:326
  8.9 19.6 %collective-permute-start.2 = (f32[384,256]{1,0:T(8,128)S(1)}, f32[384,256]{1,0:T(8,128)S(1)}, u32[]{:S(2)}, u32[]{:S(2)}) collective-permute-start(f32[384,256]{1,0:T(8,128)S(1)} %get-tuple-element.55.after), channel_id=1, source_target_pairs={{1,64},{3,66},{5,68},{7,70},{9,72},{11,74},{13,76},{15,78},{17,80}... | collective-permute-start | bytes 1179656 | tf_op jit(solution)/shard_map/ppermute | solution.py:326
  26.4 6.6 %collective-permute-start.4 = (f32[384,256]{1,0:T(8,128)S(1)}, f32[384,256]{1,0:T(8,128)S(1)}, u32[]{:S(2)}, u32[]{:S(2)}) collective-permute-start(f32[384,256]{1,0:T(8,128)S(1)} %get-tuple-element.63.after), channel_id=1, source_target_pairs={{0,65},{2,67},{4,69},{6,71},{8,73},{10,75},{12,77},{14,79},{16,81}... | collective-permute-start | bytes 1179656 | tf_op jit(solution)/shard_map/ppermute | solution.py:326
  27.8 5.3 %collective-permute-start.5 = (f32[384,256]{1,0:T(8,128)S(1)}, f32[384,256]{1,0:T(8,128)S(1)}, u32[]{:S(2)}, u32[]{:S(2)}) collective-permute-start(f32[384,256]{1,0:T(8,128)S(1)} %get-tuple-element.69), channel_id=1, source_target_pairs={{1,3},{3,5},{5,7},{7,9},{9,11},{11,13},{13,15},{15,17},{17,19},{19... | collective-permute-start | bytes 1179656 | tf_op jit(solution)/shard_map/ppermute | solution.py:326
  29.7 3.4 %collective-permute-start.6 = (f32[384,256]{1,0:T(8,128)S(1)}, f32[384,256]{1,0:T(8,128)S(1)}, u32[]{:S(2)}, u32[]{:S(2)}) collective-permute-start(f32[384,256]{1,0:T(8,128)S(1)} %get-tuple-element.66.after), channel_id=1, source_target_pairs={{0,1},{2,3},{4,5},{6,7},{8,9},{10,11},{12,13},{14,15},{16,17},{18,... | collective-permute-start | bytes 1179656 | tf_op jit(solution)/shard_map/ppermute | solution.py:326
  31.0 6.6 %collective-permute-start.7 = (f32[384,256]{1,0:T(8,128)S(1)}, f32[384,256]{1,0:T(8,128)S(1)}, u32[]{:S(2)}, u32[]{:S(2)}) collective-permute-start(f32[384,256]{1,0:T(8,128)S(1)} %get-tuple-element.78), channel_id=1, source_target_pairs={{0,3},{2,5},{4,7},{6,9},{8,11},{10,13},{12,15},{14,17},{16,19},{18... | collective-permute-start | bytes 1179656 | tf_op jit(solution)/shard_map/ppermute | solution.py:326
  37.6 7.4 %collective-permute-start.8 = (f32[384,256]{1,0:T(8,128)S(1)}, f32[384,256]{1,0:T(8,128)S(1)}, u32[]{:S(2)}, u32[]{:S(2)}) collective-permute-start(f32[384,256]{1,0:T(8,128)S(1)} %get-tuple-element.80), channel_id=1, source_target_pairs={{1,0},{3,2},{5,4},{7,6},{9,8},{11,10},{13,12},{15,14},{17,16},{19,... | collective-permute-start | bytes 1179656 | tf_op jit(solution)/shard_map/ppermute | solution.py:326
  38.9 13.0 %collective-permute-start.9 = (f32[384,256]{1,0:T(8,128)S(1)}, f32[384,256]{1,0:T(8,128)S(1)}, u32[]{:S(2)}, u32[]{:S(2)}) collective-permute-start(f32[384,256]{1,0:T(8,128)S(1)} %get-tuple-element.84), channel_id=1, source_target_pairs={{1,2},{3,4},{5,6},{7,8},{9,10},{11,12},{13,14},{15,16},{17,18},{19... | collective-permute-start | bytes 1179656 | tf_op jit(solution)/shard_map/ppermute | solution.py:326

commit v6 on v5

--- a/solution.py
+++ b/solution.py
@@ -102,51 +102,6 @@
     tables(lambda here, there: counts[here, there], neg, mask, base_ref, slope_ref)
 
 
-def folded_places(rows, width, negs, tiles):
-    half, rest = rows // 2, rows - width
-    first, second = slice(0, width), slice(width, rows)
-    counts = [
-        ((slice(0, rows), first), (slice(0, rows), first)),
-        ((slice(rows, rows + half), slice(0, rest)), (slice(0, half), second)),
-        ((slice(rows, rows + half), slice(rest, 2 * rest)), (slice(half, rows), second)),
-    ]
-    top = rows + half
-    neg = [(slice(top, top + negs), first), (slice(top + negs, top + 2 * negs), slice(0, rest))]
-    mask = (slice(top + 2 * negs, top + 2 * negs + tiles), slice(0, tiles))
-    return counts, neg, mask
-
-
-def folded_rows(rows, negs, tiles):
-    return -(-(rows + rows // 2 + 2 * negs + tiles) // 8) * 8
-
-
-def fold(pack, steps, negs, tiles, folded):
-    counts, neg, mask = pack_parts(pack, 0, steps, negs, tiles)
-    rows, width = pack.shape[1], folded.shape[1]
-    at_counts, at_neg, at_mask = folded_places(rows, width, negs, tiles)
-    for there, here in at_counts:
-        folded[there] = counts[here].astype(F32)
-    folded[at_neg[0]] = neg[:, :width].astype(F32)
-    folded[at_neg[1]] = neg[:, width:].astype(F32)
-    folded[at_mask] = mask.astype(F32)
-
-
-def tables_folded(folded, rows, negs, tiles, base_ref, slope_ref):
-    width, half = folded.shape[1], rows // 2
-    _, at_neg, at_mask = folded_places(rows, width, negs, tiles)
-
-    def block(here, there):
-        if there.stop <= width:
-            return folded[here, there]
-        low = here.stop <= half
-        row = rows + here.start - (0 if low else half)
-        column = there.start - width + (0 if low else rows - width)
-        return folded[row : row + CHUNK, column : column + there.stop - there.start]
-
-    neg = jnp.concatenate([folded[at_neg[0]], folded[at_neg[1]]], 1)
-    tables(block, neg, folded[at_mask], base_ref, slope_ref)
-
-
 def fill_pack(pack, first, steps, neg, mask):
     negs, tiles, rows = neg.shape[0], mask.shape[0], pack.shape[1]
     for i in range(steps):
@@ -174,8 +129,8 @@
 
 def first_kernel(core, kept, vert_hbm, ctx_hbm, counts_hbm, neg_hbm, mask_hbm, *refs):
     refs, (cnt, neg, mask, negcount, sems) = refs[:-5], refs[-5:]
-    before, (near, far, vert, ctx, coef_ref, new_ctx_ref, *late) = refs[:kept], refs[kept:]
-    rows, negs, tiles = cnt.shape[0], neg.shape[0], mask.shape[0]
+    near, far, vert, ctx, coef_ref, new_ctx_ref = refs[kept:]
+    rows, tiles = cnt.shape[0], mask.shape[0]
     tile = rows // tiles
 
     @pl.when(on_core(core))
@@ -204,45 +159,39 @@
         gate = gate_of(mask[:, 0], tile, 0.125 / math.sqrt(rows))
         coef = gate * ((count - negcount[...]) - (count + negcount[...]) * tanh)
         coef_ref[...] = coef
-        new_ctx_ref[: ctx.shape[0]] = context_part(vs, ctx[...], coef)
+        new_ctx_ref[...] = context_part(vs, ctx[...], coef)
         fill_pack(near, 1, 1, neg, mask)
         fill_pack(far, 2, 2, neg, mask)
         for copy in copies[5:]:
             copy.wait()
 
-    if core == 0:
-
-        @pl.when(on_core(1))
-        def _():
-            fold(far, 2, negs, tiles, new_ctx_ref)
-            late[0][...] = vertex_part(*(ref[...] for ref in before[2:]))
-
-
-def odd_near_kernel(negs, tiles, after, near, base_ref, slope_ref):
+
+def odd_near_kernel(negs, tiles, after, far_in, near, vert, ctx, coef, far, base_ref, slope_ref, new_vert_ref):
     @pl.when(on_core(1))
     def _():
         tables_from(near, 0, 1, negs, tiles, base_ref, slope_ref)
-
-
-def even_near_kernel(negs, tiles, after, near, from_odd, vert, ctx, coef, base1, slope1, base2, slope2, new_vert_ref):
+        new_vert_ref[...] = vertex_part(vert[...], ctx[...], coef[...])
+
+
+def even_near_kernel(negs, tiles, after, near, mate, vert, ctx, coef, base1, slope1, base2, slope2, new_vert_ref):
     @pl.when(on_core(0))
     def _():
         tables_from(near, 0, 1, negs, tiles, base1, slope1)
-        tables_folded(from_odd, near.shape[1], negs, tiles, base2, slope2)
+        tables_from(mate, 0, 2, negs, tiles, base2, slope2)
         new_vert_ref[...] = vertex_part(vert[...], ctx[...], coef[...])
 
 
-def odd_far_kernel(negs, tiles, after, own, from_even, base2, slope2, own_base3, own_slope3):
+def odd_far_kernel(negs, tiles, after, own, mate, base2, slope2, own_base3, own_slope3):
     @pl.when(on_core(1))
     def _():
-        tables_from(from_even, 0, 2, negs, tiles, base2, slope2)
+        tables_from(mate, 0, 2, negs, tiles, base2, slope2)
         tables_from(own, 1, 2, negs, tiles, own_base3, own_slope3)
 
 
-def last_kernel(negs, tiles, after, from_even, vert2, ctx2, coef2, vert3, ctx3, coef3, base_ref, slope_ref, even_vert_ref, odd_vert_ref):
+def last_kernel(negs, tiles, after, mate, vert2, ctx2, coef2, vert3, ctx3, coef3, base_ref, slope_ref, even_vert_ref, odd_vert_ref):
     @pl.when(on_core(1))
     def _():
-        tables_from(from_even, 1, 2, negs, tiles, base_ref, slope_ref)
+        tables_from(mate, 1, 2, negs, tiles, base_ref, slope_ref)
         even_vert_ref[...] = vertex_part(vert2[...], ctx2[...], coef2[...])
         odd_vert_ref[...] = vertex_part(vert3[...], ctx3[...], coef3[...])
 
@@ -260,7 +209,7 @@
     @pl.when(on_core(core))
     def _():
         new_vert_ref[...], new_ctx_ref[...] = pass_body(
-            vert_ref[...], ctx_ref[: vert_ref.shape[0]], base_ref[...], slope_ref[...]
+            vert_ref[...], ctx_ref[...], base_ref[...], slope_ref[...]
         )
 
 
@@ -285,7 +234,6 @@
     state = pltpu.VMEM(part, F32)
     square = pltpu.VMEM((rows, rows), F32)
     small = [pltpu.VMEM(negatives.shape, jnp.int32), pltpu.VMEM(masks.shape, jnp.int32)]
-    folded = pltpu.VMEM((folded_rows(rows, negs, tiles), part[1]), F32)
     packs = [pltpu.VMEM((packed_rows(rows, negs, tiles, steps), rows), jnp.int32) for steps in (1, 2)]
 
     def call(kernel, outs, arrays, in_specs=None, **kwargs):
@@ -302,11 +250,11 @@
         arrays = (vertex_embed, context_embed, counts, negatives, masks, *map(in_vmem, kept))
         return call(
             functools.partial(first_kernel, core, len(kept)),
-            (*packs, state, state, square) + ((state,) if core else (folded, state)),
+            (*packs, state, state, square, state),
             arrays,
             [HBM_SPEC] * 5 + [VMEM_SPEC] * len(kept),
             scratch_shapes=[pltpu.VMEM((rows, rows), jnp.int32), *small, square, pltpu.SemaphoreType.DMA((8,))],
-            input_output_aliases={5 + i: i for i in range(len(kept[:2]))},
+            input_output_aliases={5 + i: i for i in range(len(kept))},
         )
 
     def context_pass(core, after, vert, ctx, base, slope):
@@ -339,26 +287,31 @@
 
     near, far, *start_o, out = first(1)
     outer0 = moved(out, 1, 1)
-    near, far, *start_e, out, vert_o = first(0, near, far, *start_o)
-    inner0 = lax.ppermute(out, "blk", [(b, b ^ 1) for b in range(n_blk)])
-    table = call(functools.partial(odd_near_kernel, negs, tiles), (square,) * 2, (start_e[2], in_vmem(near)))
+    near, far, *start_e, out = first(0, near, far)
+    inner0 = moved(out, 0, 1)
+    far, *table, vert_o = call(
+        functools.partial(odd_near_kernel, negs, tiles),
+        (packs[1], square, square, state),
+        (start_e[2], *map(in_vmem, (far, near, *start_o))),
+        input_output_aliases={1: 0},
+    )
+    mate = lax.ppermute(far, "blk", [(b, b ^ 1) for b in range(n_blk)])
     vert_o, out = one_pass(1, table[0], vert_o, inner0, *table)
     swap1 = moved(vert_o, 1, -1, True)
     outer1 = moved(out, 1, 2)
-    arrays = (vert_o, *map(in_vmem, (near, inner0, *start_e)))
+    arrays = (vert_o, *map(in_vmem, (near, mate, *start_e)))
     *table, vert_e = call(functools.partial(even_near_kernel, negs, tiles), (square,) * 4 + (state,), arrays)
     vert_e, out = one_pass(0, table[3], vert_e, outer0, *table[:2])
     swap0 = moved(vert_e, 0, 1, True)
-    from_even = moved(far, 0, 1)
     vert_o, out = one_pass(0, vert_e, swap1, out, *table[2:])
     outer2 = moved(out, 0, 3)
     lend = moved(vert_o, 0, 1)
-    arrays = (vert_o, in_vmem(far), in_vmem(from_even))
+    arrays = (vert_o, in_vmem(far), in_vmem(mate))
     table = call(functools.partial(odd_far_kernel, negs, tiles), (square,) * 4, arrays)
     coef2, out2 = context_pass(1, table[3], swap0, outer1, *table[:2])
     coef3, out3 = context_pass(1, coef2, lend, out2, *table[2:])
     outer3 = moved(out3, 1, 1)
-    arrays = (coef3, *map(in_vmem, (from_even, swap0, outer1, coef2, lend, out2, coef3)))
+    arrays = (coef3, *map(in_vmem, (mate, swap0, outer1, coef2, lend, out2, coef3)))
     *table, vert_e, vert_o = call(functools.partial(last_kernel, negs, tiles), (square, square, state, state), arrays)
     vert_e, out = one_pass(1, table[1], vert_e, outer2, *table)
     back = moved(vert_e, 1, -1)

time: 52.9 us -> 48.1 us (0.909)
  waiting for transfers between devices: 29.8 us -> 24.8 us
    ppermute x9, waiting for transfers between devices: 29.8 us -> 24.8 us  [moved(): return lax.ppermute(value, ('grp', 'blk'), pairs)]
  transfers between devices with their start and end apart: 10 -> 10, of which waited for: 5 -> 4; matrix products, arithmetic and copies ran while one was open for 0% -> 0% of each run, Pallas kernels for 9% -> 10%
where the time goes in v6:
time: 48.1 us; the launch traced here: 47.7 us
  waiting for transfers between devices  24.8 us (52%)
  starting transfers between devices  14.2 us (30%)
  Pallas kernels  7.82 us (16%)
  between operations  0.83 us (2%)
    ppermute x9, waiting for transfers between devices, moved(): return lax.ppermute(value, ('grp', 'blk'), pairs)  24.8 us
    ppermute x9, starting transfers between devices, moved(): return lax.ppermute(value, ('grp', 'blk'), pairs)  11.7 us
    pallas_call x12, Pallas kernels, call(): pl.pallas_call(kernel, out_shape=tuple(outs), in_specs=in_specs or [ANY_S...  6.26 us
    ppermute x1, starting transfers between devices, on_device(): mate = lax.ppermute(far, 'blk', [(b, b ^ 1) for b in range(n_blk)])  2.5 us
    pallas_call x3, Pallas kernels, store(): pl.pallas_call(functools.partial(store_kernel, core, count), out_shape=(p...  1.56 us
  transfers between devices with their start and end apart: 10, of which 4 were waited for; matrix products, arithmetic and copies ran while one was open for 0% of the time, Pallas kernels for 10%

profile of v6, /device:TPU:6, one launch (start us, length us, event | category | flops | bytes accessed | tf_op | source)
XLA Modules:
  0.0 47.7 jit_solution(18444379056228349793)
XLA Ops:
  0.6 0.1 shard_map.68
  0.7 2.4 %shard_map.69 = (s32[392,384]{1,0:T(8,128)S(1)}, s32[784,384]{1,0:T(8,128)S(1)}, f32[384,256]{1,0:T(8,128)S(1)}, f32[384,256]{1,0:T(8,128)S(1)}, f32[384,384]{1,0:T(8,128)S(1)}, /*index=5*/f32[384,256]{1,0:T(8,128)S(1)}) custom-call(f32[384,256]{1,0:T(8,128)} %vert_hbm.3, f32[384,256]{1,0:T(8,128)} %ctx_hbm.3, ...), custom_call_target="tpu_custom_call", output_to_operand_aliasing={{0}: (5, {}), {1}: (6, {})} | custom-call | tf_op jit(solution)/shard_map/pallas_call | solution.py:240
  3.2 2.5 %collective-permute-start.1 = (s32[784,384]{1,0:T(8,128)S(1)}, s32[784,384]{1,0:T(8,128)S(1)}, u32[]{:S(2)}, u32[]{:S(2)}) collective-permute-start(s32[784,384]{1,0:T(8,128)S(1)} %get-tuple-element.58.own), channel_id=1, source_target_pairs={{0,1},{1,0},{2,3},{3,2},{4,5},{5,4},{6,7},{7,6},{8,9},{9,8},{10,11... | collective-permute-start | bytes 3612680 | tf_op jit(solution)/shard_map/ppermute | solution.py:298
  5.7 1.9 %collective-permute-start = (f32[384,256]{1,0:T(8,128)S(1)}, f32[384,256]{1,0:T(8,128)S(1)}, u32[]{:S(2)}, u32[]{:S(2)}) collective-permute-start(f32[384,256]{1,0:T(8,128)S(1)} %get-tuple-element.55), channel_id=1, source_target_pairs={{0,1},{2,3},{4,5},{6,7},{8,9},{10,11},{12,13},{14,15},{16,17},{18,... | collective-permute-start | bytes 1179656 | tf_op jit(solution)/shard_map/ppermute | solution.py:274
  7.6 1.3 %collective-permute-start.2 = (f32[384,256]{1,0:T(8,128)S(1)}, f32[384,256]{1,0:T(8,128)S(1)}, u32[]{:S(2)}, u32[]{:S(2)}) collective-permute-start(f32[384,256]{1,0:T(8,128)S(1)} %get-tuple-element.63), channel_id=1, source_target_pairs={{1,2},{3,4},{5,6},{7,8},{9,10},{11,12},{13,14},{15,16},{17,18},{19... | collective-permute-start | bytes 1179656 | tf_op jit(solution)/shard_map/ppermute | solution.py:274
  8.9 0.0 collective-permute-done.ctx_ref
  8.9 1.3 %collective-permute-start.3 = (f32[384,256]{1,0:T(8,128)S(1)}, f32[384,256]{1,0:T(8,128)S(1)}, u32[]{:S(2)}, u32[]{:S(2)}) collective-permute-start(f32[384,256]{1,0:T(8,128)S(1)} %get-tuple-element.57.after), channel_id=1, source_target_pairs={{1,64},{3,66},{5,68},{7,70},{9,72},{11,74},{13,76},{15,78},{17,80}... | collective-permute-start | bytes 1179656 | tf_op jit(solution)/shard_map/ppermute | solution.py:274
  10.2 0.7 %collective-permute-start.5 = (f32[384,256]{1,0:T(8,128)S(1)}, f32[384,256]{1,0:T(8,128)S(1)}, u32[]{:S(2)}, u32[]{:S(2)}) collective-permute-start(f32[384,256]{1,0:T(8,128)S(1)} %get-tuple-element.71), channel_id=1, source_target_pairs={{1,3},{3,5},{5,7},{7,9},{9,11},{11,13},{13,15},{15,17},{17,19},{19... | collective-permute-start | bytes 1179656 | tf_op jit(solution)/shard_map/ppermute | solution.py:274
  10.9 0.0 collective-permute-done.1.mate
  10.9 1.4 %shard_map.72 = (f32[384,384]{1,0:T(8,128)S(1)}, f32[384,384]{1,0:T(8,128)S(1)}, f32[384,384]{1,0:T(8,128)S(1)}, f32[384,384]{1,0:T(8,128)S(1)}, f32[384,256]{1,0:T(8,128)S(1)}) custom-call(f32[384,256]{1,0:T(8,128)S(1)} %get-tuple-element.57.after, s32[392,384]{1,0:T(8,128)S(1)} %get-tuple-element.49.near, s32[784,384]{1,0:T(8,128)S(1)} %collective-permute-done.1.mate, ...), custom_call_target="tpu_custom_call" | custom-call | tf_op jit(solution)/shard_map/pallas_call | solution.py:240
  12.3 13.1 %collective-permute-done.2.ctx_ref = f32[384,256]{1,0:T(8,128)S(1)} collective-permute-done((f32[384,256]{1,0:T(8,128)S(1)}, f32[384,256]{1,0:T(8,128)S(1)}, u32[]{:S(2)}, u32[]{:S(2)}) %collective-permute-start.2) | collective-permute-done | bytes 393248 | tf_op jit(solution)/shard_map/ppermute | solution.py:274
  25.4 1.2 %shard_map.73 = (f32[384,256]{1,0:T(8,128)S(1)}, f32[384,256]{1,0:T(8,128)S(1)}) custom-call(f32[384,384]{1,0:T(8,128)S(1)} %get-tuple-element.61.after.slope_ref, f32[384,256]{1,0:T(8,128)S(1)} %get-tuple-element.62.vert_ref, f32[384,256]{1,0:T(8,128)S(1)} %collective-permute-done.2.ctx_ref, f32[384,384]{1,0:T(8,128)S(1)} %get-tuple-element.64.base_ref, ...), custom_call_target="tpu_custom_call" | custom-call | tf_op jit(solution)/shard_map/pallas_call | solution.py:240
  26.6 1.3 %collective-permute-start.4 = (f32[384,256]{1,0:T(8,128)S(1)}, f32[384,256]{1,0:T(8,128)S(1)}, u32[]{:S(2)}, u32[]{:S(2)}) collective-permute-start(f32[384,256]{1,0:T(8,128)S(1)} %get-tuple-element.66.after), channel_id=1, source_target_pairs={{0,65},{2,67},{4,69},{6,71},{8,73},{10,75},{12,77},{14,79},{16,81}... | collective-permute-start | bytes 1179656 | tf_op jit(solution)/shard_map/ppermute | solution.py:274
  27.9 0.0 collective-permute-done.3.vert_ref
  27.9 1.2 %shard_map.74 = (f32[384,256]{1,0:T(8,128)S(1)}, f32[384,256]{1,0:T(8,128)S(1)}) custom-call(f32[384,256]{1,0:T(8,128)S(1)} %get-tuple-element.66.after, f32[384,256]{1,0:T(8,128)S(1)} %collective-permute-done.3.vert_ref, f32[384,256]{1,0:T(8,128)S(1)} %get-tuple-element.67.ctx_ref, f32[384,384]{1,0:T(8,128)S(1)} %get-tuple-element.68.base_ref, ...), custom_call_target="tpu_custom_call" | custom-call | tf_op jit(solution)/shard_map/pallas_call | solution.py:240
  29.1 1.3 %collective-permute-start.6 = (f32[384,256]{1,0:T(8,128)S(1)}, f32[384,256]{1,0:T(8,128)S(1)}, u32[]{:S(2)}, u32[]{:S(2)}) collective-permute-start(f32[384,256]{1,0:T(8,128)S(1)} %get-tuple-element.69.after), channel_id=1, source_target_pairs={{0,1},{2,3},{4,5},{6,7},{8,9},{10,11},{12,13},{14,15},{16,17},{18,... | collective-permute-start | bytes 1179656 | tf_op jit(solution)/shard_map/ppermute | solution.py:274
  30.4 1.3 %collective-permute-start.7 = (f32[384,256]{1,0:T(8,128)S(1)}, f32[384,256]{1,0:T(8,128)S(1)}, u32[]{:S(2)}, u32[]{:S(2)}) collective-permute-start(f32[384,256]{1,0:T(8,128)S(1)} %get-tuple-element.80), channel_id=1, source_target_pairs={{0,3},{2,5},{4,7},{6,9},{8,11},{10,13},{12,15},{14,17},{16,19},{18... | collective-permute-start | bytes 1179656 | tf_op jit(solution)/shard_map/ppermute | solution.py:274
  31.8 0.0 collective-permute-done.5.ctx_ref.ctx2
  31.8 1.4 %collective-permute-done.4.vert_ref.vert2 = f32[384,256]{1,0:T(8,128)S(1)} collective-permute-done((f32[384,256]{1,0:T(8,128)S(1)}, f32[384,256]{1,0:T(8,128)S(1)}, u32[]{:S(2)}, u32[]{:S(2)}) %collective-permute-start.4) | collective-permute-done | bytes 393248 | tf_op jit(solution)/shard_map/ppermute | solution.py:274
  33.1 0.0 collective-permute-done.6.vert_ref.vert3
  33.1 1.3 %collective-permute-start.9 = (f32[384,256]{1,0:T(8,128)S(1)}, f32[384,256]{1,0:T(8,128)S(1)}, u32[]{:S(2)}, u32[]{:S(2)}) collective-permute-start(f32[384,256]{1,0:T(8,128)S(1)} %get-tuple-element.86), channel_id=1, source_target_pairs={{1,2},{3,4},{5,6},{7,8},{9,10},{11,12},{13,14},{15,16},{17,18},{19... | collective-permute-start | bytes 1179656 | tf_op jit(solution)/shard_map/ppermute | solution.py:274
  34.5 2.5 %collective-permute-done.7.ctx_ref = f32[384,256]{1,0:T(8,128)S(1)} collective-permute-done((f32[384,256]{1,0:T(8,128)S(1)}, f32[384,256]{1,0:T(8,128)S(1)}, u32[]{:S(2)}, u32[]{:S(2)}) %collective-permute-start.7) | collective-permute-done | bytes 393248 | tf_op jit(solution)/shard_map/ppermute | solution.py:274
  37.0 1.3 %collective-permute-start.8 = (f32[384,256]{1,0:T(8,128)S(1)}, f32[384,256]{1,0:T(8,128)S(1)}, u32[]{:S(2)}, u32[]{:S(2)}) collective-permute-start(f32[384,256]{1,0:T(8,128)S(1)} %get-tuple-element.82), channel_id=1, source_target_pairs={{1,0},{3,2},{5,4},{7,6},{9,8},{11,10},{13,12},{15,14},{17,16},{19,... | collective-permute-start | bytes 1179656 | tf_op jit(solution)/shard_map/ppermute | solution.py:274
  38.3 7.8 %collective-permute-done.9.refs_0_ = f32[384,256]{1,0:T(8,128)S(1)} collective-permute-done((f32[384,256]{1,0:T(8,128)S(1)}, f32[384,256]{1,0:T(8,128)S(1)}, u32[]{:S(2)}, u32[]{:S(2)}) %collective-permute-start.9) | collective-permute-done | bytes 393248 | tf_op jit(solution)/shard_map/ppermute | solution.py:274
  46.1 0.8 %shard_map.82 = f32[384,256]{1,0:T(8,128)} custom-call(f32[384,256]{1,0:T(8,128)S(1)} %collective-permute-done.9.refs_0_, f32[384,256]{1,0:T(8,128)} %get-tuple-element.87.refs_1_), custom_call_target="tpu_custom_call", output_to_operand_aliasing={{}: (1, {})} | custom-call | tf_op jit(solution)/shard_map/pallas_call | solution.py:278
  46.9 0.0 collective-permute-done.8.refs_0_
  46.9 0.8 %shard_map.81 = f32[384,256]{1,0:T(8,128)} custom-call(f32[384,256]{1,0:T(8,128)S(1)} %collective-permute-done.8.refs_0_, f32[384,256]{1,0:T(8,128)} %get-tuple-element.85.refs_1_), custom_call_target="tpu_custom_call", output_to_operand_aliasing={{}: (1, {})} | custom-call | tf_op jit(solution)/shard_map/pallas_call | solution.py:278
  (8 shorter events, 0.1 us)
Async XLA Ops:
  3.2 7.8 %collective-permute-start.1 = (s32[784,384]{1,0:T(8,128)S(1)}, s32[784,384]{1,0:T(8,128)S(1)}, u32[]{:S(2)}, u32[]{:S(2)}) collective-permute-start(s32[784,384]{1,0:T(8,128)S(1)} %get-tuple-element.58.own), channel_id=1, source_target_pairs={{0,1},{1,0},{2,3},{3,2},{4,5},{5,4},{6,7},{7,6},{8,9},{9,8},{10,11... | collective-permute-start | bytes 3612680 | tf_op jit(solution)/shard_map/ppermute | solution.py:298
  5.7 3.3 %collective-permute-start = (f32[384,256]{1,0:T(8,128)S(1)}, f32[384,256]{1,0:T(8,128)S(1)}, u32[]{:S(2)}, u32[]{:S(2)}) collective-permute-start(f32[384,256]{1,0:T(8,128)S(1)} %get-tuple-element.55), channel_id=1, source_target_pairs={{0,1},{2,3},{4,5},{6,7},{8,9},{10,11},{12,13},{14,15},{16,17},{18,... | collective-permute-start | bytes 1179656 | tf_op jit(solution)/shard_map/ppermute | solution.py:274
  7.6 17.8 %collective-permute-start.2 = (f32[384,256]{1,0:T(8,128)S(1)}, f32[384,256]{1,0:T(8,128)S(1)}, u32[]{:S(2)}, u32[]{:S(2)}) collective-permute-start(f32[384,256]{1,0:T(8,128)S(1)} %get-tuple-element.63), channel_id=1, source_target_pairs={{1,2},{3,4},{5,6},{7,8},{9,10},{11,12},{13,14},{15,16},{17,18},{19... | collective-permute-start | bytes 1179656 | tf_op jit(solution)/shard_map/ppermute | solution.py:274
  8.9 18.9 %collective-permute-start.3 = (f32[384,256]{1,0:T(8,128)S(1)}, f32[384,256]{1,0:T(8,128)S(1)}, u32[]{:S(2)}, u32[]{:S(2)}) collective-permute-start(f32[384,256]{1,0:T(8,128)S(1)} %get-tuple-element.57.after), channel_id=1, source_target_pairs={{1,64},{3,66},{5,68},{7,70},{9,72},{11,74},{13,76},{15,78},{17,80}... | collective-permute-start | bytes 1179656 | tf_op jit(solution)/shard_map/ppermute | solution.py:274
  10.2 21.5 %collective-permute-start.5 = (f32[384,256]{1,0:T(8,128)S(1)}, f32[384,256]{1,0:T(8,128)S(1)}, u32[]{:S(2)}, u32[]{:S(2)}) collective-permute-start(f32[384,256]{1,0:T(8,128)S(1)} %get-tuple-element.71), channel_id=1, source_target_pairs={{1,3},{3,5},{5,7},{7,9},{9,11},{11,13},{13,15},{15,17},{17,19},{19... | collective-permute-start | bytes 1179656 | tf_op jit(solution)/shard_map/ppermute | solution.py:274
  26.6 6.6 %collective-permute-start.4 = (f32[384,256]{1,0:T(8,128)S(1)}, f32[384,256]{1,0:T(8,128)S(1)}, u32[]{:S(2)}, u32[]{:S(2)}) collective-permute-start(f32[384,256]{1,0:T(8,128)S(1)} %get-tuple-element.66.after), channel_id=1, source_target_pairs={{0,65},{2,67},{4,69},{6,71},{8,73},{10,75},{12,77},{14,79},{16,81}... | collective-permute-start | bytes 1179656 | tf_op jit(solution)/shard_map/ppermute | solution.py:274
  29.1 4.0 %collective-permute-start.6 = (f32[384,256]{1,0:T(8,128)S(1)}, f32[384,256]{1,0:T(8,128)S(1)}, u32[]{:S(2)}, u32[]{:S(2)}) collective-permute-start(f32[384,256]{1,0:T(8,128)S(1)} %get-tuple-element.69.after), channel_id=1, source_target_pairs={{0,1},{2,3},{4,5},{6,7},{8,9},{10,11},{12,13},{14,15},{16,17},{18,... | collective-permute-start | bytes 1179656 | tf_op jit(solution)/shard_map/ppermute | solution.py:274
  30.4 6.6 %collective-permute-start.7 = (f32[384,256]{1,0:T(8,128)S(1)}, f32[384,256]{1,0:T(8,128)S(1)}, u32[]{:S(2)}, u32[]{:S(2)}) collective-permute-start(f32[384,256]{1,0:T(8,128)S(1)} %get-tuple-element.80), channel_id=1, source_target_pairs={{0,3},{2,5},{4,7},{6,9},{8,11},{10,13},{12,15},{14,17},{16,19},{18... | collective-permute-start | bytes 1179656 | tf_op jit(solution)/shard_map/ppermute | solution.py:274
  33.1 13.0 %collective-permute-start.9 = (f32[384,256]{1,0:T(8,128)S(1)}, f32[384,256]{1,0:T(8,128)S(1)}, u32[]{:S(2)}, u32[]{:S(2)}) collective-permute-start(f32[384,256]{1,0:T(8,128)S(1)} %get-tuple-element.86), channel_id=1, source_target_pairs={{1,2},{3,4},{5,6},{7,8},{9,10},{11,12},{13,14},{15,16},{17,18},{19... | collective-permute-start | bytes 1179656 | tf_op jit(solution)/shard_map/ppermute | solution.py:274
  37.0 9.9 %collective-permute-start.8 = (f32[384,256]{1,0:T(8,128)S(1)}, f32[384,256]{1,0:T(8,128)S(1)}, u32[]{:S(2)}, u32[]{:S(2)}) collective-permute-start(f32[384,256]{1,0:T(8,128)S(1)} %get-tuple-element.82), channel_id=1, source_target_pairs={{1,0},{3,2},{5,4},{7,6},{9,8},{11,10},{13,12},{15,14},{17,16},{19,... | collective-permute-start | bytes 1179656 | tf_op jit(solution)/shard_map/ppermute | solution.py:274

commit v7 on v6

--- a/solution.py
+++ b/solution.py
@@ -166,19 +166,24 @@
             copy.wait()
 
 
-def odd_near_kernel(negs, tiles, after, far_in, near, vert, ctx, coef, far, base_ref, slope_ref, new_vert_ref):
+def odd_near_kernel(negs, tiles, after, near, vert, ctx, coef, base_ref, slope_ref, new_vert_ref):
     @pl.when(on_core(1))
     def _():
         tables_from(near, 0, 1, negs, tiles, base_ref, slope_ref)
         new_vert_ref[...] = vertex_part(vert[...], ctx[...], coef[...])
 
 
-def even_near_kernel(negs, tiles, after, near, mate, vert, ctx, coef, base1, slope1, base2, slope2, new_vert_ref):
+def even_near_kernel(negs, tiles, after, far_in, near, vert, ctx, coef, far, base_ref, slope_ref, new_vert_ref):
     @pl.when(on_core(0))
     def _():
-        tables_from(near, 0, 1, negs, tiles, base1, slope1)
-        tables_from(mate, 0, 2, negs, tiles, base2, slope2)
+        tables_from(near, 0, 1, negs, tiles, base_ref, slope_ref)
         new_vert_ref[...] = vertex_part(vert[...], ctx[...], coef[...])
+
+
+def even_far_kernel(negs, tiles, after, mate, base_ref, slope_ref):
+    @pl.when(on_core(0))
+    def _():
+        tables_from(mate, 0, 2, negs, tiles, base_ref, slope_ref)
 
 
 def odd_far_kernel(negs, tiles, after, own, mate, base2, slope2, own_base3, own_slope3):
@@ -289,21 +294,25 @@
     outer0 = moved(out, 1, 1)
     near, far, *start_e, out = first(0, near, far)
     inner0 = moved(out, 0, 1)
-    far, *table, vert_o = call(
+    *table, vert_o = call(
         functools.partial(odd_near_kernel, negs, tiles),
+        (square, square, state),
+        (start_e[2], *map(in_vmem, (near, *start_o))),
+    )
+    vert_o, out = one_pass(1, table[0], vert_o, inner0, *table)
+    swap1 = moved(vert_o, 1, -1, True)
+    outer1 = moved(out, 1, 2)
+    far, *table, vert_e = call(
+        functools.partial(even_near_kernel, negs, tiles),
         (packs[1], square, square, state),
-        (start_e[2], *map(in_vmem, (far, near, *start_o))),
+        (vert_o, *map(in_vmem, (far, near, *start_e))),
         input_output_aliases={1: 0},
     )
     mate = lax.ppermute(far, "blk", [(b, b ^ 1) for b in range(n_blk)])
-    vert_o, out = one_pass(1, table[0], vert_o, inner0, *table)
-    swap1 = moved(vert_o, 1, -1, True)
-    outer1 = moved(out, 1, 2)
-    arrays = (vert_o, *map(in_vmem, (near, mate, *start_e)))
-    *table, vert_e = call(functools.partial(even_near_kernel, negs, tiles), (square,) * 4 + (state,), arrays)
-    vert_e, out = one_pass(0, table[3], vert_e, outer0, *table[:2])
+    vert_e, out = one_pass(0, table[0], vert_e, outer0, *table)
     swap0 = moved(vert_e, 0, 1, True)
-    vert_o, out = one_pass(0, vert_e, swap1, out, *table[2:])
+    table = call(functools.partial(even_far_kernel, negs, tiles), (square,) * 2, (vert_e, in_vmem(mate)))
+    vert_o, out = one_pass(0, table[0], swap1, out, *table)
     outer2 = moved(out, 0, 3)
     lend = moved(vert_o, 0, 1)
     arrays = (vert_o, in_vmem(far), in_vmem(mate))

time: 48.1 us -> 56.4 us (1.17)
  waiting for transfers between devices: 24.8 us -> 33.1 us
    ppermute x9, waiting for transfers between devices: 24.8 us -> 33.1 us  [moved(): return lax.ppermute(value, ('grp', 'blk'), pairs)]
    pallas_call x12 -> x13, Pallas kernels: 6.26 us -> 6.36 us  [call(): pl.pallas_call(kernel, out_shape=tuple(outs), in_specs=in_specs or [ANY_S...]
  transfers between devices with their start and end apart: 10 -> 10, of which waited for: 4 -> 5; matrix products, arithmetic and copies ran while one was open for 0% -> 0% of each run, Pallas kernels for 10% -> 7%
where the time goes in v7:
time: 56.4 us; the launch traced here: 56.1 us
  waiting for transfers between devices  33.1 us (59%)
  starting transfers between devices  14.2 us (25%)
  Pallas kernels  7.9 us (14%)
  between operations  0.85 us (2%)
    ppermute x9, waiting for transfers between devices, moved(): return lax.ppermute(value, ('grp', 'blk'), pairs)  33.1 us
    ppermute x9, starting transfers between devices, moved(): return lax.ppermute(value, ('grp', 'blk'), pairs)  11.5 us
    pallas_call x13, Pallas kernels, call(): pl.pallas_call(kernel, out_shape=tuple(outs), in_specs=in_specs or [ANY_S...  6.36 us
    ppermute x1, starting transfers between devices, on_device(): mate = lax.ppermute(far, 'blk', [(b, b ^ 1) for b in range(n_blk)])  2.7 us
    pallas_call x3, Pallas kernels, store(): pl.pallas_call(functools.partial(store_kernel, core, count), out_shape=(p...  1.54 us
  transfers between devices with their start and end apart: 10, of which 5 were waited for; matrix products, arithmetic and copies ran while one was open for 0% of the time, Pallas kernels for 7%

profile of v7, /device:TPU:6, one launch (start us, length us, event | category | flops | bytes accessed | tf_op | source)
XLA Modules:
  0.0 56.1 jit_solution(18387752568394557679)
XLA Ops:
  0.6 0.1 shard_map.68
  0.7 2.4 %shard_map.69 = (s32[392,384]{1,0:T(8,128)S(1)}, s32[784,384]{1,0:T(8,128)S(1)}, f32[384,256]{1,0:T(8,128)S(1)}, f32[384,256]{1,0:T(8,128)S(1)}, f32[384,384]{1,0:T(8,128)S(1)}, /*index=5*/f32[384,256]{1,0:T(8,128)S(1)}) custom-call(f32[384,256]{1,0:T(8,128)} %vert_hbm.3, f32[384,256]{1,0:T(8,128)} %ctx_hbm.3, ...), custom_call_target="tpu_custom_call", output_to_operand_aliasing={{0}: (5, {}), {1}: (6, {})} | custom-call | tf_op jit(solution)/shard_map/pallas_call | solution.py:245
  3.1 1.8 %collective-permute-start = (f32[384,256]{1,0:T(8,128)S(1)}, f32[384,256]{1,0:T(8,128)S(1)}, u32[]{:S(2)}, u32[]{:S(2)}) collective-permute-start(f32[384,256]{1,0:T(8,128)S(1)} %get-tuple-element.54), channel_id=1, source_target_pairs={{0,1},{2,3},{4,5},{6,7},{8,9},{10,11},{12,13},{14,15},{16,17},{18,... | collective-permute-start | bytes 1179656 | tf_op jit(solution)/shard_map/ppermute | solution.py:279
  4.9 1.3 %collective-permute-done.ctx_ref = f32[384,256]{1,0:T(8,128)S(1)} collective-permute-done((f32[384,256]{1,0:T(8,128)S(1)}, f32[384,256]{1,0:T(8,128)S(1)}, u32[]{:S(2)}, u32[]{:S(2)}) %collective-permute-start) | collective-permute-done | bytes 393248 | tf_op jit(solution)/shard_map/ppermute | solution.py:279
  6.2 0.8 %shard_map.72 = (s32[784,384]{1,0:T(8,128)S(1)}, f32[384,384]{1,0:T(8,128)S(1)}, f32[384,384]{1,0:T(8,128)S(1)}, f32[384,256]{1,0:T(8,128)S(1)}) custom-call(f32[384,256]{1,0:T(8,128)S(1)} %get-tuple-element.56.after, s32[784,384]{1,0:T(8,128)S(1)} %get-tuple-element.57.far_in, ...), custom_call_target="tpu_custom_call", output_to_operand_aliasing={{0}: (1, {})} | custom-call | tf_op jit(solution)/shard_map/pallas_call | solution.py:245
  7.0 2.7 %collective-permute-start.2 = (s32[784,384]{1,0:T(8,128)S(1)}, s32[784,384]{1,0:T(8,128)S(1)}, u32[]{:S(2)}, u32[]{:S(2)}) collective-permute-start(s32[784,384]{1,0:T(8,128)S(1)} %get-tuple-element.65.own), channel_id=1, source_target_pairs={{0,1},{1,0},{2,3},{3,2},{4,5},{5,4},{6,7},{7,6},{8,9},{9,8},{10,11... | collective-permute-start | bytes 3612680 | tf_op jit(solution)/shard_map/ppermute | solution.py:311
  9.7 1.3 %collective-permute-start.1 = (f32[384,256]{1,0:T(8,128)S(1)}, f32[384,256]{1,0:T(8,128)S(1)}, u32[]{:S(2)}, u32[]{:S(2)}) collective-permute-start(f32[384,256]{1,0:T(8,128)S(1)} %get-tuple-element.62), channel_id=1, source_target_pairs={{1,2},{3,4},{5,6},{7,8},{9,10},{11,12},{13,14},{15,16},{17,18},{19... | collective-permute-start | bytes 1179656 | tf_op jit(solution)/shard_map/ppermute | solution.py:279
  11.0 1.3 %collective-permute-start.3 = (f32[384,256]{1,0:T(8,128)S(1)}, f32[384,256]{1,0:T(8,128)S(1)}, u32[]{:S(2)}, u32[]{:S(2)}) collective-permute-start(f32[384,256]{1,0:T(8,128)S(1)} %get-tuple-element.56.after), channel_id=1, source_target_pairs={{1,64},{3,66},{5,68},{7,70},{9,72},{11,74},{13,76},{15,78},{17,80}... | collective-permute-start | bytes 1179656 | tf_op jit(solution)/shard_map/ppermute | solution.py:279
  12.3 15.8 %collective-permute-done.1.ctx_ref = f32[384,256]{1,0:T(8,128)S(1)} collective-permute-done((f32[384,256]{1,0:T(8,128)S(1)}, f32[384,256]{1,0:T(8,128)S(1)}, u32[]{:S(2)}, u32[]{:S(2)}) %collective-permute-start.1) | collective-permute-done | bytes 393248 | tf_op jit(solution)/shard_map/ppermute | solution.py:279
  28.1 1.2 %shard_map.73 = (f32[384,256]{1,0:T(8,128)S(1)}, f32[384,256]{1,0:T(8,128)S(1)}) custom-call(f32[384,384]{1,0:T(8,128)S(1)} %get-tuple-element.60.after.base_ref, f32[384,256]{1,0:T(8,128)S(1)} %get-tuple-element.61.vert_ref, f32[384,256]{1,0:T(8,128)S(1)} %collective-permute-done.1.ctx_ref, f32[384,384]{1,0:T(8,128)S(1)} %get-tuple-element.60.after.base_ref, ...), custom_call_target="tpu_custom_call" | custom-call | tf_op jit(solution)/shard_map/pallas_call | solution.py:245
  29.3 1.3 %collective-permute-start.4 = (f32[384,256]{1,0:T(8,128)S(1)}, f32[384,256]{1,0:T(8,128)S(1)}, u32[]{:S(2)}, u32[]{:S(2)}) collective-permute-start(f32[384,256]{1,0:T(8,128)S(1)} %get-tuple-element.64.after), channel_id=1, source_target_pairs={{0,65},{2,67},{4,69},{6,71},{8,73},{10,75},{12,77},{14,79},{16,81}... | collective-permute-start | bytes 1179656 | tf_op jit(solution)/shard_map/ppermute | solution.py:279
  30.6 0.7 %collective-permute-start.5 = (f32[384,256]{1,0:T(8,128)S(1)}, f32[384,256]{1,0:T(8,128)S(1)}, u32[]{:S(2)}, u32[]{:S(2)}) collective-permute-start(f32[384,256]{1,0:T(8,128)S(1)} %get-tuple-element.71), channel_id=1, source_target_pairs={{1,3},{3,5},{5,7},{7,9},{9,11},{11,13},{13,15},{15,17},{17,19},{19... | collective-permute-start | bytes 1179656 | tf_op jit(solution)/shard_map/ppermute | solution.py:279
  31.3 0.0 collective-permute-done.2.mate
  31.3 0.7 %shard_map.74 = (f32[384,384]{1,0:T(8,128)S(1)}, f32[384,384]{1,0:T(8,128)S(1)}) custom-call(f32[384,256]{1,0:T(8,128)S(1)} %get-tuple-element.64.after, s32[784,384]{1,0:T(8,128)S(1)} %collective-permute-done.2.mate), custom_call_target="tpu_custom_call" | custom-call | tf_op jit(solution)/shard_map/pallas_call | solution.py:245
  32.0 0.0 collective-permute-done.3.vert_ref
  32.0 1.2 %shard_map.75 = (f32[384,256]{1,0:T(8,128)S(1)}, f32[384,256]{1,0:T(8,128)S(1)}) custom-call(f32[384,384]{1,0:T(8,128)S(1)} %get-tuple-element.66.after.base_ref, f32[384,256]{1,0:T(8,128)S(1)} %collective-permute-done.3.vert_ref, f32[384,256]{1,0:T(8,128)S(1)} %get-tuple-element.67.ctx_ref, f32[384,384]{1,0:T(8,128)S(1)} %get-tuple-element.66.after.base_ref, ...), custom_call_target="tpu_custom_call" | custom-call | tf_op jit(solution)/shard_map/pallas_call | solution.py:245
  33.2 1.3 %collective-permute-start.6 = (f32[384,256]{1,0:T(8,128)S(1)}, f32[384,256]{1,0:T(8,128)S(1)}, u32[]{:S(2)}, u32[]{:S(2)}) collective-permute-start(f32[384,256]{1,0:T(8,128)S(1)} %get-tuple-element.69.after), channel_id=1, source_target_pairs={{0,1},{2,3},{4,5},{6,7},{8,9},{10,11},{12,13},{14,15},{16,17},{18,... | collective-permute-start | bytes 1179656 | tf_op jit(solution)/shard_map/ppermute | solution.py:279
  34.5 1.3 %collective-permute-start.7 = (f32[384,256]{1,0:T(8,128)S(1)}, f32[384,256]{1,0:T(8,128)S(1)}, u32[]{:S(2)}, u32[]{:S(2)}) collective-permute-start(f32[384,256]{1,0:T(8,128)S(1)} %get-tuple-element.80), channel_id=1, source_target_pairs={{0,3},{2,5},{4,7},{6,9},{8,11},{10,13},{12,15},{14,17},{16,19},{18... | collective-permute-start | bytes 1179656 | tf_op jit(solution)/shard_map/ppermute | solution.py:279
  35.9 0.0 collective-permute-done.4.vert_ref.vert2
  35.9 0.0 collective-permute-done.5.ctx_ref.ctx2
  35.9 0.0 collective-permute-done.6.vert_ref.vert3
  36.0 5.1 %collective-permute-done.7.ctx_ref = f32[384,256]{1,0:T(8,128)S(1)} collective-permute-done((f32[384,256]{1,0:T(8,128)S(1)}, f32[384,256]{1,0:T(8,128)S(1)}, u32[]{:S(2)}, u32[]{:S(2)}) %collective-permute-start.7) | collective-permute-done | bytes 393248 | tf_op jit(solution)/shard_map/ppermute | solution.py:279
  41.1 1.3 %collective-permute-start.8 = (f32[384,256]{1,0:T(8,128)S(1)}, f32[384,256]{1,0:T(8,128)S(1)}, u32[]{:S(2)}, u32[]{:S(2)}) collective-permute-start(f32[384,256]{1,0:T(8,128)S(1)} %get-tuple-element.82), channel_id=1, source_target_pairs={{1,0},{3,2},{5,4},{7,6},{9,8},{11,10},{13,12},{15,14},{17,16},{19,... | collective-permute-start | bytes 1179656 | tf_op jit(solution)/shard_map/ppermute | solution.py:279
  42.4 1.3 %collective-permute-start.9 = (f32[384,256]{1,0:T(8,128)S(1)}, f32[384,256]{1,0:T(8,128)S(1)}, u32[]{:S(2)}, u32[]{:S(2)}) collective-permute-start(f32[384,256]{1,0:T(8,128)S(1)} %get-tuple-element.86), channel_id=1, source_target_pairs={{1,2},{3,4},{5,6},{7,8},{9,10},{11,12},{13,14},{15,16},{17,18},{19... | collective-permute-start | bytes 1179656 | tf_op jit(solution)/shard_map/ppermute | solution.py:279
  43.7 4.1 %collective-permute-done.8.refs_0_ = f32[384,256]{1,0:T(8,128)S(1)} collective-permute-done((f32[384,256]{1,0:T(8,128)S(1)}, f32[384,256]{1,0:T(8,128)S(1)}, u32[]{:S(2)}, u32[]{:S(2)}) %collective-permute-start.8) | collective-permute-done | bytes 393248 | tf_op jit(solution)/shard_map/ppermute | solution.py:279
  47.8 0.8 %shard_map.82 = f32[384,256]{1,0:T(8,128)} custom-call(f32[384,256]{1,0:T(8,128)S(1)} %collective-permute-done.8.refs_0_, f32[384,256]{1,0:T(8,128)} %get-tuple-element.85.refs_1_), custom_call_target="tpu_custom_call", output_to_operand_aliasing={{}: (1, {})} | custom-call | tf_op jit(solution)/shard_map/pallas_call | solution.py:283
  48.5 6.8 %collective-permute-done.9.refs_0_ = f32[384,256]{1,0:T(8,128)S(1)} collective-permute-done((f32[384,256]{1,0:T(8,128)S(1)}, f32[384,256]{1,0:T(8,128)S(1)}, u32[]{:S(2)}, u32[]{:S(2)}) %collective-permute-start.9) | collective-permute-done | bytes 393248 | tf_op jit(solution)/shard_map/ppermute | solution.py:279
  55.4 0.8 %shard_map.83 = f32[384,256]{1,0:T(8,128)} custom-call(f32[384,256]{1,0:T(8,128)S(1)} %collective-permute-done.9.refs_0_, f32[384,256]{1,0:T(8,128)} %get-tuple-element.87.refs_1_), custom_call_target="tpu_custom_call", output_to_operand_aliasing={{}: (1, {})} | custom-call | tf_op jit(solution)/shard_map/pallas_call | solution.py:283
  (8 shorter events, 0.1 us)
Async XLA Ops:
  3.1 3.1 %collective-permute-start = (f32[384,256]{1,0:T(8,128)S(1)}, f32[384,256]{1,0:T(8,128)S(1)}, u32[]{:S(2)}, u32[]{:S(2)}) collective-permute-start(f32[384,256]{1,0:T(8,128)S(1)} %get-tuple-element.54), channel_id=1, source_target_pairs={{0,1},{2,3},{4,5},{6,7},{8,9},{10,11},{12,13},{14,15},{16,17},{18,... | collective-permute-start | bytes 1179656 | tf_op jit(solution)/shard_map/ppermute | solution.py:279
  7.0 24.3 %collective-permute-start.2 = (s32[784,384]{1,0:T(8,128)S(1)}, s32[784,384]{1,0:T(8,128)S(1)}, u32[]{:S(2)}, u32[]{:S(2)}) collective-permute-start(s32[784,384]{1,0:T(8,128)S(1)} %get-tuple-element.65.own), channel_id=1, source_target_pairs={{0,1},{1,0},{2,3},{3,2},{4,5},{5,4},{6,7},{7,6},{8,9},{9,8},{10,11... | collective-permute-start | bytes 3612680 | tf_op jit(solution)/shard_map/ppermute | solution.py:311
  9.7 18.4 %collective-permute-start.1 = (f32[384,256]{1,0:T(8,128)S(1)}, f32[384,256]{1,0:T(8,128)S(1)}, u32[]{:S(2)}, u32[]{:S(2)}) collective-permute-start(f32[384,256]{1,0:T(8,128)S(1)} %get-tuple-element.62), channel_id=1, source_target_pairs={{1,2},{3,4},{5,6},{7,8},{9,10},{11,12},{13,14},{15,16},{17,18},{19... | collective-permute-start | bytes 1179656 | tf_op jit(solution)/shard_map/ppermute | solution.py:279
  11.0 21.0 %collective-permute-start.3 = (f32[384,256]{1,0:T(8,128)S(1)}, f32[384,256]{1,0:T(8,128)S(1)}, u32[]{:S(2)}, u32[]{:S(2)}) collective-permute-start(f32[384,256]{1,0:T(8,128)S(1)} %get-tuple-element.56.after), channel_id=1, source_target_pairs={{1,64},{3,66},{5,68},{7,70},{9,72},{11,74},{13,76},{15,78},{17,80}... | collective-permute-start | bytes 1179656 | tf_op jit(solution)/shard_map/ppermute | solution.py:279
  29.3 6.6 %collective-permute-start.4 = (f32[384,256]{1,0:T(8,128)S(1)}, f32[384,256]{1,0:T(8,128)S(1)}, u32[]{:S(2)}, u32[]{:S(2)}) collective-permute-start(f32[384,256]{1,0:T(8,128)S(1)} %get-tuple-element.64.after), channel_id=1, source_target_pairs={{0,65},{2,67},{4,69},{6,71},{8,73},{10,75},{12,77},{14,79},{16,81}... | collective-permute-start | bytes 1179656 | tf_op jit(solution)/shard_map/ppermute | solution.py:279
  30.6 5.3 %collective-permute-start.5 = (f32[384,256]{1,0:T(8,128)S(1)}, f32[384,256]{1,0:T(8,128)S(1)}, u32[]{:S(2)}, u32[]{:S(2)}) collective-permute-start(f32[384,256]{1,0:T(8,128)S(1)} %get-tuple-element.71), channel_id=1, source_target_pairs={{1,3},{3,5},{5,7},{7,9},{9,11},{11,13},{13,15},{15,17},{17,19},{19... | collective-permute-start | bytes 1179656 | tf_op jit(solution)/shard_map/ppermute | solution.py:279
  33.2 2.7 %collective-permute-start.6 = (f32[384,256]{1,0:T(8,128)S(1)}, f32[384,256]{1,0:T(8,128)S(1)}, u32[]{:S(2)}, u32[]{:S(2)}) collective-permute-start(f32[384,256]{1,0:T(8,128)S(1)} %get-tuple-element.69.after), channel_id=1, source_target_pairs={{0,1},{2,3},{4,5},{6,7},{8,9},{10,11},{12,13},{14,15},{16,17},{18,... | collective-permute-start | bytes 1179656 | tf_op jit(solution)/shard_map/ppermute | solution.py:279
  34.5 6.6 %collective-permute-start.7 = (f32[384,256]{1,0:T(8,128)S(1)}, f32[384,256]{1,0:T(8,128)S(1)}, u32[]{:S(2)}, u32[]{:S(2)}) collective-permute-start(f32[384,256]{1,0:T(8,128)S(1)} %get-tuple-element.80), channel_id=1, source_target_pairs={{0,3},{2,5},{4,7},{6,9},{8,11},{10,13},{12,15},{14,17},{16,19},{18... | collective-permute-start | bytes 1179656 | tf_op jit(solution)/shard_map/ppermute | solution.py:279
  41.1 6.7 %collective-permute-start.8 = (f32[384,256]{1,0:T(8,128)S(1)}, f32[384,256]{1,0:T(8,128)S(1)}, u32[]{:S(2)}, u32[]{:S(2)}) collective-permute-start(f32[384,256]{1,0:T(8,128)S(1)} %get-tuple-element.82), channel_id=1, source_target_pairs={{1,0},{3,2},{5,4},{7,6},{9,8},{11,10},{13,12},{15,14},{17,16},{19,... | collective-permute-start | bytes 1179656 | tf_op jit(solution)/shard_map/ppermute | solution.py:279
  42.4 13.0 %collective-permute-start.9 = (f32[384,256]{1,0:T(8,128)S(1)}, f32[384,256]{1,0:T(8,128)S(1)}, u32[]{:S(2)}, u32[]{:S(2)}) collective-permute-start(f32[384,256]{1,0:T(8,128)S(1)} %get-tuple-element.86), channel_id=1, source_target_pairs={{1,2},{3,4},{5,6},{7,8},{9,10},{11,12},{13,14},{15,16},{17,18},{19... | collective-permute-start | bytes 1179656 | tf_op jit(solution)/shard_map/ppermute | solution.py:279

commit v8 on v7

--- a/solution.py
+++ b/solution.py
@@ -186,28 +186,30 @@
         tables_from(mate, 0, 2, negs, tiles, base_ref, slope_ref)
 
 
-def odd_far_kernel(negs, tiles, after, own, mate, base2, slope2, own_base3, own_slope3):
+def odd_far_kernel(negs, tiles, after, own, mate, base2, slope2, own_base3, own_slope3, base, slope):
     @pl.when(on_core(1))
     def _():
-        tables_from(mate, 0, 2, negs, tiles, base2, slope2)
-        tables_from(own, 1, 2, negs, tiles, own_base3, own_slope3)
+        for pack, index, base_ref, slope_ref in ((mate, 0, base2, slope2), (own, 1, own_base3, own_slope3)):
+            tables_from(pack, index, 2, negs, tiles, base, slope)
+            base_ref[...] = jnp.transpose(base[...])
+            slope_ref[...] = jnp.transpose(slope[...])
 
 
 def last_kernel(negs, tiles, after, mate, vert2, ctx2, coef2, vert3, ctx3, coef3, base_ref, slope_ref, even_vert_ref, odd_vert_ref):
     @pl.when(on_core(1))
     def _():
         tables_from(mate, 1, 2, negs, tiles, base_ref, slope_ref)
-        even_vert_ref[...] = vertex_part(vert2[...], ctx2[...], coef2[...])
-        odd_vert_ref[...] = vertex_part(vert3[...], ctx3[...], coef3[...])
+        even_vert_ref[...] = vertex_part(vert2[...], ctx2[...], jnp.transpose(coef2[...]))
+        odd_vert_ref[...] = vertex_part(vert3[...], ctx3[...], jnp.transpose(coef3[...]))
 
 
 def context_kernel(core, after, vert_ref, ctx_ref, base_ref, slope_ref, coef_ref, new_ctx_ref):
     @pl.when(on_core(core))
     def _():
         vs, cs = halves(vert_ref[...]), halves(ctx_ref[...])
-        coef = base_ref[...] - slope_ref[...] * jnp.tanh(0.5 * product(vs, cs, NT))
+        coef = base_ref[...] - slope_ref[...] * jnp.tanh(0.5 * product(cs, vs, NT))
         coef_ref[...] = coef
-        new_ctx_ref[...] = context_part(vs, ctx_ref[...], coef)
+        new_ctx_ref[...] = ctx_ref[...] + row_product(halves(coef), vs)
 
 
 def pass_kernel(core, after, vert_ref, ctx_ref, base_ref, slope_ref, new_vert_ref, new_ctx_ref):
@@ -316,7 +318,7 @@
     outer2 = moved(out, 0, 3)
     lend = moved(vert_o, 0, 1)
     arrays = (vert_o, in_vmem(far), in_vmem(mate))
-    table = call(functools.partial(odd_far_kernel, negs, tiles), (square,) * 4, arrays)
+    table = call(functools.partial(odd_far_kernel, negs, tiles), (square,) * 4, arrays, scratch_shapes=[square, square])
     coef2, out2 = context_pass(1, table[3], swap0, outer1, *table[:2])
     coef3, out3 = context_pass(1, coef2, lend, out2, *table[2:])
     outer3 = moved(out3, 1, 1)

time: 56.4 us -> 56.4 us (level)
  no operation moved by 1% of the time
where the time goes in v8:
time: 56.4 us; the launch traced here: 56.1 us
  waiting for transfers between devices  33.1 us (59%)
  starting transfers between devices  14.2 us (25%)
  Pallas kernels  7.9 us (14%)
  between operations  0.85 us (2%)
    ppermute x9, waiting for transfers between devices, moved(): return lax.ppermute(value, ('grp', 'blk'), pairs)  33.1 us
    ppermute x9, starting transfers between devices, moved(): return lax.ppermute(value, ('grp', 'blk'), pairs)  11.5 us
    pallas_call x13, Pallas kernels, call(): pl.pallas_call(kernel, out_shape=tuple(outs), in_specs=in_specs or [ANY_S...  6.36 us
    ppermute x1, starting transfers between devices, on_device(): mate = lax.ppermute(far, 'blk', [(b, b ^ 1) for b in range(n_blk)])  2.7 us
    pallas_call x3, Pallas kernels, store(): pl.pallas_call(functools.partial(store_kernel, core, count), out_shape=(p...  1.54 us
  transfers between devices with their start and end apart: 10, of which 5 were waited for; matrix products, arithmetic and copies ran while one was open for 0% of the time, Pallas kernels for 7%

profile of v8, /device:TPU:6, one launch (start us, length us, event | category | flops | bytes accessed | tf_op | source)
XLA Modules:
  0.0 56.1 jit_solution(6172983732331116157)
XLA Ops:
  0.6 0.1 shard_map.68
  0.7 2.4 %shard_map.69 = (s32[392,384]{1,0:T(8,128)S(1)}, s32[784,384]{1,0:T(8,128)S(1)}, f32[384,256]{1,0:T(8,128)S(1)}, f32[384,256]{1,0:T(8,128)S(1)}, f32[384,384]{1,0:T(8,128)S(1)}, /*index=5*/f32[384,256]{1,0:T(8,128)S(1)}) custom-call(f32[384,256]{1,0:T(8,128)} %vert_hbm.3, f32[384,256]{1,0:T(8,128)} %ctx_hbm.3, ...), custom_call_target="tpu_custom_call", output_to_operand_aliasing={{0}: (5, {}), {1}: (6, {})} | custom-call | tf_op jit(solution)/shard_map/pallas_call | solution.py:247
  3.1 1.8 %collective-permute-start = (f32[384,256]{1,0:T(8,128)S(1)}, f32[384,256]{1,0:T(8,128)S(1)}, u32[]{:S(2)}, u32[]{:S(2)}) collective-permute-start(f32[384,256]{1,0:T(8,128)S(1)} %get-tuple-element.54), channel_id=1, source_target_pairs={{0,1},{2,3},{4,5},{6,7},{8,9},{10,11},{12,13},{14,15},{16,17},{18,... | collective-permute-start | bytes 1179656 | tf_op jit(solution)/shard_map/ppermute | solution.py:281
  4.9 1.3 %collective-permute-done.ctx_ref = f32[384,256]{1,0:T(8,128)S(1)} collective-permute-done((f32[384,256]{1,0:T(8,128)S(1)}, f32[384,256]{1,0:T(8,128)S(1)}, u32[]{:S(2)}, u32[]{:S(2)}) %collective-permute-start) | collective-permute-done | bytes 393248 | tf_op jit(solution)/shard_map/ppermute | solution.py:281
  6.2 0.8 %shard_map.72 = (s32[784,384]{1,0:T(8,128)S(1)}, f32[384,384]{1,0:T(8,128)S(1)}, f32[384,384]{1,0:T(8,128)S(1)}, f32[384,256]{1,0:T(8,128)S(1)}) custom-call(f32[384,256]{1,0:T(8,128)S(1)} %get-tuple-element.56.after, s32[784,384]{1,0:T(8,128)S(1)} %get-tuple-element.57.far_in, ...), custom_call_target="tpu_custom_call", output_to_operand_aliasing={{0}: (1, {})} | custom-call | tf_op jit(solution)/shard_map/pallas_call | solution.py:247
  7.0 2.7 %collective-permute-start.2 = (s32[784,384]{1,0:T(8,128)S(1)}, s32[784,384]{1,0:T(8,128)S(1)}, u32[]{:S(2)}, u32[]{:S(2)}) collective-permute-start(s32[784,384]{1,0:T(8,128)S(1)} %get-tuple-element.65.own), channel_id=1, source_target_pairs={{0,1},{1,0},{2,3},{3,2},{4,5},{5,4},{6,7},{7,6},{8,9},{9,8},{10,11... | collective-permute-start | bytes 3612680 | tf_op jit(solution)/shard_map/ppermute | solution.py:313
  9.7 1.3 %collective-permute-start.1 = (f32[384,256]{1,0:T(8,128)S(1)}, f32[384,256]{1,0:T(8,128)S(1)}, u32[]{:S(2)}, u32[]{:S(2)}) collective-permute-start(f32[384,256]{1,0:T(8,128)S(1)} %get-tuple-element.62), channel_id=1, source_target_pairs={{1,2},{3,4},{5,6},{7,8},{9,10},{11,12},{13,14},{15,16},{17,18},{19... | collective-permute-start | bytes 1179656 | tf_op jit(solution)/shard_map/ppermute | solution.py:281
  11.0 1.3 %collective-permute-start.3 = (f32[384,256]{1,0:T(8,128)S(1)}, f32[384,256]{1,0:T(8,128)S(1)}, u32[]{:S(2)}, u32[]{:S(2)}) collective-permute-start(f32[384,256]{1,0:T(8,128)S(1)} %get-tuple-element.56.after), channel_id=1, source_target_pairs={{1,64},{3,66},{5,68},{7,70},{9,72},{11,74},{13,76},{15,78},{17,80}... | collective-permute-start | bytes 1179656 | tf_op jit(solution)/shard_map/ppermute | solution.py:281
  12.3 15.8 %collective-permute-done.1.ctx_ref = f32[384,256]{1,0:T(8,128)S(1)} collective-permute-done((f32[384,256]{1,0:T(8,128)S(1)}, f32[384,256]{1,0:T(8,128)S(1)}, u32[]{:S(2)}, u32[]{:S(2)}) %collective-permute-start.1) | collective-permute-done | bytes 393248 | tf_op jit(solution)/shard_map/ppermute | solution.py:281
  28.1 1.2 %shard_map.73 = (f32[384,256]{1,0:T(8,128)S(1)}, f32[384,256]{1,0:T(8,128)S(1)}) custom-call(f32[384,384]{1,0:T(8,128)S(1)} %get-tuple-element.60.after.base_ref, f32[384,256]{1,0:T(8,128)S(1)} %get-tuple-element.61.vert_ref, f32[384,256]{1,0:T(8,128)S(1)} %collective-permute-done.1.ctx_ref, f32[384,384]{1,0:T(8,128)S(1)} %get-tuple-element.60.after.base_ref, ...), custom_call_target="tpu_custom_call" | custom-call | tf_op jit(solution)/shard_map/pallas_call | solution.py:247
  29.3 1.3 %collective-permute-start.4 = (f32[384,256]{1,0:T(8,128)S(1)}, f32[384,256]{1,0:T(8,128)S(1)}, u32[]{:S(2)}, u32[]{:S(2)}) collective-permute-start(f32[384,256]{1,0:T(8,128)S(1)} %get-tuple-element.64.after), channel_id=1, source_target_pairs={{0,65},{2,67},{4,69},{6,71},{8,73},{10,75},{12,77},{14,79},{16,81}... | collective-permute-start | bytes 1179656 | tf_op jit(solution)/shard_map/ppermute | solution.py:281
  30.6 0.7 %collective-permute-start.5 = (f32[384,256]{1,0:T(8,128)S(1)}, f32[384,256]{1,0:T(8,128)S(1)}, u32[]{:S(2)}, u32[]{:S(2)}) collective-permute-start(f32[384,256]{1,0:T(8,128)S(1)} %get-tuple-element.71), channel_id=1, source_target_pairs={{1,3},{3,5},{5,7},{7,9},{9,11},{11,13},{13,15},{15,17},{17,19},{19... | collective-permute-start | bytes 1179656 | tf_op jit(solution)/shard_map/ppermute | solution.py:281
  31.3 0.0 collective-permute-done.2.mate
  31.3 0.7 %shard_map.74 = (f32[384,384]{1,0:T(8,128)S(1)}, f32[384,384]{1,0:T(8,128)S(1)}) custom-call(f32[384,256]{1,0:T(8,128)S(1)} %get-tuple-element.64.after, s32[784,384]{1,0:T(8,128)S(1)} %collective-permute-done.2.mate), custom_call_target="tpu_custom_call" | custom-call | tf_op jit(solution)/shard_map/pallas_call | solution.py:247
  32.0 0.0 collective-permute-done.3.vert_ref
  32.0 1.2 %shard_map.75 = (f32[384,256]{1,0:T(8,128)S(1)}, f32[384,256]{1,0:T(8,128)S(1)}) custom-call(f32[384,384]{1,0:T(8,128)S(1)} %get-tuple-element.66.after.base_ref, f32[384,256]{1,0:T(8,128)S(1)} %collective-permute-done.3.vert_ref, f32[384,256]{1,0:T(8,128)S(1)} %get-tuple-element.67.ctx_ref, f32[384,384]{1,0:T(8,128)S(1)} %get-tuple-element.66.after.base_ref, ...), custom_call_target="tpu_custom_call" | custom-call | tf_op jit(solution)/shard_map/pallas_call | solution.py:247
  33.2 1.3 %collective-permute-start.6 = (f32[384,256]{1,0:T(8,128)S(1)}, f32[384,256]{1,0:T(8,128)S(1)}, u32[]{:S(2)}, u32[]{:S(2)}) collective-permute-start(f32[384,256]{1,0:T(8,128)S(1)} %get-tuple-element.69.after), channel_id=1, source_target_pairs={{0,1},{2,3},{4,5},{6,7},{8,9},{10,11},{12,13},{14,15},{16,17},{18,... | collective-permute-start | bytes 1179656 | tf_op jit(solution)/shard_map/ppermute | solution.py:281
  34.5 1.3 %collective-permute-start.7 = (f32[384,256]{1,0:T(8,128)S(1)}, f32[384,256]{1,0:T(8,128)S(1)}, u32[]{:S(2)}, u32[]{:S(2)}) collective-permute-start(f32[384,256]{1,0:T(8,128)S(1)} %get-tuple-element.80), channel_id=1, source_target_pairs={{0,3},{2,5},{4,7},{6,9},{8,11},{10,13},{12,15},{14,17},{16,19},{18... | collective-permute-start | bytes 1179656 | tf_op jit(solution)/shard_map/ppermute | solution.py:281
  35.9 0.0 collective-permute-done.4.vert_ref.vert2
  35.9 0.0 collective-permute-done.5.ctx_ref.ctx2
  35.9 0.0 collective-permute-done.6.vert_ref.vert3
  36.0 5.1 %collective-permute-done.7.ctx_ref = f32[384,256]{1,0:T(8,128)S(1)} collective-permute-done((f32[384,256]{1,0:T(8,128)S(1)}, f32[384,256]{1,0:T(8,128)S(1)}, u32[]{:S(2)}, u32[]{:S(2)}) %collective-permute-start.7) | collective-permute-done | bytes 393248 | tf_op jit(solution)/shard_map/ppermute | solution.py:281
  41.1 1.3 %collective-permute-start.8 = (f32[384,256]{1,0:T(8,128)S(1)}, f32[384,256]{1,0:T(8,128)S(1)}, u32[]{:S(2)}, u32[]{:S(2)}) collective-permute-start(f32[384,256]{1,0:T(8,128)S(1)} %get-tuple-element.82), channel_id=1, source_target_pairs={{1,0},{3,2},{5,4},{7,6},{9,8},{11,10},{13,12},{15,14},{17,16},{19,... | collective-permute-start | bytes 1179656 | tf_op jit(solution)/shard_map/ppermute | solution.py:281
  42.4 1.3 %collective-permute-start.9 = (f32[384,256]{1,0:T(8,128)S(1)}, f32[384,256]{1,0:T(8,128)S(1)}, u32[]{:S(2)}, u32[]{:S(2)}) collective-permute-start(f32[384,256]{1,0:T(8,128)S(1)} %get-tuple-element.86), channel_id=1, source_target_pairs={{1,2},{3,4},{5,6},{7,8},{9,10},{11,12},{13,14},{15,16},{17,18},{19... | collective-permute-start | bytes 1179656 | tf_op jit(solution)/shard_map/ppermute | solution.py:281
  43.7 4.1 %collective-permute-done.8.refs_0_ = f32[384,256]{1,0:T(8,128)S(1)} collective-permute-done((f32[384,256]{1,0:T(8,128)S(1)}, f32[384,256]{1,0:T(8,128)S(1)}, u32[]{:S(2)}, u32[]{:S(2)}) %collective-permute-start.8) | collective-permute-done | bytes 393248 | tf_op jit(solution)/shard_map/ppermute | solution.py:281
  47.8 0.8 %shard_map.82 = f32[384,256]{1,0:T(8,128)} custom-call(f32[384,256]{1,0:T(8,128)S(1)} %collective-permute-done.8.refs_0_, f32[384,256]{1,0:T(8,128)} %get-tuple-element.85.refs_1_), custom_call_target="tpu_custom_call", output_to_operand_aliasing={{}: (1, {})} | custom-call | tf_op jit(solution)/shard_map/pallas_call | solution.py:285
  48.5 6.8 %collective-permute-done.9.refs_0_ = f32[384,256]{1,0:T(8,128)S(1)} collective-permute-done((f32[384,256]{1,0:T(8,128)S(1)}, f32[384,256]{1,0:T(8,128)S(1)}, u32[]{:S(2)}, u32[]{:S(2)}) %collective-permute-start.9) | collective-permute-done | bytes 393248 | tf_op jit(solution)/shard_map/ppermute | solution.py:281
  55.4 0.8 %shard_map.83 = f32[384,256]{1,0:T(8,128)} custom-call(f32[384,256]{1,0:T(8,128)S(1)} %collective-permute-done.9.refs_0_, f32[384,256]{1,0:T(8,128)} %get-tuple-element.87.refs_1_), custom_call_target="tpu_custom_call", output_to_operand_aliasing={{}: (1, {})} | custom-call | tf_op jit(solution)/shard_map/pallas_call | solution.py:285
  (8 shorter events, 0.1 us)
Async XLA Ops:
  3.1 3.1 %collective-permute-start = (f32[384,256]{1,0:T(8,128)S(1)}, f32[384,256]{1,0:T(8,128)S(1)}, u32[]{:S(2)}, u32[]{:S(2)}) collective-permute-start(f32[384,256]{1,0:T(8,128)S(1)} %get-tuple-element.54), channel_id=1, source_target_pairs={{0,1},{2,3},{4,5},{6,7},{8,9},{10,11},{12,13},{14,15},{16,17},{18,... | collective-permute-start | bytes 1179656 | tf_op jit(solution)/shard_map/ppermute | solution.py:281
  7.0 24.3 %collective-permute-start.2 = (s32[784,384]{1,0:T(8,128)S(1)}, s32[784,384]{1,0:T(8,128)S(1)}, u32[]{:S(2)}, u32[]{:S(2)}) collective-permute-start(s32[784,384]{1,0:T(8,128)S(1)} %get-tuple-element.65.own), channel_id=1, source_target_pairs={{0,1},{1,0},{2,3},{3,2},{4,5},{5,4},{6,7},{7,6},{8,9},{9,8},{10,11... | collective-permute-start | bytes 3612680 | tf_op jit(solution)/shard_map/ppermute | solution.py:313
  9.7 18.4 %collective-permute-start.1 = (f32[384,256]{1,0:T(8,128)S(1)}, f32[384,256]{1,0:T(8,128)S(1)}, u32[]{:S(2)}, u32[]{:S(2)}) collective-permute-start(f32[384,256]{1,0:T(8,128)S(1)} %get-tuple-element.62), channel_id=1, source_target_pairs={{1,2},{3,4},{5,6},{7,8},{9,10},{11,12},{13,14},{15,16},{17,18},{19... | collective-permute-start | bytes 1179656 | tf_op jit(solution)/shard_map/ppermute | solution.py:281
  11.0 21.0 %collective-permute-start.3 = (f32[384,256]{1,0:T(8,128)S(1)}, f32[384,256]{1,0:T(8,128)S(1)}, u32[]{:S(2)}, u32[]{:S(2)}) collective-permute-start(f32[384,256]{1,0:T(8,128)S(1)} %get-tuple-element.56.after), channel_id=1, source_target_pairs={{1,64},{3,66},{5,68},{7,70},{9,72},{11,74},{13,76},{15,78},{17,80}... | collective-permute-start | bytes 1179656 | tf_op jit(solution)/shard_map/ppermute | solution.py:281
  29.3 6.6 %collective-permute-start.4 = (f32[384,256]{1,0:T(8,128)S(1)}, f32[384,256]{1,0:T(8,128)S(1)}, u32[]{:S(2)}, u32[]{:S(2)}) collective-permute-start(f32[384,256]{1,0:T(8,128)S(1)} %get-tuple-element.64.after), channel_id=1, source_target_pairs={{0,65},{2,67},{4,69},{6,71},{8,73},{10,75},{12,77},{14,79},{16,81}... | collective-permute-start | bytes 1179656 | tf_op jit(solution)/shard_map/ppermute | solution.py:281
  30.6 5.3 %collective-permute-start.5 = (f32[384,256]{1,0:T(8,128)S(1)}, f32[384,256]{1,0:T(8,128)S(1)}, u32[]{:S(2)}, u32[]{:S(2)}) collective-permute-start(f32[384,256]{1,0:T(8,128)S(1)} %get-tuple-element.71), channel_id=1, source_target_pairs={{1,3},{3,5},{5,7},{7,9},{9,11},{11,13},{13,15},{15,17},{17,19},{19... | collective-permute-start | bytes 1179656 | tf_op jit(solution)/shard_map/ppermute | solution.py:281
  33.2 2.7 %collective-permute-start.6 = (f32[384,256]{1,0:T(8,128)S(1)}, f32[384,256]{1,0:T(8,128)S(1)}, u32[]{:S(2)}, u32[]{:S(2)}) collective-permute-start(f32[384,256]{1,0:T(8,128)S(1)} %get-tuple-element.69.after), channel_id=1, source_target_pairs={{0,1},{2,3},{4,5},{6,7},{8,9},{10,11},{12,13},{14,15},{16,17},{18,... | collective-permute-start | bytes 1179656 | tf_op jit(solution)/shard_map/ppermute | solution.py:281
  34.5 6.6 %collective-permute-start.7 = (f32[384,256]{1,0:T(8,128)S(1)}, f32[384,256]{1,0:T(8,128)S(1)}, u32[]{:S(2)}, u32[]{:S(2)}) collective-permute-start(f32[384,256]{1,0:T(8,128)S(1)} %get-tuple-element.80), channel_id=1, source_target_pairs={{0,3},{2,5},{4,7},{6,9},{8,11},{10,13},{12,15},{14,17},{16,19},{18... | collective-permute-start | bytes 1179656 | tf_op jit(solution)/shard_map/ppermute | solution.py:281
  41.1 6.7 %collective-permute-start.8 = (f32[384,256]{1,0:T(8,128)S(1)}, f32[384,256]{1,0:T(8,128)S(1)}, u32[]{:S(2)}, u32[]{:S(2)}) collective-permute-start(f32[384,256]{1,0:T(8,128)S(1)} %get-tuple-element.82), channel_id=1, source_target_pairs={{1,0},{3,2},{5,4},{7,6},{9,8},{11,10},{13,12},{15,14},{17,16},{19,... | collective-permute-start | bytes 1179656 | tf_op jit(solution)/shard_map/ppermute | solution.py:281
  42.4 13.0 %collective-permute-start.9 = (f32[384,256]{1,0:T(8,128)S(1)}, f32[384,256]{1,0:T(8,128)S(1)}, u32[]{:S(2)}, u32[]{:S(2)}) collective-permute-start(f32[384,256]{1,0:T(8,128)S(1)} %get-tuple-element.86), channel_id=1, source_target_pairs={{1,2},{3,4},{5,6},{7,8},{9,10},{11,12},{13,14},{15,16},{17,18},{19... | collective-permute-start | bytes 1179656 | tf_op jit(solution)/shard_map/ppermute | solution.py:281
